TPU v7x, 32 devices: a whole 2x2x4 slice. The times are simulated.
32 devices in a mesh: branch: 2 (over x), tensor: 4 (over y, core), dp: 4 (over z).
Axes of the slice: x: 2, y: 2, z: 4, core: 2. Of those that a mesh axis runs over, the one named last changes fastest.
Arguments:
- tokens: bfloat16 [8192, 2048], P('dp'), may hold values from -6 to 6
- lengths: int32 [4], P('dp'), may hold values from 128 to 2048, as said below
- valid_mask: int32 [8192], P('dp'), may hold values 0 or 1
- ln1_gain: float32 [2048], replicated, may hold values from 0.1 to 1.9
- ln1_bias: float32 [2048], replicated, may hold values from -4 to 4
- qkv_weight: bfloat16 [2048, 6144], P('dp', 'tensor'), may hold values from -0.125 to 0.125
- qkv_bias: float32 [6144], P('tensor'), may hold values from -6 to 6
- out_weight: bfloat16 [2048, 2048], P('tensor', 'dp'), may hold values from -1 to 1
- out_bias: float32 [2048], replicated, may hold values from -4 to 4
- ln2_gain: float32 [2048], replicated, may hold values from 0.1 to 1.9
- ln2_bias: float32 [2048], replicated, may hold values from -4 to 4
- up_weight: bfloat16 [2048, 8192], P('dp', 'tensor'), may hold values from -0.125 to 0.125
- up_bias: float32 [8192], P('tensor'), may hold values from -6 to 6
- down_weight: bfloat16 [8192, 2048], P('tensor', 'dp'), may hold values from -0.0625 to 0.0625
- down_bias: float32 [2048], replicated, may hold values from -4 to 4
- out_grad: bfloat16 [8192, 2048], P('dp'), may hold values from -6 to 6
Outputs:
- layer_output: bfloat16 [8192, 2048], P('dp')
- x_grad: bfloat16 [8192, 2048], P('dp')
- ln1_gain_grad: float32 [2048], replicated
- ln1_bias_grad: float32 [2048], replicated
- qkv_weight_grad: float32 [2048, 6144], P(('branch', 'dp'), 'tensor')
- qkv_bias_grad: float32 [6144], P('tensor')
- out_weight_grad: float32 [2048, 2048], P('tensor', ('branch', 'dp'))
- out_bias_grad: float32 [2048], replicated
- ln2_gain_grad: float32 [2048], replicated
- ln2_bias_grad: float32 [2048], replicated
- up_weight_grad: float32 [2048, 8192], P(('branch', 'dp'), 'tensor')
- up_bias_grad: float32 [8192], P('tensor')
- down_weight_grad: float32 [8192, 2048], P('tensor', ('branch', 'dp'))
- down_bias_grad: float32 [2048], replicated
Inputs may be any that keep to these rules, and one draw needn't show every extreme that they name: `lengths`: each sequence's length; the longest is exactly 2048. `valid_mask`: 1 marks a token that takes part; slots at or past their sequence's length are padding whatever the mask says.
All inputs are finite; a program needn't handle non-finite values. No bound on the sum of `valid_mask` on one device may be relied on, other than what follows from the above.
Results may differ from a plain program's by a relative error of at most 0.0098.
Values may be sent and summed in bfloat16 or wider, within the bound.
No kernel may reach another device: no remote copies, remote signals or barrier semaphores. Data moves between devices by JAX's collectives and lax.ppermute only.
A program may use at most 384 MiB of HBM per device.

v0:
```python
from functools import partial

import jax
import jax.numpy as jnp
from jax import lax
from jax.sharding import PartitionSpec as P

HEAD_DIM = 256
SEQ_LEN = 2048
QBLOCK = 512
ROT = 64


norm_eps = 1e-05
rope_base = 10000.0
masked_score = -1e30


def layer_norm(rows, gain, shift):
    row_mean = jnp.mean(rows, axis=-1, keepdims=True)
    centred = rows - row_mean
    inv_std = lax.rsqrt(jnp.mean(centred * centred, axis=-1, keepdims=True) + norm_eps)
    unit_rows = centred * inv_std
    return (unit_rows * gain + shift, unit_rows, inv_std)


def norm_back(normed_grad, gain, unit_rows, inv_std):
    unit_grad = normed_grad * gain
    return inv_std * (
        unit_grad
        - jnp.mean(unit_grad, axis=-1, keepdims=True)
        - unit_rows * jnp.mean(unit_grad * unit_rows, axis=-1, keepdims=True)
    )


def rope_tables(length, rotary):
    half_rot = rotary // 2
    inv_freq = rope_base ** (-2.0 * jnp.arange(half_rot, dtype=jnp.float32) / rotary)
    phase_angle = jnp.arange(length, dtype=jnp.float32)[:, None] * inv_freq[None, :]
    return (jnp.cos(phase_angle), jnp.sin(phase_angle))


def rotate(values, cos_table, sin_table, rotary):
    half_rot = rotary // 2
    lead_part = values[..., :half_rot]
    tail_part = values[..., half_rot:rotary]
    cos_part = cos_table[:, None, :]
    sin_part = sin_table[:, None, :]
    return jnp.concatenate(
        [
            lead_part * cos_part - tail_part * sin_part,
            tail_part * cos_part + lead_part * sin_part,
            values[..., rotary:],
        ],
        axis=-1,
    )


def pad_columns(matrix, total):
    return jnp.pad(matrix, ((0, 0), (0, total - matrix.shape[1])))


def pad_leading(matrix, total):
    return jnp.pad(matrix, ((0, total - matrix.shape[0]), (0, 0)))


def allow_block(block_idx, key_end, seq_valid):
    query_pos = block_idx * QBLOCK + jnp.arange(QBLOCK)
    key_pos = jnp.arange(key_end)
    earlier = key_pos[None, :] <= query_pos[:, None]
    itself = key_pos[None, :] == query_pos[:, None]
    return earlier & (seq_valid[None, :key_end] | itself)


def block_scores(query_block, key_rows, allowed, score_scale):
    scores = (
        jnp.einsum("qhd,khd->hqk", query_block, key_rows, preferred_element_type=jnp.float32)
        * score_scale
    )
    return jnp.where(allowed[None], scores, masked_score)


def attend_forward(operands):
    query_rows, key_rows, value_rows, seq_valid = operands
    seq_len = query_rows.shape[0]
    score_scale = query_rows.shape[-1] ** (-0.5)
    attended_list = []
    total_list = []
    for block_idx in range(seq_len // QBLOCK):
        key_end = (block_idx + 1) * QBLOCK
        allowed = allow_block(block_idx, key_end, seq_valid)
        scores = block_scores(
            query_rows[block_idx * QBLOCK : key_end], key_rows[:key_end], allowed, score_scale
        )
        row_max = jnp.max(scores, axis=-1, keepdims=True)
        exp_scores = jnp.exp(scores - row_max)
        row_total = jnp.sum(exp_scores, axis=-1, keepdims=True)
        attn_probs = (exp_scores / row_total).astype(jnp.bfloat16)
        attended = jnp.einsum(
            "hqk,khd->qhd", attn_probs, value_rows[:key_end], preferred_element_type=jnp.float32
        )
        attended_list.append(attended.astype(jnp.bfloat16))
        total_list.append(row_max[..., 0] + jnp.log(row_total[..., 0]))
    return (jnp.concatenate(attended_list, axis=0), jnp.concatenate(total_list, axis=1))


def attend_backward(operands):
    query_rows, key_rows, value_rows, attended_grad, log_total, seq_valid = operands
    seq_len, head_count, head_dim = query_rows.shape
    score_scale = head_dim ** (-0.5)
    query_grad_list = []
    key_grad = jnp.zeros((seq_len, head_count, head_dim), jnp.float32)
    value_grad = jnp.zeros((seq_len, head_count, head_dim), jnp.float32)
    for block_idx in range(seq_len // QBLOCK):
        key_end = (block_idx + 1) * QBLOCK
        query_block = query_rows[block_idx * QBLOCK : key_end]
        grad_block = attended_grad[block_idx * QBLOCK : key_end]
        allowed = allow_block(block_idx, key_end, seq_valid)
        scores = block_scores(query_block, key_rows[:key_end], allowed, score_scale)
        attn_probs = jnp.exp(scores - log_total[:, block_idx * QBLOCK : key_end, None])
        probs_grad = jnp.einsum(
            "qhd,khd->hqk", grad_block, value_rows[:key_end], preferred_element_type=jnp.float32
        )
        row_dot = jnp.sum(attn_probs * probs_grad, axis=-1, keepdims=True)
        score_grad = (attn_probs * (probs_grad - row_dot)).astype(jnp.bfloat16)
        query_grad_list.append(
            jnp.einsum(
                "hqk,khd->qhd", score_grad, key_rows[:key_end], preferred_element_type=jnp.float32
            )
            * score_scale
        )
        pad_rows = ((0, seq_len - key_end), (0, 0), (0, 0))
        key_term = (
            jnp.einsum("hqk,qhd->khd", score_grad, query_block, preferred_element_type=jnp.float32)
            * score_scale
        )
        value_term = jnp.einsum(
            "hqk,qhd->khd",
            attn_probs.astype(jnp.bfloat16),
            grad_block,
            preferred_element_type=jnp.float32,
        )
        key_grad = key_grad + jnp.pad(key_term, pad_rows)
        value_grad = value_grad + jnp.pad(value_term, pad_rows)
    return (jnp.concatenate(query_grad_list, axis=0), key_grad, value_grad)


def local(
    tokens,
    lengths,
    valid_mask,
    ln1_gain,
    ln1_bias,
    qkv_weight,
    qkv_bias,
    out_weight,
    out_bias,
    ln2_gain,
    ln2_bias,
    up_weight,
    up_bias,
    down_weight,
    down_bias,
    out_grad,
):
    row_count, width = tokens.shape
    seq_count = row_count // SEQ_LEN
    qkv_cols = qkv_bias.shape[0]
    out_rows = out_weight.shape[0]
    up_cols = up_bias.shape[0]
    wide_cols = max(qkv_cols, up_cols)
    tall_rows = max(out_rows, up_cols)
    is_attention = lax.axis_index("branch") == 0
    positions = jnp.arange(SEQ_LEN, dtype=jnp.int32)
    seq_valid = (valid_mask.reshape(seq_count, SEQ_LEN) == 1) & (
        positions[None, :] < lengths[:, None]
    )
    validity = seq_valid.reshape(row_count).astype(jnp.float32)
    rows_f32 = tokens.astype(jnp.float32)
    grad_rows = out_grad * validity.astype(jnp.bfloat16)[:, None]
    zero_width = jnp.zeros((width,), jnp.float32)
    first_local = jnp.where(
        is_attention, pad_columns(qkv_weight, wide_cols), pad_columns(up_weight, wide_cols)
    )
    second_local = jnp.where(
        is_attention, pad_leading(out_weight, tall_rows), pad_leading(down_weight, tall_rows)
    )
    first_full, second_full = (
        lax.all_gather(first_local, "dp", axis=0, tiled=True),
        lax.all_gather(second_local, "dp", axis=1, tiled=True),
    )

    def attention_half():
        qkv_full = first_full[:, :qkv_cols]
        out_full = second_full[:out_rows]
        normed, unit_rows, inv_std = layer_norm(rows_f32, ln1_gain, ln1_bias)
        normed_low = normed.astype(jnp.bfloat16)
        head_count = qkv_cols // (3 * HEAD_DIM)
        projected = jnp.dot(normed_low, qkv_full, preferred_element_type=jnp.float32) + qkv_bias
        projected = projected.reshape(seq_count, SEQ_LEN, head_count, 3, HEAD_DIM)
        cos_table, sin_table = rope_tables(SEQ_LEN, ROT)
        query_rows = rotate(projected[:, :, :, 0], cos_table, sin_table, ROT).astype(jnp.bfloat16)
        key_rows = rotate(projected[:, :, :, 1], cos_table, sin_table, ROT).astype(jnp.bfloat16)
        value_rows = projected[:, :, :, 2].astype(jnp.bfloat16)
        attended, log_total = lax.map(attend_forward, (query_rows, key_rows, value_rows, seq_valid))
        attended_flat = attended.reshape(row_count, head_count * HEAD_DIM)
        branch_part = jnp.dot(attended_flat, out_full, preferred_element_type=jnp.float32)
        out_grad_full = jnp.einsum(
            "rc,rd->cd", attended_flat, grad_rows, preferred_element_type=jnp.float32
        )
        attended_grad = jnp.einsum(
            "rd,cd->rc", grad_rows, out_full, preferred_element_type=jnp.float32
        ).astype(jnp.bfloat16)
        attended_grad = attended_grad.reshape(seq_count, SEQ_LEN, head_count, HEAD_DIM)
        query_grad, key_grad, value_grad = lax.map(
            attend_backward, (query_rows, key_rows, value_rows, attended_grad, log_total, seq_valid)
        )
        query_grad = rotate(query_grad, cos_table, -sin_table, ROT)
        key_grad = rotate(key_grad, cos_table, -sin_table, ROT)
        qkv_grad = (
            jnp.stack([query_grad, key_grad, value_grad], axis=3)
            .reshape(row_count, qkv_cols)
            .astype(jnp.bfloat16)
        )
        qkv_grad_full = jnp.einsum(
            "rd,rc->dc", normed_low, qkv_grad, preferred_element_type=jnp.float32
        )
        qkv_bias_part = jnp.sum(qkv_grad, axis=0, dtype=jnp.float32)
        normed_grad = jnp.einsum(
            "rc,dc->rd", qkv_grad, qkv_full, preferred_element_type=jnp.float32
        )
        input_part = norm_back(normed_grad, ln1_gain, unit_rows, inv_std)
        gain_part = jnp.sum(normed_grad * unit_rows, axis=0)
        shift_part = jnp.sum(normed_grad, axis=0)
        first_pack = pad_columns(qkv_grad_full, wide_cols).reshape(2, width // 2, wide_cols)
        second_pack = pad_leading(out_grad_full, tall_rows).reshape(tall_rows, 2, width // 2)
        return (
            branch_part,
            input_part,
            first_pack,
            second_pack,
            gain_part,
            shift_part,
            zero_width,
            zero_width,
            qkv_bias_part,
            jnp.zeros((up_cols,), jnp.float32),
        )

    def feedforward_half():
        normed, unit_rows, inv_std = layer_norm(rows_f32, ln2_gain, ln2_bias)
        normed_low = normed.astype(jnp.bfloat16)
        hidden = jnp.dot(normed_low, first_full, preferred_element_type=jnp.float32) + up_bias
        activated, gelu_back = jax.vjp(partial(jax.nn.gelu, approximate=False), hidden)
        activated_low = activated.astype(jnp.bfloat16)
        branch_part = jnp.dot(activated_low, second_full, preferred_element_type=jnp.float32)
        down_grad_full = jnp.einsum(
            "rf,rd->fd", activated_low, grad_rows, preferred_element_type=jnp.float32
        )
        activated_grad = jnp.einsum(
            "rd,fd->rf", grad_rows, second_full, preferred_element_type=jnp.float32
        )
        hidden_grad = gelu_back(activated_grad)[0].astype(jnp.bfloat16)
        up_grad_full = jnp.einsum(
            "rd,rf->df", normed_low, hidden_grad, preferred_element_type=jnp.float32
        )
        up_bias_part = jnp.sum(hidden_grad, axis=0, dtype=jnp.float32)
        normed_grad = jnp.einsum(
            "rf,df->rd", hidden_grad, first_full, preferred_element_type=jnp.float32
        )
        input_part = norm_back(normed_grad, ln2_gain, unit_rows, inv_std)
        gain_part = jnp.sum(normed_grad * unit_rows, axis=0)
        shift_part = jnp.sum(normed_grad, axis=0)
        first_pack = pad_columns(up_grad_full, wide_cols).reshape(2, width // 2, wide_cols)
        second_pack = pad_leading(down_grad_full, tall_rows).reshape(tall_rows, 2, width // 2)
        return (
            branch_part,
            input_part,
            first_pack,
            second_pack,
            zero_width,
            zero_width,
            gain_part,
            shift_part,
            jnp.zeros((qkv_cols,), jnp.float32),
            up_bias_part,
        )

    (
        branch_part,
        input_part,
        first_pack,
        second_pack,
        norm1_gain_part,
        norm1_shift_part,
        norm2_gain_part,
        norm2_shift_part,
        qkv_bias_part,
        up_bias_part,
    ) = lax.cond(is_attention, attention_half, feedforward_half)
    first_reduced, second_reduced = (
        lax.psum_scatter(first_pack, "dp", scatter_dimension=1, tiled=True),
        lax.psum_scatter(second_pack, "dp", scatter_dimension=2, tiled=True),
    )
    qkv_grads = jnp.where(is_attention, first_reduced[:, :, :qkv_cols], 0.0)
    up_grads = jnp.where(is_attention, 0.0, first_reduced)
    out_grads = jnp.where(is_attention, second_reduced[:out_rows], 0.0)
    down_grads = jnp.where(is_attention, 0.0, second_reduced)
    leading = is_attention & (lax.axis_index("tensor") == 0)
    bias_rows = jnp.where(leading, jnp.sum(grad_rows, axis=0, dtype=jnp.float32), 0.0)
    norm1_gain_grad, norm1_shift_grad, norm2_gain_grad, norm2_shift_grad, bias_grad = lax.psum(
        (norm1_gain_part, norm1_shift_part, norm2_gain_part, norm2_shift_part, bias_rows),
        ("branch", "tensor", "dp"),
    )
    qkv_bias_grad, up_bias_grad = lax.psum((qkv_bias_part, up_bias_part), ("branch", "dp"))
    qkv_half, out_half, up_half, down_half = (
        lax.psum_scatter(qkv_grads, "branch", scatter_dimension=0, tiled=True),
        lax.psum_scatter(out_grads, "branch", scatter_dimension=1, tiled=True),
        lax.psum_scatter(up_grads, "branch", scatter_dimension=0, tiled=True),
        lax.psum_scatter(down_grads, "branch", scatter_dimension=1, tiled=True),
    )
    shift_sum = out_bias + down_bias
    branch_total, input_total = lax.psum((branch_part, input_part), ("branch", "tensor"))
    output_rows = (rows_f32 + validity[:, None] * (branch_total + shift_sum)).astype(jnp.bfloat16)
    grad_input = (out_grad.astype(jnp.float32) + input_total).astype(jnp.bfloat16)
    return (
        output_rows,
        grad_input,
        norm1_gain_grad,
        norm1_shift_grad,
        qkv_half[0],
        qkv_bias_grad,
        out_half[:, 0, :],
        bias_grad,
        norm2_gain_grad,
        norm2_shift_grad,
        up_half[0],
        up_bias_grad,
        down_half[:, 0, :],
        bias_grad,
    )


def solution(mesh):
    return jax.shard_map(
        local,
        mesh=mesh,
        in_specs=(
            P("dp", None),
            P("dp"),
            P("dp"),
            P(),
            P(),
            P("dp", "tensor"),
            P("tensor"),
            P("tensor", "dp"),
            P(),
            P(),
            P(),
            P("dp", "tensor"),
            P("tensor"),
            P("tensor", "dp"),
            P(),
            P("dp", None),
        ),
        out_specs=(
            P("dp", None),
            P("dp", None),
            P(),
            P(),
            P(("branch", "dp"), "tensor"),
            P("tensor"),
            P("tensor", ("branch", "dp")),
            P(),
            P(),
            P(),
            P(("branch", "dp"), "tensor"),
            P("tensor"),
            P("tensor", ("branch", "dp")),
            P(),
        ),
        check_vma=False,
    )
```

profile of v0, /device:TPU:0, one launch (start us, length us, event | category | flops | bytes accessed | tf_op | source)
XLA Modules:
  0.0 1820.3 jit_solution(7224682014483728834)
XLA Ops:
  7.3 3.6 pad_select_fusion.1
  13.4 12.9 convert_element_type.201
  27.5 9.4 convert_reduce_fusion.2
  36.9 127.0 %all-gather.3.cloned.1.call-done = bf16[2048,2048]{1,0:T(8,128)(2,1)} async-done(((bf16[512,2048]{1,0:T(8,128)(2,1)}), bf16[2048,2048]{1,0:T(8,128)(2,1)}) %all-gather.3.cloned.1.call-update) | async-done | bytes 8388624 | tf_op jit(solution)/shard_map/all_gather | solution.py:189
  164.0 150.0 %all-gather.5.cloned.1.call-done = bf16[2048,2048]{1,0:T(8,128)(2,1)} async-done(((bf16[2048,512]{1,0:T(8,128)(2,1)}), bf16[2048,2048]{1,0:T(8,128)(2,1)}) %all-gather.5.cloned.1.call-update) | async-done | bytes 8388624 | tf_op jit(solution)/shard_map/all_gather | solution.py:190
  314.0 333.1 %conditional.1 = (f32[2048,2048]{1,0:T(8,128)}, f32[2048,2048]{1,0:T(8,128)}, f32[2,1024,2048]{2,1,0:T(8,128)}, f32[2048,2,1024]{2,1,0:T(2,128)}, f32[2048]{0:T(...) conditional(s32[]{:T(128)} %convert_element_type.203, ...), branch_computations={%region_0.8_spmd, %region_8.28_spmd} | conditional | flops 103536394240 | bytes 1090880128 | solution.py:300
  317.0 6.6 reduce_sum.200
  323.6 7.6 multiply_reduce_fusion.6
  331.2 22.2 %convolution_add_fusion = f32[2048,1536]{0,1:T(8,128)} fusion(f32[1536]{0:T(1024)S(1)} %get-tuple-element.142, bf16[2048,2048]{1,0:T(8,128)(2,1)} %get-tuple-element.74, f32[2048,2048]{1,0:T(8,128)} %get-tuple-element.71, f32[2048]{0:T(1024)S(1)} %get-tuple-element.141, f32[2048]{0:T(1024)S(1)} %get-tuple-element.140, f32[2048]{0:T(1024)S(1)} %add_rsqrt_fusion.1, ...), kind=kOutput, calls=%fused_computation.40 | convolution fusion | flops 12909019136 | bytes 35690496 | tf_op jit(solution)/shard_map/cond/branch_1_fun/dot_general | solution.py:199
  353.4 8.0 fusion.87
  361.4 5.3 copy.184
  366.8 5.3 copy.183
  372.1 4.7 fusion.78
  376.8 4.7 subtract_convert_fusion
  385.3 3.7 pad_maximum_fusion
  392.9 7.1 convolution_convert_fusion
  423.2 5.1 fusion.89
  429.7 8.3 multiply_reduce_fusion.8
  437.9 4.4 multiply_convert_fusion.1
  444.4 5.4 fusion.58
  449.8 4.5 maximum_bitcast_fusion
  457.1 4.0 multiply_bitcast_fusion
  461.1 4.0 fusion.25
  465.1 8.1 fusion.19
  473.2 4.5 multiply_subtract_fusion.1
  490.8 4.1 fusion.18
  494.9 3.5 convert_reduce_fusion.1
  498.5 8.8 copy.147
  507.2 28.3 %multiply_reduce_fusion.4 = (f32[2048]{0:T(1024)}, f32[2048]{0:T(1024)S(1)}, f32[2048]{0:T(1024)S(1)}, f32[2048]{0:T(1024)}, f32[2048,2048]{1,0:T(8,128)}) fusion(f32[2048,2048]{1,0:T(8,128)} %get-tuple-element.71, f32[2048]{0:T(1024)S(1)} %add_rsqrt_fusion.1, f32[2048]{0:T(1024)S(1)} %broadcast_multiply_fusion.5, f32[2048]{0:T(1024)S(1)} %get-tuple-element.140, ...), kind=kOutput, calls=%fused_computation.31 | convolution fusion | flops 12922642432 | bytes 46194688 | tf_op jit(solution)/shard_map/cond/branch_1_fun/rc,dc->rd/dot_general | solution.py:229
  535.5 16.9 subtract_multiply_fusion.2
  552.4 22.7 %fusion.82 = f32[2048,1536]{1,0:T(8,128)} fusion(bf16[2048,1536]{0,1:T(8,128)(2,1)} %bitcast.216, f32[2048,2048]{1,0:T(8,128)} %get-tuple-element.71, f32[2048]{0:T(1024)S(1)} %copy-done.67, f32[2048]{0:T(1024)S(1)} %get-tuple-element.140, f32[2048]{0:T(1024)S(1)} %add_rsqrt_fusion.1, f32[2048]{0:T(1024)S(1)} %broadcast_multiply_fusion.5), kind=kOutput, calls=%fused_computation.189 | convolution fusion | flops 12905873408 | bytes 35684352 | tf_op jit(solution)/shard_map/cond/branch_1_fun/rd,rc->dc/dot_general | solution.py:225
  575.1 12.7 pad.39
  596.2 4.2 fusion.64
  600.7 4.5 fusion.95
  605.2 8.1 pad.40
  613.3 22.1 %reshape.604 = f32[2048,2,1024]{2,1,0:T(2,128)} reshape(f32[2048,2048]{1,0:T(8,128)} %pad.40) | data formatting | bytes 33554432 | tf_op jit(solution)/shard_map/cond/branch_1_fun/reshape | solution.py:236
  635.3 9.7 fusion.45
  647.1 15.9 copy.149
  664.2 276.7 %reduce-scatter.11.cloned.1.call-done = f32[2048,2,256]{2,0,1:T(8,128)} async-done(((f32[2048,2,1024]{2,0,1:T(8,128)}), f32[2048,2,256]{2,0,1:T(8,128)}) %reduce-scatter.11.cloned.1.call-update) | async-done | bytes 4194320 | tf_op jit(solution)/shard_map/reduce_scatter | solution.py:303
  943.2 280.9 %reduce-scatter.7.cloned.1.call-done = f32[2,256,2048]{2,1,0:T(8,128)} async-done(((f32[2,1024,2048]{2,1,0:T(8,128)}), f32[2,256,2048]{2,1,0:T(8,128)}) %reduce-scatter.7.cloned.1.call-update) | async-done | bytes 4194320 | tf_op jit(solution)/shard_map/reduce_scatter | solution.py:302
  1224.2 3.7 slice_select_fusion
  1233.1 48.7 %all-reduce.10 = (f32[2048]{0:T(1024)}, f32[2048]{0:T(1024)}, f32[2048]{0:T(1024)S(1)}, f32[2048]{0:T(1024)}, f32[2048]{0:T(1024)}) all-reduce(f32[2048]{0:T(1024)} %get-tuple-element.123, f32[2048]{0:T(1024)} %get-tuple-element.124, ...), channel_id=1, replica_groups=mesh['branch'=2,'tensor'=4,'dp'=4] {'branch','tensor','dp'}, use_global_device_ids=true, to_apply=%region_30.31 | all-reduce | flops 10240 | bytes 81920 | tf_op jit(solution)/shard_map/psum | solution.py:311
  1281.8 38.6 %all-reduce.11 = (f32[1536]{0:T(1024)}, f32[2048]{0:T(1024)}) all-reduce(f32[1536]{0:T(1024)} %get-tuple-element.126, f32[2048]{0:T(1024)} %get-tuple-element.130), channel_id=1, replica_groups=mesh['branch'=2,'tensor'=4,'dp'=4] {'branch','dp'}, use_global_device_ids=true, to_apply=%region_34.35 | all-reduce | flops 3584 | bytes 28672 | tf_op jit(solution)/shard_map/psum | solution.py:315
  1320.4 308.6 %all-reduce.15.cloned.1.call-done = (f32[2048,2048]{1,0:T(8,128)}, f32[2048,2048]{1,0:T(8,128)}) async-done(((f32[2048,2048]{1,0:T(8,128)}, f32[2048,2048]{1,0:T(8,128)}), (f32[2048,2048]{1,0:T(8,128)}, f32[2048,2048]{1,0:T(8,128)})) %all-reduce.15.cloned.1.call-update) | async-done | bytes 33554448 | tf_op jit(solution)/shard_map/psum | solution.py:323
  1629.0 23.7 %add_convert_fusion.9 = (bf16[2048,2048]{1,0:T(8,128)(2,1)}, bf16[2048,2048]{1,0:T(8,128)(2,1)}) fusion(f32[2048,2048]{1,0:T(8,128)} %get-tuple-element.189, bf16[2048,2048]{1,0:T(8,128)(2,1)} %param.33, f32[2048,2048]{1,0:T(8,128)} %get-tuple-element.188, f32[2048]{0:T(1024)S(1)} %add.219, f32[2048]{0:T(1024)S(1)} %copy-done.35, bf16[2048,2048]{1,0:T(8,128)(2,1)} %param.18), kind=kLoop, calls=%fused_computation.191 | loop fusion | flops 33554432 | bytes 67125248 | tf_op jit(solution)/shard_map/convert_element_type | solution.py:325
  1652.7 45.6 %reduce-scatter.9.cloned.1.call-done = f32[1,256,1536]{2,1,0:T(8,128)} async-done(((f32[2,256,1536]{2,1,0:T(8,128)}), f32[1,256,1536]{2,1,0:T(8,128)}) %reduce-scatter.9.cloned.1.call-update) | async-done | bytes 1572880 | tf_op jit(solution)/shard_map/reduce_scatter | solution.py:317
  1698.3 57.3 %reduce-scatter.17.cloned.1.call-done = f32[2048,1,256]{2,0,1:T(8,128)} async-done(((f32[2048,2,256]{2,0,1:T(8,128)}), f32[2048,1,256]{2,0,1:T(8,128)}) %reduce-scatter.17.cloned.1.call-update) | async-done | bytes 2097168 | tf_op jit(solution)/shard_map/reduce_scatter | solution.py:320
  1755.6 57.3 %reduce-scatter.15.cloned.1.call-done = f32[1,256,2048]{2,1,0:T(8,128)} async-done(((f32[2,256,2048]{2,1,0:T(8,128)}), f32[1,256,2048]{2,1,0:T(8,128)}) %reduce-scatter.15.cloned.1.call-update) | async-done | bytes 2097168 | tf_op jit(solution)/shard_map/reduce_scatter | solution.py:319
  (235 shorter events, 72.3 us)
Async XLA Ops:
  7.2 156.8 %all-gather.3.cloned.1.call-start = ((), (), s32[]{:S(2)}) async-start(), calls=%async_computation.6 | async-start | bytes 10485760 | tf_op jit(solution)/shard_map/all_gather | solution.py:189
  10.8 303.1 %all-gather.5.cloned.1.call-start = ((), (), s32[]{:S(2)}) async-start(), calls=%async_computation.7 | async-start | bytes 10485760 | tf_op jit(solution)/shard_map/all_gather | solution.py:190
  12.7 928.2 %reduce-scatter.11.cloned.1.call-start = ((), (), s32[]{:S(2)}) async-start(), calls=%async_computation.10 | async-start | bytes 20971520 | tf_op jit(solution)/shard_map/reduce_scatter | solution.py:303
  13.4 12.9 copy-start.59
  27.4 286.5 %copy-start.38 = (pred[2048]{0:T(1024)(128)(4,1)S(1)}, pred[2048]{0:T(1024)(128)(4,1)}, u32[]{:S(2)}) copy-start(pred[2048]{0:T(1024)(128)(4,1)} %copy-done.37) | copy-start | bytes 6148
  27.4 286.5 %copy-start.55 = (f32[2048]{0:T(1024)S(1)}, f32[2048]{0:T(1024)}, u32[]{:S(2)}) copy-start(f32[2048]{0:T(1024)} %param.27) | copy-start | bytes 24580
  27.4 286.5 %copy-start.56 = (f32[2048]{0:T(1024)S(1)}, f32[2048]{0:T(1024)}, u32[]{:S(2)}) copy-start(f32[2048]{0:T(1024)} %param.21) | copy-start | bytes 24580
  27.4 286.5 %copy-start.61 = (f32[2048]{0:T(1024)S(1)}, f32[2048]{0:T(1024)}, u32[]{:S(2)}) copy-start(f32[2048]{0:T(1024)} %param.30) | copy-start | bytes 24580
  27.4 286.5 %copy-start.62 = (f32[2048]{0:T(1024)S(1)}, f32[2048]{0:T(1024)}, u32[]{:S(2)}) copy-start(f32[2048]{0:T(1024)} %param.28) | copy-start | bytes 24580
  27.5 286.5 %copy-start.65 = (f32[2048]{0:T(1024)S(1)}, f32[2048]{0:T(1024)}, u32[]{:S(2)}) copy-start(f32[2048]{0:T(1024)} %param.22) | copy-start | bytes 24580
  27.5 286.5 %copy-start.68 = (f32[1536]{0:T(1024)S(1)}, f32[1536]{0:T(1024)}, u32[]{:S(2)}) copy-start(f32[1536]{0:T(1024)} %param.24) | copy-start | bytes 18436
  317.0 14.2 copy-start.66
  376.8 4.8 copy-start.4
  384.5 8.4 slice-start.4
  385.3 7.6 slice-start.5
  389.0 22.5 %copy-start.21 = (bf16[1,2048,2,256]{3,1,2,0:T(8,128)(2,1)}, bf16[1,2048,2,256]{3,1,2,0:T(8,128)(2,1)S(1)}, u32[]{:S(2)}) copy-start(bf16[1,2048,2,256]{3,1,2,0:T(8,128)(2,1)S(1)} %get-tuple-element.240) | copy-start | bytes 6291460 | tf_op jit(solution)/shard_map/cond
  389.0 22.5 %copy-start.32 = (bf16[1,2048,2,256]{3,1,2,0:T(8,128)(2,1)}, bf16[1,2048,2,256]{3,1,2,0:T(8,128)(2,1)S(1)}, u32[]{:S(2)}) copy-start(bf16[1,2048,2,256]{3,1,2,0:T(8,128)(2,1)S(1)} %get-tuple-element.241) | copy-start | bytes 6291460 | tf_op jit(solution)/shard_map/cond
  389.8 10.3 copy-start.43
  390.1 10.0 copy-start.45
  392.9 21.3 %copy-start.11 = (bf16[1,2048,2,256]{1,3,2,0:T(8,128)(2,1)}, bf16[1,2048,2,256]{1,3,2,0:T(8,128)(2,1)S(1)}, u32[]{:S(2)}) copy-start(bf16[1,2048,2,256]{1,3,2,0:T(8,128)(2,1)S(1)} %fusion.81) | copy-start | bytes 6291460 | tf_op jit(solution)/shard_map/cond
  400.3 5.8 copy-start.22
  400.3 13.9 copy-start.26
  401.7 4.4 copy-start.16
  404.9 81.4 %copy-start.2 = (f32[2,512,1024]{2,1,0:T(8,128)}, f32[2,512,1024]{2,1,0:T(8,128)S(1)}, u32[]{:S(2)}) copy-start(f32[2,512,1024]{2,1,0:T(8,128)S(1)} %get-tuple-element.228) | copy-start | bytes 12582916 | tf_op jit(solution)/shard_map/cond
  413.1 75.7 %copy-start.1 = (f32[2,512,1536]{2,1,0:T(8,128)}, f32[2,512,1536]{2,1,0:T(8,128)S(1)}, u32[]{:S(2)}) copy-start(f32[2,512,1536]{2,1,0:T(8,128)S(1)} %get-tuple-element.226) | copy-start | bytes 18874372 | tf_op jit(solution)/shard_map/cond
  417.7 5.5 copy-start.14
  428.3 9.6 copy-start.39
  428.3 62.4 %copy-start = (f32[2,512,2048]{2,1,0:T(8,128)}, f32[2,512,2048]{2,1,0:T(8,128)S(1)}, u32[]{:S(2)}) copy-start(f32[2,512,2048]{2,1,0:T(8,128)S(1)} %get-tuple-element.224) | copy-start | bytes 25165828 | tf_op jit(solution)/shard_map/cond
  429.6 8.3 copy-start.41
  465.1 8.1 copy-start.5
  465.1 8.1 copy-start.28
  481.8 4.5 copy-start.23
  490.7 4.2 copy-start.17
  535.5 16.9 copy-start.67
  575.1 13.3 copy-start.44
  575.1 13.3 copy-start.46
  588.4 5.1 slice-start.2
  590.7 5.1 slice-start
  593.8 6.9 slice-start.6
  596.2 4.5 slice-start.7
  663.0 561.2 %reduce-scatter.7.cloned.1.call-start = ((), (), s32[]{:S(2)}) async-start(), calls=%async_computation.8 | async-start | bytes 20971520 | tf_op jit(solution)/shard_map/reduce_scatter | solution.py:302
  663.6 965.4 %all-reduce.15.cloned.1.call-start = ((), (), s32[]{:S(2)}) async-start(), calls=%async_computation.14 | async-start | bytes 67108864 | tf_op jit(solution)/shard_map/psum | solution.py:323
  664.2 988.6 %reduce-scatter.13.cloned.1.call-start = ((), (), s32[]{:S(2)}) async-start(), calls=%async_computation.11 | async-start | bytes 1572864 | tf_op jit(solution)/shard_map/reduce_scatter | solution.py:318
  943.2 755.1 %reduce-scatter.9.cloned.1.call-start = ((), (), s32[]{:S(2)}) async-start(), calls=%async_computation.9 | async-start | bytes 4718592 | tf_op jit(solution)/shard_map/reduce_scatter | solution.py:317
  1228.0 527.7 %reduce-scatter.17.cloned.1.call-start = ((), (), s32[]{:S(2)}) async-start(), calls=%async_computation.13 | async-start | bytes 6291456 | tf_op jit(solution)/shard_map/reduce_scatter | solution.py:320
  1230.4 398.5 %copy-start.35 = (f32[2048]{0:T(1024)S(1)}, f32[2048]{0:T(1024)}, u32[]{:S(2)}) copy-start(f32[2048]{0:T(1024)} %get-tuple-element.197) | copy-start | bytes 24580
  1230.4 582.5 %reduce-scatter.15.cloned.1.call-start = ((), (), s32[]{:S(2)}) async-start(), calls=%async_computation.12 | async-start | bytes 6291456 | tf_op jit(solution)/shard_map/reduce_scatter | solution.py:319
  1281.8 531.1 %copy-start.60 = (f32[2048]{0:T(1024)}, f32[2048]{0:T(1024)S(1)}, u32[]{:S(2)}) copy-start(f32[2048]{0:T(1024)S(1)} %get-tuple-element.291) | copy-start | bytes 24580
  (33 other events, 90.9 us)
Sparse Core Ops, SparseCore 0:
  11.0 152.9 all-gather.2
  166.1 147.7 all-gather.4
  663.1 277.7 reduce-scatter.10
  943.1 281.0 reduce-scatter.6
  1228.1 400.8 all-reduce.14
  1631.6 20.3 reduce-scatter.12
  1654.9 43.4 reduce-scatter.8
  1701.2 54.3 reduce-scatter.16
  1758.5 54.3 reduce-scatter.14
where the time goes:
time: 1830 us; the launch traced here: 1820 us
  waiting for transfers between devices  1300 us (71%)
  matrix products  165 us (9%)
  other arithmetic  141 us (8%)
  local copies, waits for them, and re-layouts  103 us (6%)
  blocking collectives  87.2 us (5%)
    psum x1, waiting for transfers between devices, local(): lax.psum((branch_part, input_part), ('branch', 'tensor'))  309 us
    reduce_scatter x1, waiting for transfers between devices, local(): lax.psum_scatter(first_pack, 'dp', scatter_dimension=1, tiled=True)  281 us
    reduce_scatter x1, waiting for transfers between devices, local(): lax.psum_scatter(second_pack, 'dp', scatter_dimension=2, tiled=True)  277 us
    all_gather x1, waiting for transfers between devices, local(): lax.all_gather(second_local, 'dp', axis=1, tiled=True)  150 us
    all_gather x1, waiting for transfers between devices, local(): lax.all_gather(first_local, 'dp', axis=0, tiled=True)  127 us
    reduce_scatter x1, waiting for transfers between devices, local(): lax.psum_scatter(up_grads, 'branch', scatter_dimension=0, tiled=True)  57.3 us
    reduce_scatter x1, waiting for transfers between devices, local(): lax.psum_scatter(down_grads, 'branch', scatter_dimension=1, tiled=True)  57.3 us
    psum x1, blocking collectives, local(): lax.psum((norm1_gain_part, norm1_shift_part, norm2_gain_part, norm2_shift...  48.7 us
  transfers between devices with their start and end apart: 9, of which 8 were waited for; matrix products, arithmetic and copies ran while one was open for 3% of the time, Pallas kernels for 0%

commit v1 on v0

v1 whole, which is shorter than its diff:
```python
from functools import partial

import jax
import jax.numpy as jnp
from jax import lax
from jax.sharding import PartitionSpec as P

HEAD_DIM = 256
SEQ_LEN = 2048
QBLOCK = 512
ROT = 64
BF16 = jnp.bfloat16
F32 = jnp.float32

norm_eps = 1e-05
rope_base = 10000.0
masked_score = -1e30


def layer_norm(rows):
    row_mean = jnp.mean(rows, axis=-1, keepdims=True)
    centred = rows - row_mean
    inv_std = lax.rsqrt(jnp.mean(centred * centred, axis=-1, keepdims=True) + norm_eps)
    return centred * inv_std, inv_std


def rope_tables(length, rotary):
    half_rot = rotary // 2
    inv_freq = rope_base ** (-2.0 * jnp.arange(half_rot, dtype=F32) / rotary)
    phase_angle = jnp.arange(length, dtype=F32)[:, None] * inv_freq[None, :]
    return (jnp.cos(phase_angle), jnp.sin(phase_angle))


def rotate(values, cos_table, sin_table, rotary):
    half_rot = rotary // 2
    lead_part = values[..., :half_rot]
    tail_part = values[..., half_rot:rotary]
    cos_part = cos_table[:, None, :]
    sin_part = sin_table[:, None, :]
    return jnp.concatenate(
        [
            lead_part * cos_part - tail_part * sin_part,
            tail_part * cos_part + lead_part * sin_part,
            values[..., rotary:],
        ],
        axis=-1,
    )


def allow_block(block_idx, key_end, seq_valid):
    query_pos = block_idx * QBLOCK + jnp.arange(QBLOCK)
    key_pos = jnp.arange(key_end)
    earlier = key_pos[None, :] <= query_pos[:, None]
    itself = key_pos[None, :] == query_pos[:, None]
    return earlier & (seq_valid[None, :key_end] | itself)


def block_scores(query_block, key_rows, allowed, score_scale):
    scores = (
        jnp.einsum("qhd,khd->hqk", query_block, key_rows, preferred_element_type=F32)
        * score_scale
    )
    return jnp.where(allowed[None], scores, masked_score)


def attend_forward(query_rows, key_rows, value_rows, seq_valid):
    seq_len = query_rows.shape[0]
    score_scale = query_rows.shape[-1] ** (-0.5)
    attended_list = []
    total_list = []
    for block_idx in range(seq_len // QBLOCK):
        key_end = (block_idx + 1) * QBLOCK
        allowed = allow_block(block_idx, key_end, seq_valid)
        scores = block_scores(
            query_rows[block_idx * QBLOCK : key_end], key_rows[:key_end], allowed, score_scale
        )
        row_max = jnp.max(scores, axis=-1, keepdims=True)
        exp_scores = jnp.exp(scores - row_max)
        row_total = jnp.sum(exp_scores, axis=-1, keepdims=True)
        attn_probs = (exp_scores / row_total).astype(BF16)
        attended = jnp.einsum(
            "hqk,khd->qhd", attn_probs, value_rows[:key_end], preferred_element_type=F32
        )
        attended_list.append(attended.astype(BF16))
        total_list.append(row_max[..., 0] + jnp.log(row_total[..., 0]))
    return (jnp.concatenate(attended_list, axis=0), jnp.concatenate(total_list, axis=1))


def attend_backward(query_rows, key_rows, value_rows, attended_grad, log_total, seq_valid):
    seq_len, head_count, head_dim = query_rows.shape
    score_scale = head_dim ** (-0.5)
    query_grad_list = []
    key_grad = jnp.zeros((seq_len, head_count, head_dim), F32)
    value_grad = jnp.zeros((seq_len, head_count, head_dim), F32)
    for block_idx in range(seq_len // QBLOCK):
        key_end = (block_idx + 1) * QBLOCK
        query_block = query_rows[block_idx * QBLOCK : key_end]
        grad_block = attended_grad[block_idx * QBLOCK : key_end]
        allowed = allow_block(block_idx, key_end, seq_valid)
        scores = block_scores(query_block, key_rows[:key_end], allowed, score_scale)
        attn_probs = jnp.exp(scores - log_total[:, block_idx * QBLOCK : key_end, None])
        probs_grad = jnp.einsum(
            "qhd,khd->hqk", grad_block, value_rows[:key_end], preferred_element_type=F32
        )
        row_dot = jnp.sum(attn_probs * probs_grad, axis=-1, keepdims=True)
        score_grad = (attn_probs * (probs_grad - row_dot)).astype(BF16)
        query_grad_list.append(
            jnp.einsum(
                "hqk,khd->qhd", score_grad, key_rows[:key_end], preferred_element_type=F32
            )
            * score_scale
        )
        pad_rows = ((0, seq_len - key_end), (0, 0), (0, 0))
        key_term = (
            jnp.einsum("hqk,qhd->khd", score_grad, query_block, preferred_element_type=F32)
            * score_scale
        )
        value_term = jnp.einsum(
            "hqk,qhd->khd",
            attn_probs.astype(BF16),
            grad_block,
            preferred_element_type=F32,
        )
        key_grad = key_grad + jnp.pad(key_term, pad_rows)
        value_grad = value_grad + jnp.pad(value_term, pad_rows)
    return (jnp.concatenate(query_grad_list, axis=0), key_grad, value_grad)


CORE = [(0, 1), (1, 0), (2, 3), (3, 2)]
YAX = [(0, 2), (2, 0), (1, 3), (3, 1)]
XAX = [(0, 1), (1, 0)]


def core_swap(block):
    return lax.ppermute(block, "tensor", CORE)


def y_swap(block):
    return lax.ppermute(block, "tensor", YAX)


def x_swap(block):
    return lax.ppermute(block, "branch", XAX)


def pick(array, index, size, axis=0):
    return lax.dynamic_slice_in_dim(array, index * size, size, axis)


def chain_gather(shard, place, count):
    buffer = jnp.zeros((3 * count - 2,) + shard.shape, shard.dtype)
    buffer = lax.dynamic_update_slice_in_dim(buffer, shard[None], place + count - 1, 0)
    right = left = shard
    for step in range(count - 1):
        right = lax.ppermute(right, "dp", [(k, k + 1) for k in range(step, count - 1)])
        left = lax.ppermute(left, "dp", [(k + 1, k) for k in range(count - 1 - step)])
        buffer = lax.dynamic_update_slice_in_dim(buffer, right[None], place - 1 - step + count - 1, 0)
        buffer = lax.dynamic_update_slice_in_dim(buffer, left[None], place + 1 + step + count - 1, 0)
    return buffer[count - 1 : 2 * count - 1]


def chain_reduce(piece, place, count):
    right = left = None
    for step in range(count - 1):
        right_send = piece(jnp.minimum(count - 1 - step + place, count - 1))
        left_send = piece(jnp.maximum(place - (count - 1 - step), 0))
        if right is not None:
            right_send = right_send.astype(F32) + right.astype(F32)
            left_send = left_send.astype(F32) + left.astype(F32)
        right = lax.ppermute(right_send.astype(BF16), "dp", [(k, k + 1) for k in range(step + 1)])
        left = lax.ppermute(
            left_send.astype(BF16), "dp", [(count - 1 - k, count - 2 - k) for k in range(step + 1)]
        )
    return piece(place).astype(F32) + right.astype(F32) + left.astype(F32)


def add16(first, second):
    return (first.astype(F32) + second.astype(F32)).astype(BF16)


def plane_reduce(part, core, why, ex):
    rows = part.shape[0]
    half, quarter, eighth, sixteenth = rows // 2, rows // 4, rows // 8, rows // 16
    mine = pick(part, core, half)
    mine = add16(mine, core_swap(pick(part, 1 - core, half)))
    first, second = mine[:quarter], mine[quarter:]
    first_next = y_swap(pick(first, 1 - why, eighth))
    second_next = x_swap(pick(second, 1 - ex, eighth))
    first = add16(pick(first, why, eighth), first_next)
    second = add16(pick(second, ex, eighth), second_next)
    first_next = x_swap(pick(first, 1 - ex, sixteenth))
    second_next = y_swap(pick(second, 1 - why, sixteenth))
    first = pick(first, ex, sixteenth).astype(F32) + first_next.astype(F32)
    second = pick(second, why, sixteenth).astype(F32) + second_next.astype(F32)
    return first, second


def own_rows(array, core, why, ex):
    rows = array.shape[0]
    sixteenth = rows // 16
    first = core * 8 + why * 2 + ex
    second = core * 8 + 4 + ex * 2 + why
    return pick(array, first, sixteenth), pick(array, second, sixteenth)


def join(low_index, mine, other, axis=0):
    return jnp.where(
        low_index == 0,
        jnp.concatenate([mine, other], axis),
        jnp.concatenate([other, mine], axis),
    )


def plane_gather(first, second, core, why, ex):
    first_next, second_next = x_swap(first), y_swap(second)
    first, second = join(ex, first, first_next), join(why, second, second_next)
    first_next, second_next = y_swap(first), x_swap(second)
    first, second = join(why, first, first_next), join(ex, second, second_next)
    mine = jnp.concatenate([first, second], 0)
    return join(core, mine, core_swap(mine))


def local(
    tokens,
    lengths,
    valid_mask,
    ln1_gain,
    ln1_bias,
    qkv_weight,
    qkv_bias,
    out_weight,
    out_bias,
    ln2_gain,
    ln2_bias,
    up_weight,
    up_bias,
    down_weight,
    down_bias,
    out_grad,
    *,
    count,
):
    row_count, width = tokens.shape
    seq_count = row_count // SEQ_LEN
    ex = lax.axis_index("branch")
    tensor_at = lax.axis_index("tensor")
    why, core = tensor_at // 2, tensor_at % 2
    place = lax.axis_index("dp")
    qkv_cols = qkv_bias.shape[0] // 2
    head_rows = out_weight.shape[0] // 2
    units = up_bias.shape[0] // 2
    head_count = qkv_cols // (3 * HEAD_DIM)
    chunk = width // (2 * count)

    qkv_full = chain_gather(pick(qkv_weight, ex, qkv_cols, 1), place, count).reshape(width, qkv_cols)
    out_full = chain_gather(pick(out_weight, ex, head_rows, 0), place, count)
    out_full = out_full.transpose(1, 0, 2).reshape(head_rows, width)
    up_full = chain_gather(pick(up_weight, ex, units, 1), place, count).reshape(width, units)
    down_full = chain_gather(pick(down_weight, ex, units, 0), place, count)
    down_full = down_full.transpose(1, 0, 2).reshape(units, width)

    positions = jnp.arange(SEQ_LEN, dtype=jnp.int32)
    seq_valid = (valid_mask.reshape(seq_count, SEQ_LEN) == 1) & (
        positions[None, :] < lengths[:, None]
    )
    validity = seq_valid.reshape(row_count).astype(F32)
    unit_rows, inv_std = layer_norm(tokens.astype(F32))
    grad_rows = out_grad * validity.astype(BF16)[:, None]
    normed1 = (unit_rows * ln1_gain + ln1_bias).astype(BF16)
    normed2 = (unit_rows * ln2_gain + ln2_bias).astype(BF16)
    cos_table, sin_table = rope_tables(SEQ_LEN, ROT)

    projected = jnp.dot(normed1, qkv_full, preferred_element_type=F32) + pick(qkv_bias, ex, qkv_cols)
    projected = projected.reshape(row_count, head_count, 3, HEAD_DIM)
    query_rows = rotate(projected[:, :, 0], cos_table, sin_table, ROT).astype(BF16)
    key_rows = rotate(projected[:, :, 1], cos_table, sin_table, ROT).astype(BF16)
    value_rows = projected[:, :, 2].astype(BF16)
    attended, log_total = attend_forward(query_rows, key_rows, value_rows, seq_valid[0])
    attended = attended.reshape(row_count, head_rows)
    out_partial = jnp.einsum("rc,rd->cd", attended, grad_rows, preferred_element_type=F32).astype(BF16)
    out_reduced = chain_reduce(
        lambda j: pick(out_partial.reshape(head_rows, 2, count, chunk), j, 1, 2), place, count
    )[:, :, 0]
    attended_grad = jnp.einsum("rd,cd->rc", grad_rows, out_full, preferred_element_type=F32).astype(BF16)
    query_grad, key_grad, value_grad = attend_backward(
        query_rows,
        key_rows,
        value_rows,
        attended_grad.reshape(row_count, head_count, HEAD_DIM),
        log_total,
        seq_valid[0],
    )
    query_grad = rotate(query_grad, cos_table, -sin_table, ROT)
    key_grad = rotate(key_grad, cos_table, -sin_table, ROT)
    qkv_grad = (
        jnp.stack([query_grad, key_grad, value_grad], axis=2).reshape(row_count, qkv_cols).astype(BF16)
    )
    qkv_partial = jnp.einsum("rd,rc->dc", normed1, qkv_grad, preferred_element_type=F32).astype(BF16)
    qkv_reduced = chain_reduce(
        lambda j: pick(qkv_partial.reshape(2, count, chunk, qkv_cols), j, 1, 1), place, count
    )[:, 0]
    qkv_bias_part = jnp.sum(qkv_grad, axis=0, dtype=F32)
    normed1_grad = jnp.einsum("rc,dc->rd", qkv_grad, qkv_full, preferred_element_type=F32)

    hidden = jnp.dot(normed2, up_full, preferred_element_type=F32) + pick(up_bias, ex, units)
    activated, gelu_back = jax.vjp(partial(jax.nn.gelu, approximate=False), hidden)
    activated = activated.astype(BF16)
    down_partial = jnp.einsum("rf,rd->fd", activated, grad_rows, preferred_element_type=F32).astype(BF16)
    down_reduced = chain_reduce(
        lambda j: pick(down_partial.reshape(units, 2, count, chunk), j, 1, 2), place, count
    )[:, :, 0]
    branch_part = jnp.dot(attended, out_full, preferred_element_type=F32)
    branch_part = branch_part + jnp.dot(activated, down_full, preferred_element_type=F32)
    branch_part = branch_part.astype(BF16)
    branch_first, branch_second = plane_reduce(branch_part, core, why, ex)

    activated_grad = jnp.einsum("rd,fd->rf", grad_rows, down_full, preferred_element_type=F32)
    hidden_grad = gelu_back(activated_grad)[0].astype(BF16)
    up_partial = jnp.einsum("rd,rf->df", normed2, hidden_grad, preferred_element_type=F32).astype(BF16)
    up_reduced = chain_reduce(
        lambda j: pick(up_partial.reshape(2, count, chunk, units), j, 1, 1), place, count
    )[:, 0]
    up_bias_part = jnp.sum(hidden_grad, axis=0, dtype=F32)
    normed2_grad = jnp.einsum("rf,df->rd", hidden_grad, up_full, preferred_element_type=F32)
    input_part = (normed1_grad * ln1_gain + normed2_grad * ln2_gain).astype(BF16)
    input_first, input_second = plane_reduce(input_part, core, why, ex)

    shift_sum = out_bias + down_bias
    tokens_own = own_rows(tokens, core, why, ex)
    validity_own = own_rows(validity, core, why, ex)
    out_grad_own = own_rows(out_grad, core, why, ex)

    def output_of(token_rows, valid_rows, total):
        return (token_rows.astype(F32) + valid_rows[:, None] * (total + shift_sum)).astype(BF16)

    output_rows = plane_gather(
        output_of(tokens_own[0], validity_own[0], branch_first),
        output_of(tokens_own[1], validity_own[1], branch_second),
        core,
        why,
        ex,
    )

    def input_of(token_rows, grad_own, total):
        unit_own, inv_own = layer_norm(token_rows.astype(F32))
        back = inv_own * (
            total
            - jnp.mean(total, axis=-1, keepdims=True)
            - unit_own * jnp.mean(total * unit_own, axis=-1, keepdims=True)
        )
        return (grad_own.astype(F32) + back).astype(BF16)

    grad_input = plane_gather(
        input_of(tokens_own[0], out_grad_own[0], input_first),
        input_of(tokens_own[1], out_grad_own[1], input_second),
        core,
        why,
        ex,
    )

    vectors = jnp.concatenate(
        [
            jnp.sum(normed1_grad * unit_rows, axis=0),
            jnp.sum(normed1_grad, axis=0),
            jnp.sum(normed2_grad * unit_rows, axis=0),
            jnp.sum(normed2_grad, axis=0),
            jnp.sum(grad_rows, axis=0, dtype=F32),
            qkv_bias_part,
            up_bias_part,
        ]
    ).reshape(-1, 128)
    hops = [
        lax.ppermute(vectors, "dp", [(k, (k + hop) % count) for k in range(count)])
        for hop in range(1, count)
    ]
    vectors = sum(hops, vectors)
    norm_rows, bias_rows = 4 * width // 128, width // 128
    norms, bias_grad, biases = (
        vectors[:norm_rows],
        vectors[norm_rows : norm_rows + bias_rows].reshape(width),
        vectors[norm_rows + bias_rows :],
    )
    for swap in (core_swap, y_swap, x_swap):
        norms = norms + swap(norms)
    norms = norms.reshape(4, width)
    other = x_swap(biases).reshape(-1)
    biases = biases.reshape(-1)
    qkv_bias_grad = join(ex, biases[:qkv_cols], other[:qkv_cols])
    up_bias_grad = join(ex, biases[qkv_cols:], other[qkv_cols:])

    def share(reduced, axis_of_pair, axis):
        mine = lax.dynamic_index_in_dim(reduced, ex, axis_of_pair, keepdims=False)
        given = lax.dynamic_index_in_dim(reduced, 1 - ex, axis_of_pair, keepdims=False)
        return join(ex, mine, x_swap(given.astype(BF16)).astype(F32), axis)

    return (
        output_rows,
        grad_input,
        norms[0],
        norms[1],
        share(qkv_reduced, 0, 1),
        qkv_bias_grad,
        share(out_reduced, 1, 0),
        bias_grad,
        norms[2],
        norms[3],
        share(up_reduced, 0, 1),
        up_bias_grad,
        share(down_reduced, 1, 0),
        bias_grad,
    )


def solution(mesh):
    return jax.shard_map(
        partial(local, count=mesh.shape["dp"]),
        mesh=mesh,
        in_specs=(
            P("dp", None),
            P("dp"),
            P("dp"),
            P(),
            P(),
            P("dp", "tensor"),
            P("tensor"),
            P("tensor", "dp"),
            P(),
            P(),
            P(),
            P("dp", "tensor"),
            P("tensor"),
            P("tensor", "dp"),
            P(),
            P("dp", None),
        ),
        out_specs=(
            P("dp", None),
            P("dp", None),
            P(),
            P(),
            P(("branch", "dp"), "tensor"),
            P("tensor"),
            P("tensor", ("branch", "dp")),
            P(),
            P(),
            P(),
            P(("branch", "dp"), "tensor"),
            P("tensor"),
            P("tensor", ("branch", "dp")),
            P(),
        ),
        check_vma=False,
    )
```

time: 1830 us -> 818 us (0.45)
  waiting for transfers between devices: 1300 us -> 252 us
  starting transfers between devices: 0.37 us -> 149 us
  blocking collectives: 87.2 us -> 0 us
  other arithmetic: 141 us -> 105 us
    reduce_scatter x6 -> x0, waiting for transfers between devices: 718 us -> none  [the longest x1 281 us: local(): lax.psum_scatter(first_pack, 'dp', scatter_dimension=1, tiled=True)]
    psum x1 -> x0, waiting for transfers between devices: 309 us -> none  [local(): lax.psum((branch_part, input_part), ('branch', 'tensor'))]
    all_gather x2 -> x0, waiting for transfers between devices: 277 us -> none  [the longest x1 150 us: local(): lax.all_gather(second_local, 'dp', axis=1, tiled=True)]
    ppermute x0 -> x79, waiting for transfers between devices: none -> 252 us  [the longest x12 84.1 us: chain_gather(): lax.ppermute(left, 'dp', [(k + 1, k) for k in range(count - 1 - step)])]
    ppermute x0 -> x79, starting transfers between devices: none -> 149 us  [the longest x12 55.4 us: chain_reduce(): lax.ppermute(right_send.astype(BF16), 'dp', [(k, k + 1) for k in range(st...]
    psum x2 -> x0, blocking collectives: 87.2 us -> none  [the longest x1 48.7 us: local(): lax.psum((norm1_gain_part, norm1_shift_part, norm2_gain_part, norm2_shift...]
    dot_general x10 -> x16, matrix products: 104 us -> 166 us  [the longest x1 31.8 us: local(): jnp.dot(normed2, up_full, preferred_element_type=F32)]
    dynamic_update_slice x0 -> x28, local copies, waits for them, and re-layouts: none -> 36.2 us  [the longest x12 18.4 us: chain_gather(): lax.dynamic_update_slice_in_dim(buffer, right[None], place - 1 - step + c...]
  transfers between devices with their start and end apart: 9 -> 79, of which waited for: 8 -> 32; matrix products, arithmetic and copies ran while one was open for 3% -> 48% of each run, Pallas kernels for 0% -> 0%
where the time goes in v1:
time: 818 us; the launch traced here: 805 us
  waiting for transfers between devices  252 us (31%)
  matrix products  182 us (22%)
  starting transfers between devices  149 us (18%)
  local copies, waits for them, and re-layouts  113 us (14%)
  other arithmetic  105 us (13%)
    ppermute x12, waiting for transfers between devices, chain_gather(): lax.ppermute(left, 'dp', [(k + 1, k) for k in range(count - 1 - step)])  84.1 us
    ppermute x14, waiting for transfers between devices, x_swap(): return lax.ppermute(block, 'branch', XAX)  71.7 us
    ppermute x12, waiting for transfers between devices, chain_reduce(): lax.ppermute(right_send.astype(BF16), 'dp', [(k, k + 1) for k in range(st...  66.8 us
    ppermute x12, starting transfers between devices, chain_reduce(): lax.ppermute(right_send.astype(BF16), 'dp', [(k, k + 1) for k in range(st...  55.4 us
    dynamic_slice x19, local copies, waits for them, and re-layouts, pick(): return lax.dynamic_slice_in_dim(array, index * size, size, axis)  33.4 us
    dot_general x1, matrix products, local(): jnp.dot(normed2, up_full, preferred_element_type=F32)  31.8 us
    ppermute x12, starting transfers between devices, chain_gather(): lax.ppermute(right, 'dp', [(k, k + 1) for k in range(step, count - 1)])  27 us
    ppermute x9, waiting for transfers between devices, y_swap(): return lax.ppermute(block, 'tensor', YAX)  26.1 us
  transfers between devices with their start and end apart: 79, of which 32 were waited for; matrix products, arithmetic and copies ran while one was open for 48% of the time, Pallas kernels for 0%

profile of v1, /device:TPU:0, one launch (start us, length us, event | category | flops | bytes accessed | tf_op | source)
XLA Modules:
  0.0 804.5 jit_solution(15467632376065611071)
XLA Ops:
  3.2 6.3 collective-permute-start.6
  11.4 5.5 collective-permute-start.18
  26.3 4.5 convert_reduce_fusion
  34.9 5.7 fusion.12
  43.5 5.8 convert_reduce_fusion.1
  50.0 5.5 broadcast_in_dim.104
  57.1 5.4 fusion.7
  87.2 6.2 fusion.49
  109.0 15.2 %collective-permute-done.13 = bf16[512,1024]{1,0:T(8,128)(2,1)S(1)} collective-permute-done((bf16[512,1024]{1,0:T(8,128)(2,1)}, bf16[512,1024]{1,0:T(8,128)(2,1)S(1)}, u32[]{:S(2)}, u32[]{:S(2)}) %collective-permute-start.13) | collective-permute-done | bytes 1048608 | tf_op jit(solution)/shard_map/ppermute | solution.py:156
  129.1 11.9 %collective-permute-done.3 = bf16[512,768]{1,0:T(8,128)(2,1)S(1)} collective-permute-done((bf16[512,768]{1,0:T(8,128)(2,1)S(1)}, bf16[512,768]{1,0:T(8,128)(2,1)S(1)}, u32[]{:S(2)}, u32[]{:S(2)}) %collective-permute-start.3) | collective-permute-done | bytes 786464 | tf_op jit(solution)/shard_map/ppermute | solution.py:156
  142.6 20.9 %collective-permute-done.21 = bf16[1024,512]{0,1:T(8,128)(2,1)} collective-permute-done((bf16[1024,512]{0,1:T(8,128)(2,1)}, bf16[1024,512]{0,1:T(8,128)(2,1)}, u32[]{:S(2)}, u32[]{:S(2)}) %collective-permute-start.21) | collective-permute-done | bytes 1048608 | tf_op jit(solution)/shard_map/ppermute | solution.py:156
  174.0 11.9 %collective-permute-done.15 = bf16[512,1024]{1,0:T(8,128)(2,1)S(1)} collective-permute-done((bf16[512,1024]{1,0:T(8,128)(2,1)S(1)}, bf16[512,1024]{1,0:T(8,128)(2,1)S(1)}, u32[]{:S(2)}, u32[]{:S(2)}) %collective-permute-start.15) | collective-permute-done | bytes 1048608 | tf_op jit(solution)/shard_map/ppermute | solution.py:156
  189.5 13.3 %collective-permute-done.5 = bf16[512,768]{1,0:T(8,128)(2,1)S(1)} collective-permute-done((bf16[512,768]{1,0:T(8,128)(2,1)S(1)}, bf16[512,768]{1,0:T(8,128)(2,1)S(1)}, u32[]{:S(2)}, u32[]{:S(2)}) %collective-permute-start.5) | collective-permute-done | bytes 786464 | tf_op jit(solution)/shard_map/ppermute | solution.py:156
  207.5 10.4 %broadcast_add_fusion = f32[2048,768]{0,1:T(8,128)S(1)} fusion(f32[768]{0:T(1024)S(1)} %dynamic_slice.211, bf16[2048,2048]{1,0:T(8,128)(2,1)} %fusion.7, bf16[2048,768]{1,0:T(8,128)(2,1)} %bitcast.315), kind=kOutput, calls=%fused_computation.80 | convolution fusion | flops 6444023808 | bytes 17828864 | tf_op jit(solution)/shard_map/dot_general | solution.py:273
  247.4 8.7 %convolution_convert_fusion.1 = bf16[2048,768]{1,0:T(8,128)(2,1)} fusion(bf16[2048,2048]{1,0:T(8,128)(2,1)S(1)} %bitcast.308, bf16[2048,768]{0,1:T(8,128)(2,1)S(1)} %bitcast.317), kind=kOutput, calls=%fused_computation.71 | convolution fusion | flops 6444023808 | bytes 14680064 | tf_op jit(solution)/shard_map/rd,rc->dc/dot_general | solution.py:298
  259.4 4.5 constant_dynamic-slice_fusion.15
  266.5 10.5 %fusion.156 = f32[2048,2048]{1,0:T(8,128)} fusion(bf16[2048,768]{0,1:T(8,128)(2,1)S(1)} %bitcast.318, bf16[2048,768]{1,0:T(8,128)(2,1)S(1)} %bitcast.316), kind=kOutput, calls=%fused_computation.405 | convolution fusion | flops 6442450944 | bytes 23068672 | tf_op jit(solution)/shard_map/rc,dc->rd/dot_general | solution.py:303
  285.5 5.3 collective-permute-start.50
  301.8 5.2 collective-permute-start.60
  310.4 5.4 slice.276
  315.8 31.8 %multiply_convert_fusion = (bf16[2048,1024]{1,0:T(8,128)(2,1)}, f32[2048,1024]{1,0:T(8,128)}, f32[2048,1024]{1,0:T(8,128)}) fusion(f32[1024]{0:T(1024)S(1)} %copy-done.51, bf16[2048,1024]{1,0:T(8,128)(2,1)} %bitcast.311, bf16[2048,2048]{1,0:T(8,128)(2,1)S(1)} %bitcast.286, f32[2048]{0:T(1024)S(1)} %copy-done.56, f32[2048]{0:T(1024)S(1)} %copy-done.57, ...), kind=kOutput, calls=%fused_computation.26 | convolution fusion | flops 8753512448 | bytes 33591296 | tf_op jit(solution)/shard_map/dot_general | solution.py:305
  347.6 12.5 %fusion.35 = bf16[1024,2048]{1,0:T(8,128)(2,1)} fusion(bf16[2048,1024]{1,0:T(8,128)(2,1)} %get-tuple-element.34, bf16[2048,2048]{1,0:T(8,128)(2,1)S(1)} %bitcast.297, bf16[2048]{0:T(1024)(128)(2,1)S(1)} %get-tuple-element.30), kind=kOutput, calls=%fused_computation.66 | convolution fusion | flops 8596226048 | bytes 16781312 | tf_op jit(solution)/shard_map/rf,rd->fd/dot_general | solution.py:308
  360.1 14.2 %fusion.155 = f32[2048,2048]{1,0:T(8,128)} fusion(bf16[2048,1024]{1,0:T(8,128)(2,1)} %get-tuple-element.34, bf16[1024,2048]{0,1:T(8,128)(2,1)S(1)} %bitcast.309), kind=kOutput, calls=%fused_computation.404 | convolution fusion | flops 8589934592 | bytes 25165824 | tf_op jit(solution)/shard_map/dot_general | solution.py:313
  374.2 20.1 %convert_reduce_fusion.2 = (f32[1024]{0:T(1024)S(1)}, bf16[2048,1024]{1,0:T(8,128)(2,1)}) fusion(f32[2048,1024]{1,0:T(8,128)} %get-tuple-element.35, bf16[1024,2048]{0,1:T(8,128)(2,1)} %bitcast.310, bf16[2048,2048]{1,0:T(8,128)(2,1)} %param.31, bf16[2048]{0:T(1024)(128)(2,1)S(1)} %get-tuple-element.30, f32[2048,1024]{1,0:T(8,128)} %get-tuple-element.90, ...), kind=kOutput, calls=%fused_computation.22 | convolution fusion | flops 8629779456 | bytes 33566720 | tf_op jit(solution)/shard_map/rd,fd->rf/dot_general | solution.py:317
  394.3 14.3 %convolution_convert_fusion = bf16[2048,1024]{1,0:T(8,128)(2,1)} fusion(bf16[2048,1024]{1,0:T(8,128)(2,1)} %get-tuple-element.108, bf16[2048,2048]{1,0:T(8,128)(2,1)S(1)} %bitcast.286, f32[2048]{0:T(1024)S(1)} %copy-done.56, f32[2048]{0:T(1024)S(1)} %copy-done.57, f32[2048]{0:T(1024)S(1)} %add_rsqrt_fusion, f32[2048]{0:T(1024)S(1)} %broadcast_multiply_fusion), kind=kOutput, calls=%fused_computation.67 | convolution fusion | flops 8617197568 | bytes 16809984 | tf_op jit(solution)/shard_map/rd,rf->df/dot_general | solution.py:319
  408.7 22.7 %fusion.142 = (f32[2048]{0:T(1024)S(1)}, f32[2048]{0:T(1024)S(1)}, bf16[2048,2048]{1,0:T(8,128)(2,1)}, f32[2048]{0:T(1024)S(1)}, f32[2048]{0:T(1024)S(1)}) fusion(f32[2048]{0:T(1024)S(1)} %add_rsqrt_fusion, f32[2048]{0:T(1024)S(1)} %broadcast_multiply_fusion, bf16[2048,2048]{1,0:T(8,128)(2,1)} %param.16, f32[2048]{0:T(1024)S(1)} %copy-done.57, ...), kind=kOutput, calls=%fused_computation.392 | convolution fusion | flops 8644452352 | bytes 42008576 | tf_op jit(solution)/shard_map/rf,df->rd/dot_general | solution.py:324
  431.6 8.0 reshape.804
  439.6 9.6 %add_convert_fusion.1 = bf16[2048,2048]{1,0:T(8,128)(2,1)} fusion(f32[2048,2048]{1,0:T(8,128)} %fusion.155, bf16[256,2048]{0,1:T(8,128)(2,1)S(1)} %bitcast.314, bf16[512,1,256]{0,2,1:T(8,128)(2,1)S(1)} %copy-done.36, bf16[512,1,256]{0,2,1:T(8,128)(2,1)S(1)} %copy-done.34, bf16[512,1,256]{0,2,1:T(8,128)(2,1)S(1)} %copy-done.32, ...), kind=kOutput, calls=%fused_computation.17 | convolution fusion | flops 2160066560 | bytes 27262976 | tf_op jit(solution)/shard_map/dot_general | solution.py:312
  449.2 16.2 %constant_dynamic-slice_fusion.6 = (bf16[1024,2,1,256]{3,2,1,0:T(2,128)(2,1)}, bf16[1024,2,1,256]{3,2,1,0:T(2,128)(2,1)S(1)}, bf16[1024,2,1,256]{3,2,1,0:T(2,128...) fusion(bf16[1024,2,4,256]{3,2,1,0:T(4,128)(2,1)S(1)} %copy-done, ...), kind=kLoop, calls=%fused_computation.319 | loop fusion | bytes 14680092 | tf_op jit(solution)/shard_map/dynamic_slice | solution.py:147
  492.8 29.5 %collective-permute-done.51 = bf16[2,1,256,768]{3,2,1,0:T(8,128)(2,1)S(1)} collective-permute-done((bf16[2,1,256,768]{3,2,1,0:T(8,128)(2,1)S(1)}, bf16[2,1,256,768]{3,2,1,0:T(8,128)(2,1)S(1)}, u32[]{:S(2)}, u32[]{:S(2)}) %collective-permute-start.51) | collective-permute-done | bytes 786464 | tf_op jit(solution)/shard_map/ppermute | solution.py:170
  532.2 11.0 %collective-permute-done.72 = bf16[1024,2,1,256]{3,0,2,1:T(8,128)(2,1)S(1)} collective-permute-done((bf16[1024,2,1,256]{3,0,2,1:T(8,128)(2,1)S(1)}, bf16[1024,2,1,256]{3,0,2,1:T(8,128)(2,1)S(1)}, u32[]{:S(2)}, u32[]{:S(2)}) %collective-permute-start.72) | collective-permute-done | bytes 1048608 | tf_op jit(solution)/shard_map/ppermute | solution.py:170
  551.5 6.2 collective-permute-start.52
  560.7 10.5 %collective-permute-done.66 = bf16[2,1,256,1024]{3,2,1,0:T(8,128)(2,1)S(1)} collective-permute-done((bf16[2,1,256,1024]{3,2,1,0:T(8,128)(2,1)S(1)}, bf16[2,1,256,1024]{3,2,1,0:T(8,128)(2,1)S(1)}, u32[]{:S(2)}, u32[]{:S(2)}) %collective-permute-start.66) | collective-permute-done | bytes 1048608 | tf_op jit(solution)/shard_map/ppermute | solution.py:170
  573.5 5.4 add_convert_fusion.2
  590.3 16.5 %collective-permute-done.39 = bf16[256,2048]{1,0:T(8,128)(2,1)} collective-permute-done((bf16[256,2048]{1,0:T(8,128)(2,1)}, bf16[256,2048]{1,0:T(8,128)(2,1)}, u32[]{:S(2)}, u32[]{:S(2)}) %collective-permute-start.39) | collective-permute-done | bytes 1048608 | tf_op jit(solution)/shard_map/ppermute | solution.py:143
  612.3 14.2 %collective-permute-done.29 = bf16[256,2048]{1,0:T(8,128)(2,1)S(1)} collective-permute-done((bf16[256,2048]{1,0:T(8,128)(2,1)S(1)}, bf16[256,2048]{1,0:T(8,128)(2,1)S(1)}, u32[]{:S(2)}, u32[]{:S(2)}) %collective-permute-start.29) | collective-permute-done | bytes 1048608 | tf_op jit(solution)/shard_map/ppermute | solution.py:143
  643.0 6.2 collective-permute-done.30
  659.6 8.1 %collective-permute-done.27 = bf16[128,2048]{1,0:T(8,128)(2,1)S(1)} collective-permute-done((bf16[128,2048]{1,0:T(8,128)(2,1)S(1)}, bf16[128,2048]{1,0:T(8,128)(2,1)S(1)}, u32[]{:S(2)}, u32[]{:S(2)}) %collective-permute-start.27) | collective-permute-done | bytes 524320 | tf_op jit(solution)/shard_map/ppermute | solution.py:143
  679.0 5.1 collective-permute-start.73
  685.9 14.3 %collective-permute-done.28 = bf16[256,2048]{1,0:T(8,128)(2,1)S(1)} collective-permute-done((bf16[256,2048]{1,0:T(8,128)(2,1)S(1)}, bf16[256,2048]{1,0:T(8,128)(2,1)S(1)}, u32[]{:S(2)}, u32[]{:S(2)}) %collective-permute-start.28) | collective-permute-done | bytes 1048608 | tf_op jit(solution)/shard_map/ppermute | solution.py:139
  710.3 5.7 collective-permute-done.42
  727.5 4.8 collective-permute-start.74
  736.6 6.4 collective-permute-done.56
  743.1 13.3 %collective-permute-start.67 = (bf16[2,1,256,1024]{3,2,1,0:T(8,128)(2,1)S(1)}, bf16[2,1,256,1024]{3,2,1,0:T(8,128)(2,1)S(1)}, u32[]{:S(2)}, u32[]{:S(2)}) collective-permute-start(bf16[2,1,256,1024]{3,2,1,0:T(8,128)(2,1)S(1)} %copy-done.25), channel_id=1, source_target_pairs={{0,1},{1,2},{2,3},{4,5},{5,6},{6,7},{8,9},{9,10},{10,11},{12,13},{... | collective-permute-start | bytes 3145736 | tf_op jit(solution)/shard_map/ppermute | solution.py:170
  763.2 14.2 %collective-permute-done.67 = bf16[2,1,256,1024]{3,2,1,0:T(8,128)(2,1)S(1)} collective-permute-done((bf16[2,1,256,1024]{3,2,1,0:T(8,128)(2,1)S(1)}, bf16[2,1,256,1024]{3,2,1,0:T(8,128)(2,1)S(1)}, u32[]{:S(2)}, u32[]{:S(2)}) %collective-permute-start.67) | collective-permute-done | bytes 1048608 | tf_op jit(solution)/shard_map/ppermute | solution.py:170
  783.3 6.3 collective-permute-done.71
  791.3 6.1 maximum_select_fusion
  797.4 6.1 maximum_select_fusion.1
  (487 shorter events, 293.5 us)
Async XLA Ops:
  1.9 62.1 %collective-permute-start.7 = (bf16[256,512]{0,1:T(8,128)(2,1)S(1)}, bf16[256,512]{0,1:T(8,128)(2,1)}, u32[]{:S(2)}, u32[]{:S(2)}) collective-permute-start(bf16[256,512]{0,1:T(8,128)(2,1)S(1)} %copy.60), channel_id=1, source_target_pairs={{1,0},{2,1},{3,2},{5,4},{6,5},{7,6},{9,8},{10,9},{11,10},{13,12},{... | collective-permute-start | bytes 786440 | tf_op jit(solution)/shard_map/ppermute | solution.py:156
  3.2 62.1 %collective-permute-start.6 = (bf16[256,512]{0,1:T(8,128)(2,1)S(1)}, bf16[256,512]{0,1:T(8,128)(2,1)}, u32[]{:S(2)}, u32[]{:S(2)}) collective-permute-start(bf16[256,512]{0,1:T(8,128)(2,1)S(1)} %copy.60), channel_id=1, source_target_pairs={{0,1},{1,2},{2,3},{4,5},{5,6},{6,7},{8,9},{9,10},{10,11},{12,13},{... | collective-permute-start | bytes 786440 | tf_op jit(solution)/shard_map/ppermute | solution.py:155
  10.1 90.8 %collective-permute-start.19 = (bf16[1024,512]{0,1:T(8,128)(2,1)S(1)}, bf16[1024,512]{0,1:T(8,128)(2,1)}, u32[]{:S(2)}, u32[]{:S(2)}) collective-permute-start(bf16[1024,512]{0,1:T(8,128)(2,1)S(1)} %copy.61), channel_id=1, source_target_pairs={{1,0},{2,1},{3,2},{5,4},{6,5},{7,6},{9,8},{10,9},{11,10},{13,12},{... | collective-permute-start | bytes 3145736 | tf_op jit(solution)/shard_map/ppermute | solution.py:156
  11.4 90.8 %collective-permute-start.18 = (bf16[1024,512]{0,1:T(8,128)(2,1)S(1)}, bf16[1024,512]{0,1:T(8,128)(2,1)}, u32[]{:S(2)}, u32[]{:S(2)}) collective-permute-start(bf16[1024,512]{0,1:T(8,128)(2,1)S(1)} %copy.61), channel_id=1, source_target_pairs={{0,1},{1,2},{2,3},{4,5},{5,6},{6,7},{8,9},{9,10},{10,11},{12,13},{... | collective-permute-start | bytes 3145736 | tf_op jit(solution)/shard_map/ppermute | solution.py:155
  22.0 71.4 %collective-permute-start = (bf16[512,768]{1,0:T(8,128)(2,1)}, bf16[512,768]{1,0:T(8,128)(2,1)}, u32[]{:S(2)}, u32[]{:S(2)}) collective-permute-start(bf16[512,768]{1,0:T(8,128)(2,1)} %get-tuple-element.33), channel_id=1, source_target_pairs={{0,1},{1,2},{2,3},{4,5},{5,6},{6,7},{8,9},{9,10},{10,11},{12,13},{... | collective-permute-start | bytes 2359304 | tf_op jit(solution)/shard_map/ppermute | solution.py:155
  83.2 23.1 %collective-permute-start.12 = (bf16[512,1024]{1,0:T(8,128)(2,1)}, bf16[512,1024]{1,0:T(8,128)(2,1)S(1)}, u32[]{:S(2)}, u32[]{:S(2)}) collective-permute-start(bf16[512,1024]{1,0:T(8,128)(2,1)} %get-tuple-element.37), channel_id=1, source_target_pairs={{0,1},{1,2},{2,3},{4,5},{5,6},{6,7},{8,9},{9,10},{10,11},{12,13},{... | collective-permute-start | bytes 3145736 | tf_op jit(solution)/shard_map/ppermute | solution.py:155
  93.4 30.7 %collective-permute-start.13 = (bf16[512,1024]{1,0:T(8,128)(2,1)}, bf16[512,1024]{1,0:T(8,128)(2,1)S(1)}, u32[]{:S(2)}, u32[]{:S(2)}) collective-permute-start(bf16[512,1024]{1,0:T(8,128)(2,1)} %get-tuple-element.37), channel_id=1, source_target_pairs={{1,0},{2,1},{3,2},{5,4},{6,5},{7,6},{9,8},{10,9},{11,10},{13,12},{... | collective-permute-start | bytes 3145736 | tf_op jit(solution)/shard_map/ppermute | solution.py:156
  99.3 27.5 %collective-permute-start.2 = (bf16[512,768]{1,0:T(8,128)(2,1)}, bf16[512,768]{1,0:T(8,128)(2,1)S(1)}, u32[]{:S(2)}, u32[]{:S(2)}) collective-permute-start(bf16[512,768]{1,0:T(8,128)(2,1)} %collective-permute-done), channel_id=1, source_target_pairs={{1,2},{2,3},{5,6},{6,7},{9,10},{10,11},{13,14},{14,15},{17,18},{18... | collective-permute-start | bytes 2359304 | tf_op jit(solution)/shard_map/ppermute | solution.py:155
  101.0 40.0 %collective-permute-start.3 = (bf16[512,768]{1,0:T(8,128)(2,1)S(1)}, bf16[512,768]{1,0:T(8,128)(2,1)S(1)}, u32[]{:S(2)}, u32[]{:S(2)}) collective-permute-start(bf16[512,768]{1,0:T(8,128)(2,1)S(1)} %collective-permute-done.1), channel_id=1, source_target_pairs={{1,0},{2,1},{5,4},{6,5},{9,8},{10,9},{13,12},{14,13},{17,16},{18,1... | collective-permute-start | bytes 2359304 | tf_op jit(solution)/shard_map/ppermute | solution.py:156
  102.3 61.3 %collective-permute-start.21 = (bf16[1024,512]{0,1:T(8,128)(2,1)}, bf16[1024,512]{0,1:T(8,128)(2,1)}, u32[]{:S(2)}, u32[]{:S(2)}) collective-permute-start(bf16[1024,512]{0,1:T(8,128)(2,1)} %collective-permute-done.19), channel_id=1, source_target_pairs={{1,0},{2,1},{5,4},{6,5},{9,8},{10,9},{13,12},{14,13},{17,16},{18,1... | collective-permute-start | bytes 3145736 | tf_op jit(solution)/shard_map/ppermute | solution.py:156
  106.3 58.6 %collective-permute-start.20 = (bf16[1024,512]{0,1:T(8,128)(2,1)}, bf16[1024,512]{0,1:T(8,128)(2,1)}, u32[]{:S(2)}, u32[]{:S(2)}) collective-permute-start(bf16[1024,512]{0,1:T(8,128)(2,1)} %collective-permute-done.18), channel_id=1, source_target_pairs={{1,2},{2,3},{5,6},{6,7},{9,10},{10,11},{13,14},{14,15},{17,18},{18... | collective-permute-start | bytes 3145736 | tf_op jit(solution)/shard_map/ppermute | solution.py:155
  124.2 44.7 %collective-permute-start.14 = (bf16[512,1024]{1,0:T(8,128)(2,1)S(1)}, bf16[512,1024]{1,0:T(8,128)(2,1)}, u32[]{:S(2)}, u32[]{:S(2)}) collective-permute-start(bf16[512,1024]{1,0:T(8,128)(2,1)S(1)} %collective-permute-done.12), channel_id=1, source_target_pairs={{1,2},{2,3},{5,6},{6,7},{9,10},{10,11},{13,14},{14,15},{17,18},{18... | collective-permute-start | bytes 3145736 | tf_op jit(solution)/shard_map/ppermute | solution.py:155
  126.9 59.1 %collective-permute-start.15 = (bf16[512,1024]{1,0:T(8,128)(2,1)S(1)}, bf16[512,1024]{1,0:T(8,128)(2,1)S(1)}, u32[]{:S(2)}, u32[]{:S(2)}) collective-permute-start(bf16[512,1024]{1,0:T(8,128)(2,1)S(1)} %collective-permute-done.13), channel_id=1, source_target_pairs={{1,0},{2,1},{5,4},{6,5},{9,8},{10,9},{13,12},{14,13},{17,16},{18,1... | collective-permute-start | bytes 3145736 | tf_op jit(solution)/shard_map/ppermute | solution.py:156
  141.0 47.6 %collective-permute-start.4 = (bf16[512,768]{1,0:T(8,128)(2,1)S(1)}, bf16[512,768]{1,0:T(8,128)(2,1)S(1)}, u32[]{:S(2)}, u32[]{:S(2)}) collective-permute-start(bf16[512,768]{1,0:T(8,128)(2,1)S(1)} %collective-permute-done.2), channel_id=1, source_target_pairs={{2,3},{6,7},{10,11},{14,15},{18,19},{22,23},{26,27},{30,31}} | collective-permute-start | bytes 2359304 | tf_op jit(solution)/shard_map/ppermute | solution.py:155
  163.6 39.2 %collective-permute-start.5 = (bf16[512,768]{1,0:T(8,128)(2,1)S(1)}, bf16[512,768]{1,0:T(8,128)(2,1)S(1)}, u32[]{:S(2)}, u32[]{:S(2)}) collective-permute-start(bf16[512,768]{1,0:T(8,128)(2,1)S(1)} %collective-permute-done.3), channel_id=1, source_target_pairs={{1,0},{5,4},{9,8},{13,12},{17,16},{21,20},{25,24},{29,28}} | collective-permute-start | bytes 2359304 | tf_op jit(solution)/shard_map/ppermute | solution.py:156
  164.9 130.4 %collective-permute-start.23 = (bf16[1024,512]{0,1:T(8,128)(2,1)}, bf16[1024,512]{0,1:T(8,128)(2,1)}, u32[]{:S(2)}, u32[]{:S(2)}) collective-permute-start(bf16[1024,512]{0,1:T(8,128)(2,1)} %collective-permute-done.21), channel_id=1, source_target_pairs={{1,0},{5,4},{9,8},{13,12},{17,16},{21,20},{25,24},{29,28}} | collective-permute-start | bytes 3145736 | tf_op jit(solution)/shard_map/ppermute | solution.py:156
  168.9 122.6 %collective-permute-start.22 = (bf16[1024,512]{0,1:T(8,128)(2,1)}, bf16[1024,512]{0,1:T(8,128)(2,1)}, u32[]{:S(2)}, u32[]{:S(2)}) collective-permute-start(bf16[1024,512]{0,1:T(8,128)(2,1)} %collective-permute-done.20), channel_id=1, source_target_pairs={{2,3},{6,7},{10,11},{14,15},{18,19},{22,23},{26,27},{30,31}} | collective-permute-start | bytes 3145736 | tf_op jit(solution)/shard_map/ppermute | solution.py:155
  185.9 115.9 %collective-permute-start.16 = (bf16[512,1024]{1,0:T(8,128)(2,1)}, bf16[512,1024]{1,0:T(8,128)(2,1)}, u32[]{:S(2)}, u32[]{:S(2)}) collective-permute-start(bf16[512,1024]{1,0:T(8,128)(2,1)} %collective-permute-done.14), channel_id=1, source_target_pairs={{2,3},{6,7},{10,11},{14,15},{18,19},{22,23},{26,27},{30,31}} | collective-permute-start | bytes 3145736 | tf_op jit(solution)/shard_map/ppermute | solution.py:155
  281.9 27.4 %collective-permute-start.17 = (bf16[512,1024]{1,0:T(8,128)(2,1)S(1)}, bf16[512,1024]{1,0:T(8,128)(2,1)S(1)}, u32[]{:S(2)}, u32[]{:S(2)}) collective-permute-start(bf16[512,1024]{1,0:T(8,128)(2,1)S(1)} %copy-done.24), channel_id=1, source_target_pairs={{1,0},{5,4},{9,8},{13,12},{17,16},{21,20},{25,24},{29,28}} | collective-permute-start | bytes 3145736 | tf_op jit(solution)/shard_map/ppermute | solution.py:156
  285.5 190.6 %collective-permute-start.50 = (bf16[2,1,256,768]{3,2,1,0:T(8,128)(2,1)}, bf16[2,1,256,768]{3,2,1,0:T(8,128)(2,1)}, u32[]{:S(2)}, u32[]{:S(2)}) collective-permute-start(bf16[2,1,256,768]{3,2,1,0:T(8,128)(2,1)} %get-tuple-element.66), channel_id=1, source_target_pairs={{0,1},{4,5},{8,9},{12,13},{16,17},{20,21},{24,25},{28,29}} | collective-permute-start | bytes 2359304 | tf_op jit(solution)/shard_map/ppermute | solution.py:170
  291.5 194.9 %collective-permute-start.53 = (bf16[2,1,256,768]{3,2,1,0:T(8,128)(2,1)}, bf16[2,1,256,768]{3,2,1,0:T(8,128)(2,1)}, u32[]{:S(2)}, u32[]{:S(2)}) collective-permute-start(bf16[2,1,256,768]{3,2,1,0:T(8,128)(2,1)} %get-tuple-element.67), channel_id=1, source_target_pairs={{3,2},{7,6},{11,10},{15,14},{19,18},{23,22},{27,26},{31,30}} | collective-permute-start | bytes 2359304 | tf_op jit(solution)/shard_map/ppermute | solution.py:171
  295.3 172.7 %collective-permute-start.63 = (bf16[256,2,1,256]{3,0,2,1:T(8,128)(2,1)}, bf16[256,2,1,256]{3,0,2,1:T(8,128)(2,1)}, u32[]{:S(2)}, u32[]{:S(2)}) collective-permute-start(bf16[256,2,1,256]{3,0,2,1:T(8,128)(2,1)} %add_convert_fusion.21), channel_id=1, source_target_pairs={{3,2},{2,1},{1,0},{7,6},{6,5},{5,4},{11,10},{10,9},{9,8},{15,14},{... | collective-permute-start | bytes 786440 | tf_op jit(solution)/shard_map/ppermute | solution.py:171
  301.8 167.8 %collective-permute-start.60 = (bf16[256,2,1,256]{3,0,2,1:T(8,128)(2,1)}, bf16[256,2,1,256]{3,0,2,1:T(8,128)(2,1)}, u32[]{:S(2)}, u32[]{:S(2)}) collective-permute-start(bf16[256,2,1,256]{3,0,2,1:T(8,128)(2,1)} %add_convert_fusion.23), channel_id=1, source_target_pairs={{0,1},{1,2},{2,3},{4,5},{5,6},{6,7},{8,9},{9,10},{10,11},{12,13},{... | collective-permute-start | bytes 786440 | tf_op jit(solution)/shard_map/ppermute | solution.py:170
  431.5 46.8 %collective-permute-start.45 = (f32[94,128]{1,0:T(8,128)S(1)}, f32[94,128]{1,0:T(8,128)S(1)}, u32[]{:S(2)}, u32[]{:S(2)}) collective-permute-start(f32[94,128]{1,0:T(8,128)S(1)} %bitcast.323), channel_id=1, source_target_pairs={{0,2},{1,3},{2,0},{3,1},{4,6},{5,7},{6,4},{7,5},{8,10},{9,11},{10,... | collective-permute-start | bytes 144392 | tf_op jit(solution)/shard_map/ppermute | solution.py:373
  469.6 103.9 %collective-permute-start.34 = (bf16[1024,2048]{1,0:T(8,128)(2,1)S(1)}, bf16[1024,2048]{1,0:T(8,128)(2,1)}, u32[]{:S(2)}, u32[]{:S(2)}) collective-permute-start(bf16[1024,2048]{1,0:T(8,128)(2,1)S(1)} %constant_dynamic-slice_fusion.22), channel_id=1, source_target_pairs={{0,4},{4,0},{8,12},{12,8},{1,5},{5,1},{9,13},{13,9},{2,6},{6,2},{1... | collective-permute-start | bytes 12582920 | tf_op jit(solution)/shard_map/ppermute | solution.py:135
  478.3 46.5 %collective-permute-start.65 = (bf16[2,1,256,1024]{3,2,1,0:T(8,128)(2,1)S(1)}, bf16[2,1,256,1024]{3,2,1,0:T(8,128)(2,1)S(1)}, u32[]{:S(2)}, u32[]{:S(2)}) collective-permute-start(bf16[2,1,256,1024]{3,2,1,0:T(8,128)(2,1)S(1)} %copy-done.22), channel_id=1, source_target_pairs={{0,1},{4,5},{8,9},{12,13},{16,17},{20,21},{24,25},{28,29}} | collective-permute-start | bytes 3145736 | tf_op jit(solution)/shard_map/ppermute | solution.py:170
  482.0 40.3 %collective-permute-start.51 = (bf16[2,1,256,768]{3,2,1,0:T(8,128)(2,1)S(1)}, bf16[2,1,256,768]{3,2,1,0:T(8,128)(2,1)S(1)}, u32[]{:S(2)}, u32[]{:S(2)}) collective-permute-start(bf16[2,1,256,768]{3,2,1,0:T(8,128)(2,1)S(1)} %add_convert_fusion.20), channel_id=1, source_target_pairs={{0,1},{1,2},{4,5},{5,6},{8,9},{9,10},{12,13},{13,14},{16,17},{17,1... | collective-permute-start | bytes 2359304 | tf_op jit(solution)/shard_map/ppermute | solution.py:170
  488.4 43.1 %collective-permute-start.75 = (bf16[1024,2,1,256]{3,0,2,1:T(8,128)(2,1)S(1)}, bf16[1024,2,1,256]{3,0,2,1:T(8,128)(2,1)S(1)}, u32[]{:S(2)}, u32[]{:S(2)}) collective-permute-start(bf16[1024,2,1,256]{3,0,2,1:T(8,128)(2,1)S(1)} %copy-done.21), channel_id=1, source_target_pairs={{3,2},{7,6},{11,10},{15,14},{19,18},{23,22},{27,26},{31,30}} | collective-permute-start | bytes 3145736 | tf_op jit(solution)/shard_map/ppermute | solution.py:171
  490.4 52.9 %collective-permute-start.72 = (bf16[1024,2,1,256]{3,0,2,1:T(8,128)(2,1)S(1)}, bf16[1024,2,1,256]{3,0,2,1:T(8,128)(2,1)S(1)}, u32[]{:S(2)}, u32[]{:S(2)}) collective-permute-start(bf16[1024,2,1,256]{3,0,2,1:T(8,128)(2,1)S(1)} %copy.72), channel_id=1, source_target_pairs={{0,1},{4,5},{8,9},{12,13},{16,17},{20,21},{24,25},{28,29}} | collective-permute-start | bytes 3145736 | tf_op jit(solution)/shard_map/ppermute | solution.py:170
  522.3 62.2 %collective-permute-start.24 = (bf16[1024,2048]{1,0:T(8,128)(2,1)}, bf16[1024,2048]{1,0:T(8,128)(2,1)}, u32[]{:S(2)}, u32[]{:S(2)}) collective-permute-start(bf16[1024,2048]{1,0:T(8,128)(2,1)} %constant_dynamic-slice_fusion.27), channel_id=1, source_target_pairs={{0,4},{4,0},{8,12},{12,8},{1,5},{5,1},{9,13},{13,9},{2,6},{6,2},{1... | collective-permute-start | bytes 12582920 | tf_op jit(solution)/shard_map/ppermute | solution.py:135
  530.8 28.1 %collective-permute-start.68 = (bf16[2,1,256,1024]{3,2,1,0:T(8,128)(2,1)S(1)}, bf16[2,1,256,1024]{3,2,1,0:T(8,128)(2,1)S(1)}, u32[]{:S(2)}, u32[]{:S(2)}) collective-permute-start(bf16[2,1,256,1024]{3,2,1,0:T(8,128)(2,1)S(1)} %get-tuple-element.59), channel_id=1, source_target_pairs={{3,2},{7,6},{11,10},{15,14},{19,18},{23,22},{27,26},{31,30}} | collective-permute-start | bytes 3145736 | tf_op jit(solution)/shard_map/ppermute | solution.py:171
  543.3 27.9 %collective-permute-start.66 = (bf16[2,1,256,1024]{3,2,1,0:T(8,128)(2,1)S(1)}, bf16[2,1,256,1024]{3,2,1,0:T(8,128)(2,1)S(1)}, u32[]{:S(2)}, u32[]{:S(2)}) collective-permute-start(bf16[2,1,256,1024]{3,2,1,0:T(8,128)(2,1)S(1)} %add_convert_fusion.12), channel_id=1, source_target_pairs={{0,1},{1,2},{4,5},{5,6},{8,9},{9,10},{12,13},{13,14},{16,17},{17,1... | collective-permute-start | bytes 3145736 | tf_op jit(solution)/shard_map/ppermute | solution.py:170
  551.5 172.1 %collective-permute-start.52 = (bf16[2,1,256,768]{3,2,1,0:T(8,128)(2,1)}, bf16[2,1,256,768]{3,2,1,0:T(8,128)(2,1)}, u32[]{:S(2)}, u32[]{:S(2)}) collective-permute-start(bf16[2,1,256,768]{3,2,1,0:T(8,128)(2,1)} %get-tuple-element.64), channel_id=1, source_target_pairs={{0,1},{1,2},{2,3},{4,5},{5,6},{6,7},{8,9},{9,10},{10,11},{12,13},{... | collective-permute-start | bytes 2359304 | tf_op jit(solution)/shard_map/ppermute | solution.py:170
  558.9 112.5 %collective-permute-start.76 = (bf16[1024,2,1,256]{3,0,2,1:T(8,128)(2,1)}, bf16[1024,2,1,256]{3,0,2,1:T(8,128)(2,1)}, u32[]{:S(2)}, u32[]{:S(2)}) collective-permute-start(bf16[1024,2,1,256]{3,0,2,1:T(8,128)(2,1)} %add_convert_fusion.6), channel_id=1, source_target_pairs={{3,2},{2,1},{7,6},{6,5},{11,10},{10,9},{15,14},{14,13},{19,18},{18... | collective-permute-start | bytes 3145736 | tf_op jit(solution)/shard_map/ppermute | solution.py:171
  580.4 26.3 %collective-permute-start.39 = (bf16[256,2048]{1,0:T(8,128)(2,1)}, bf16[256,2048]{1,0:T(8,128)(2,1)}, u32[]{:S(2)}, u32[]{:S(2)}) collective-permute-start(bf16[256,2048]{1,0:T(8,128)(2,1)} %constant_dynamic-slice_fusion.19), channel_id=1, source_target_pairs={{0,16},{16,0},{1,17},{17,1},{2,18},{18,2},{3,19},{19,3},{4,20},{20... | collective-permute-start | bytes 3145736 | tf_op jit(solution)/shard_map/ppermute | solution.py:143
  583.2 27.0 %collective-permute-start.35 = (bf16[256,2048]{1,0:T(8,128)(2,1)}, bf16[256,2048]{1,0:T(8,128)(2,1)}, u32[]{:S(2)}, u32[]{:S(2)}) collective-permute-start(bf16[256,2048]{1,0:T(8,128)(2,1)} %constant_dynamic-slice_fusion.21), channel_id=1, source_target_pairs={{0,8},{8,0},{4,12},{12,4},{1,9},{9,1},{5,13},{13,5},{2,10},{10,2},... | collective-permute-start | bytes 3145736 | tf_op jit(solution)/shard_map/ppermute | solution.py:139
  589.4 37.0 %collective-permute-start.29 = (bf16[256,2048]{1,0:T(8,128)(2,1)S(1)}, bf16[256,2048]{1,0:T(8,128)(2,1)S(1)}, u32[]{:S(2)}, u32[]{:S(2)}) collective-permute-start(bf16[256,2048]{1,0:T(8,128)(2,1)S(1)} %constant_dynamic-slice_fusion.24), channel_id=1, source_target_pairs={{0,16},{16,0},{1,17},{17,1},{2,18},{18,2},{3,19},{19,3},{4,20},{20... | collective-permute-start | bytes 3145736 | tf_op jit(solution)/shard_map/ppermute | solution.py:143
  606.8 26.0 %collective-permute-start.25 = (bf16[256,2048]{1,0:T(8,128)(2,1)S(1)}, bf16[256,2048]{1,0:T(8,128)(2,1)S(1)}, u32[]{:S(2)}, u32[]{:S(2)}) collective-permute-start(bf16[256,2048]{1,0:T(8,128)(2,1)S(1)} %constant_dynamic-slice_fusion.26), channel_id=1, source_target_pairs={{0,8},{8,0},{4,12},{12,4},{1,9},{9,1},{5,13},{13,5},{2,10},{10,2},... | collective-permute-start | bytes 3145736 | tf_op jit(solution)/shard_map/ppermute | solution.py:139
  610.2 32.8 %collective-permute-start.40 = (bf16[128,2048]{1,0:T(8,128)(2,1)S(1)}, bf16[128,2048]{1,0:T(8,128)(2,1)S(1)}, u32[]{:S(2)}, u32[]{:S(2)}) collective-permute-start(bf16[128,2048]{1,0:T(8,128)(2,1)S(1)} %constant_dynamic-slice_fusion.18), channel_id=1, source_target_pairs={{0,8},{8,0},{4,12},{12,4},{1,9},{9,1},{5,13},{13,5},{2,10},{10,2},... | collective-permute-start | bytes 1572872 | tf_op jit(solution)/shard_map/ppermute | solution.py:139
  670.1 30.1 %collective-permute-start.28 = (bf16[256,2048]{1,0:T(8,128)(2,1)S(1)}, bf16[256,2048]{1,0:T(8,128)(2,1)S(1)}, u32[]{:S(2)}, u32[]{:S(2)}) collective-permute-start(bf16[256,2048]{1,0:T(8,128)(2,1)S(1)} %maximum_select_fusion.9), channel_id=1, source_target_pairs={{0,8},{8,0},{4,12},{12,4},{1,9},{9,1},{5,13},{13,5},{2,10},{10,2},... | collective-permute-start | bytes 3145736 | tf_op jit(solution)/shard_map/ppermute | solution.py:139
  671.4 32.5 %collective-permute-start.32 = (bf16[256,2048]{1,0:T(8,128)(2,1)S(1)}, bf16[256,2048]{1,0:T(8,128)(2,1)S(1)}, u32[]{:S(2)}, u32[]{:S(2)}) collective-permute-start(bf16[256,2048]{1,0:T(8,128)(2,1)S(1)} %maximum_select_fusion.10), channel_id=1, source_target_pairs={{0,16},{16,0},{1,17},{17,1},{2,18},{18,2},{3,19},{19,3},{4,20},{20... | collective-permute-start | bytes 3145736 | tf_op jit(solution)/shard_map/ppermute | solution.py:143
  679.0 27.6 %collective-permute-start.73 = (bf16[1024,2,1,256]{3,0,2,1:T(8,128)(2,1)S(1)}, bf16[1024,2,1,256]{3,0,2,1:T(8,128)(2,1)}, u32[]{:S(2)}, u32[]{:S(2)}) collective-permute-start(bf16[1024,2,1,256]{3,0,2,1:T(8,128)(2,1)S(1)} %copy-done.26), channel_id=1, source_target_pairs={{0,1},{1,2},{4,5},{5,6},{8,9},{9,10},{12,13},{13,14},{16,17},{17,1... | collective-permute-start | bytes 3145736 | tf_op jit(solution)/shard_map/ppermute | solution.py:170
  684.4 40.9 %collective-permute-start.55 = (bf16[2,1,256,768]{3,2,1,0:T(8,128)(2,1)}, bf16[2,1,256,768]{3,2,1,0:T(8,128)(2,1)}, u32[]{:S(2)}, u32[]{:S(2)}) collective-permute-start(bf16[2,1,256,768]{3,2,1,0:T(8,128)(2,1)} %add_convert_fusion.17), channel_id=1, source_target_pairs={{3,2},{2,1},{1,0},{7,6},{6,5},{5,4},{11,10},{10,9},{9,8},{15,14},{... | collective-permute-start | bytes 2359304 | tf_op jit(solution)/shard_map/ppermute | solution.py:171
  706.6 84.7 %collective-permute-start.33 = (bf16[1024,2048]{1,0:T(8,128)(2,1)S(1)}, bf16[1024,2048]{1,0:T(8,128)(2,1)S(1)}, u32[]{:S(2)}, u32[]{:S(2)}) collective-permute-start(bf16[1024,2048]{1,0:T(8,128)(2,1)S(1)} %pad_maximum_fusion), channel_id=1, source_target_pairs={{0,4},{4,0},{8,12},{12,8},{1,5},{5,1},{9,13},{13,9},{2,6},{6,2},{1... | collective-permute-start | bytes 12582920 | tf_op jit(solution)/shard_map/ppermute | solution.py:135
  718.7 37.6 %collective-permute-start.77 = (bf16[1024,2,1,256]{3,0,2,1:T(8,128)(2,1)}, bf16[1024,2,1,256]{3,0,2,1:T(8,128)(2,1)}, u32[]{:S(2)}, u32[]{:S(2)}) collective-permute-start(bf16[1024,2,1,256]{3,0,2,1:T(8,128)(2,1)} %add_convert_fusion.5), channel_id=1, source_target_pairs={{3,2},{2,1},{1,0},{7,6},{6,5},{5,4},{11,10},{10,9},{9,8},{15,14},{... | collective-permute-start | bytes 3145736 | tf_op jit(solution)/shard_map/ppermute | solution.py:171
  725.2 72.2 %collective-permute-start.43 = (bf16[1024,2048]{1,0:T(8,128)(2,1)}, bf16[1024,2048]{1,0:T(8,128)(2,1)S(1)}, u32[]{:S(2)}, u32[]{:S(2)}) collective-permute-start(bf16[1024,2048]{1,0:T(8,128)(2,1)} %pad_maximum_fusion.1), channel_id=1, source_target_pairs={{0,4},{4,0},{8,12},{12,8},{1,5},{5,1},{9,13},{13,9},{2,6},{6,2},{1... | collective-permute-start | bytes 12582920 | tf_op jit(solution)/shard_map/ppermute | solution.py:135
  727.5 32.2 %collective-permute-start.74 = (bf16[1024,2,1,256]{3,0,2,1:T(8,128)(2,1)}, bf16[1024,2,1,256]{3,0,2,1:T(8,128)(2,1)S(1)}, u32[]{:S(2)}, u32[]{:S(2)}) collective-permute-start(bf16[1024,2,1,256]{3,0,2,1:T(8,128)(2,1)} %add_convert_fusion.7), channel_id=1, source_target_pairs={{0,1},{1,2},{2,3},{4,5},{5,6},{6,7},{8,9},{9,10},{10,11},{12,13},{... | collective-permute-start | bytes 3145736 | tf_op jit(solution)/shard_map/ppermute | solution.py:170
  743.1 34.3 %collective-permute-start.67 = (bf16[2,1,256,1024]{3,2,1,0:T(8,128)(2,1)S(1)}, bf16[2,1,256,1024]{3,2,1,0:T(8,128)(2,1)S(1)}, u32[]{:S(2)}, u32[]{:S(2)}) collective-permute-start(bf16[2,1,256,1024]{3,2,1,0:T(8,128)(2,1)S(1)} %copy-done.25), channel_id=1, source_target_pairs={{0,1},{1,2},{2,3},{4,5},{5,6},{6,7},{8,9},{9,10},{10,11},{12,13},{... | collective-permute-start | bytes 3145736 | tf_op jit(solution)/shard_map/ppermute | solution.py:170
  (101 other events, 1629.2 us)

commit v2 on v1

v2 whole, which is shorter than its diff:
```python
from functools import partial

import jax
import jax.numpy as jnp
from jax import lax
from jax.experimental import pallas as pl
from jax.experimental.pallas import tpu as pltpu
from jax.sharding import PartitionSpec as P

HEAD_DIM = 256
SEQ_LEN = 2048
ROT = 64
LANES = 128
BF16 = jnp.bfloat16
F32 = jnp.float32

norm_eps = 1e-05
rope_base = 10000.0
masked_score = -1e30


def rope_tables(length, rotary):
    half_rot = rotary // 2
    inv_freq = rope_base ** (-2.0 * jnp.arange(half_rot, dtype=F32) / rotary)
    phase_angle = jnp.arange(length, dtype=F32)[:, None] * inv_freq[None, :]
    return (jnp.cos(phase_angle), jnp.sin(phase_angle))


def rope_back_cols(grad, cos_t, sin_t):
    half = ROT // 2
    lead, tail = grad[:half], grad[half:ROT]
    return jnp.concatenate(
        [lead * cos_t + tail * sin_t, tail * cos_t - lead * sin_t, grad[ROT:]], axis=0
    )


def nn(first, second):
    return lax.dot_general(first, second, (((1,), (0,)), ((), ())), preferred_element_type=F32)


def nt(first, second):
    return lax.dot_general(first, second, (((1,), (1,)), ((), ())), preferred_element_type=F32)


def project_kernel(rows_ref, weight_ref, bias_ref, cos_ref, ahead_ref, behind_ref, out_ref):
    out = nn(rows_ref[...], weight_ref[...]) + bias_ref[...]
    half = ROT // 2
    for part in range(2):
        base = part * HEAD_DIM
        lead = out[:, base : base + LANES]
        turned = (
            lead * cos_ref[...]
            + pltpu.roll(lead, LANES - half, 1) * ahead_ref[...]
            + pltpu.roll(lead, half, 1) * behind_ref[...]
        )
        scale = HEAD_DIM**-0.5 if part == 0 else 1.0
        out_ref[:, base : base + LANES] = (turned * scale).astype(BF16)
        rest = out[:, base + LANES : base + HEAD_DIM]
        out_ref[:, base + LANES : base + HEAD_DIM] = (rest * scale).astype(BF16)
    out_ref[:, 2 * HEAD_DIM :] = out[:, 2 * HEAD_DIM :].astype(BF16)


def params(limit=None):
    return pltpu.CompilerParams(dimension_semantics=("arbitrary",), vmem_limit_bytes=limit)


def cost(flops, bytes_accessed, transcendentals=0):
    return pl.CostEstimate(
        flops=flops // 1000, transcendentals=0, bytes_accessed=bytes_accessed // 1000
    )


def project(rows, weight, bias, tables, block=512):
    count, width = rows.shape
    cols = bias.shape[1]
    table_spec = pl.BlockSpec((block, LANES), lambda i: (i, 0))
    return pl.pallas_call(
        project_kernel,
        grid=(count // block,),
        in_specs=[
            pl.BlockSpec((block, width), lambda i: (i, 0)),
            pl.BlockSpec((width, cols), lambda i: (0, 0)),
            pl.BlockSpec((1, cols), lambda i: (0, 0)),
            table_spec,
            table_spec,
            table_spec,
        ],
        out_specs=pl.BlockSpec((block, cols), lambda i: (i, 0)),
        out_shape=jax.ShapeDtypeStruct((count, cols), BF16),
        compiler_params=params(),
        cost_estimate=cost(2 * count * width * cols, 2 * (count * width + width * cols + count * cols)),
        name="project",
    )(rows, weight, bias, *tables)


def spread(column, width):
    return jnp.concatenate([column] * (width // LANES), axis=1)


def masked(scores, bias, block_idx, block):
    start = block_idx * block
    own = scores[start:]
    key_at = lax.broadcasted_iota(jnp.int32, own.shape, 0)
    query_at = lax.broadcasted_iota(jnp.int32, own.shape, 1)
    shift = spread(bias, block)
    own = jnp.where(
        key_at < query_at, own + shift[start:], jnp.where(key_at == query_at, own, masked_score)
    )
    if block_idx == 0:
        return own
    return jnp.concatenate([scores[:start] + shift[:start], own], axis=0)


def attend_kernel(query_ref, key_ref, value_ref, bias_ref, out_ref, total_ref, value_t, *, block):
    at = pl.program_id(0)

    @pl.when(at == 0)
    def _():
        value_t[...] = value_ref[...].T

    for block_idx in range(key_ref.shape[0] // block):

        @pl.when(at == block_idx)
        def _(block_idx=block_idx):
            end = (block_idx + 1) * block
            scores = masked(
                nt(key_ref[:end], query_ref[...]), bias_ref[:end], block_idx, block
            )
            top = jnp.max(scores, axis=0, keepdims=True)
            weights = jnp.exp(scores - top)
            total = jnp.sum(weights, axis=0, keepdims=True)
            out = nn(value_t[:, :end], weights.astype(BF16)) / total
            out_ref[...] = out.T.astype(BF16)
            total_ref[...] = jnp.broadcast_to(top + jnp.log(total), total_ref.shape)


def attend(qkv, bias, block=512):
    count = qkv.shape[0]
    pairs = count * (count + block) // 2
    return pl.pallas_call(
        partial(attend_kernel, block=block),
        grid=(count // block,),
        in_specs=[
            pl.BlockSpec((block, HEAD_DIM), lambda i: (i, 0)),
            pl.BlockSpec((count, HEAD_DIM), lambda i: (0, 1)),
            pl.BlockSpec((count, HEAD_DIM), lambda i: (0, 2)),
            pl.BlockSpec((count, LANES), lambda i: (0, 0)),
        ],
        out_specs=[
            pl.BlockSpec((block, HEAD_DIM), lambda i: (i, 0)),
            pl.BlockSpec((8, block), lambda i: (0, i)),
        ],
        out_shape=[
            jax.ShapeDtypeStruct((count, HEAD_DIM), BF16),
            jax.ShapeDtypeStruct((8, count), F32),
        ],
        scratch_shapes=[pltpu.VMEM((HEAD_DIM, count), BF16)],
        compiler_params=params(),
        cost_estimate=cost(4 * pairs * HEAD_DIM, 8 * count * HEAD_DIM, pairs),
        name="attend",
    )(qkv, qkv, qkv, bias)


def attend_back_kernel(
    query_ref, key_ref, value_ref, grad_ref, total_ref, bias_ref, cos_ref, sin_ref,
    out_ref, sums_ref, key_t, key_grad, value_grad, *, block
):
    at = pl.program_id(0)
    count = key_ref.shape[0]
    blocks = count // block

    @pl.when(at == 0)
    def _():
        key_t[...] = key_ref[...].T
        key_grad[...] = jnp.zeros_like(key_grad)
        value_grad[...] = jnp.zeros_like(value_grad)
        sums_ref[...] = jnp.zeros_like(sums_ref)

    for block_idx in range(blocks):

        @pl.when(at == block_idx)
        def _(block_idx=block_idx):
            start, end = block_idx * block, (block_idx + 1) * block
            query, grad = query_ref[...], grad_ref[...]
            scores = masked(nt(key_ref[:end], query), bias_ref[:end], block_idx, block)
            probs = jnp.exp(scores - total_ref[0:1])
            probs_grad = nt(value_ref[:end], grad)
            dots = jnp.sum(probs * probs_grad, axis=0, keepdims=True)
            score_grad = (probs * (probs_grad - dots)).astype(BF16)
            value_grad[:end] += nn(probs.astype(BF16), grad)
            key_grad[:end] += nn(score_grad, query)
            query_grad = nn(key_t[:, :end], score_grad) * (HEAD_DIM**-0.5)
            query_grad = rope_back_cols(
                query_grad, cos_ref[:, start:end], sin_ref[:, start:end]
            ).T.astype(BF16)
            out_ref[start:end, :HEAD_DIM] = query_grad
            sums_ref[:, :HEAD_DIM] += jnp.sum(query_grad.astype(F32), axis=0, keepdims=True)

    @pl.when(at == blocks - 1)
    def _():
        turned = rope_back_cols(key_grad[...].T, cos_ref[...], sin_ref[...]).T.astype(BF16)
        out_ref[:, HEAD_DIM : 2 * HEAD_DIM] = turned
        sums_ref[:, HEAD_DIM : 2 * HEAD_DIM] = jnp.sum(turned.astype(F32), axis=0, keepdims=True)
        low = value_grad[...].astype(BF16)
        out_ref[:, 2 * HEAD_DIM :] = low
        sums_ref[:, 2 * HEAD_DIM :] = jnp.sum(low.astype(F32), axis=0, keepdims=True)


def attend_back(qkv, grad, total, bias, cos_t, sin_t, block=512):
    count = qkv.shape[0]
    pairs = count * (count + block) // 2
    half = ROT // 2
    return pl.pallas_call(
        partial(attend_back_kernel, block=block),
        grid=(count // block,),
        in_specs=[
            pl.BlockSpec((block, HEAD_DIM), lambda i: (i, 0)),
            pl.BlockSpec((count, HEAD_DIM), lambda i: (0, 1)),
            pl.BlockSpec((count, HEAD_DIM), lambda i: (0, 2)),
            pl.BlockSpec((block, HEAD_DIM), lambda i: (i, 0)),
            pl.BlockSpec((8, block), lambda i: (0, i)),
            pl.BlockSpec((count, LANES), lambda i: (0, 0)),
            pl.BlockSpec((half, count), lambda i: (0, 0)),
            pl.BlockSpec((half, count), lambda i: (0, 0)),
        ],
        out_specs=[
            pl.BlockSpec((count, 3 * HEAD_DIM), lambda i: (0, 0)),
            pl.BlockSpec((1, 3 * HEAD_DIM), lambda i: (0, 0)),
        ],
        out_shape=[
            jax.ShapeDtypeStruct((count, 3 * HEAD_DIM), BF16),
            jax.ShapeDtypeStruct((1, 3 * HEAD_DIM), F32),
        ],
        scratch_shapes=[
            pltpu.VMEM((HEAD_DIM, count), BF16),
            pltpu.VMEM((count, HEAD_DIM), F32),
            pltpu.VMEM((count, HEAD_DIM), F32),
        ],
        compiler_params=params(),
        cost_estimate=cost(10 * pairs * HEAD_DIM, 16 * count * HEAD_DIM, pairs),
        name="attend_back",
    )(qkv, qkv, qkv, grad, total, bias, cos_t, sin_t)


def up_kernel(rows_ref, weight_ref, bias_ref, act_ref, slope_ref, *, chunk):
    rows = rows_ref[...]
    for at in range(0, weight_ref.shape[1], chunk):
        span = slice(at, at + chunk)
        hidden = nn(rows, weight_ref[:, span]) + bias_ref[:, span]
        share = 0.5 + 0.5 * lax.erf(hidden * 0.7071067811865476)
        density = jnp.exp(hidden * hidden * -0.5) * 0.3989422804014327
        act_ref[:, span] = (hidden * share).astype(BF16)
        slope_ref[:, span] = (share + hidden * density).astype(slope_ref.dtype)


def up_gelu(rows, weight, bias, block=256, chunk=256):
    count, width = rows.shape
    units = weight.shape[1]
    out_spec = pl.BlockSpec((block, units), lambda i: (i, 0))
    return pl.pallas_call(
        partial(up_kernel, chunk=chunk),
        grid=(count // block,),
        in_specs=[
            pl.BlockSpec((block, width), lambda i: (i, 0)),
            pl.BlockSpec((width, units), lambda i: (0, 0)),
            pl.BlockSpec((1, units), lambda i: (0, 0)),
        ],
        out_specs=[out_spec, out_spec],
        out_shape=[
            jax.ShapeDtypeStruct((count, units), BF16),
            jax.ShapeDtypeStruct((count, units), F32),
        ],
        compiler_params=params(),
        cost_estimate=cost(
            2 * count * width * units, 2 * (count * width + width * units + 3 * count * units), count * units
        ),
        name="up_gelu",
    )(rows, weight, bias)


def slope_kernel(grad_ref, weight_ref, slope_ref, out_ref, sums_ref, *, chunk):
    @pl.when(pl.program_id(0) == 0)
    def _():
        sums_ref[...] = jnp.zeros_like(sums_ref)

    grad = grad_ref[...]
    for at in range(0, weight_ref.shape[1], chunk):
        span = slice(at, at + chunk)
        low = (nn(grad, weight_ref[:, span]) * slope_ref[:, span]).astype(BF16)
        out_ref[:, span] = low
        sums_ref[:, span] += jnp.sum(low.astype(F32), axis=0, keepdims=True)


def hidden_back(grad, weight, slope, block=256, chunk=256):
    count, width = grad.shape
    units = weight.shape[1]
    return pl.pallas_call(
        partial(slope_kernel, chunk=chunk),
        grid=(count // block,),
        in_specs=[
            pl.BlockSpec((block, width), lambda i: (i, 0)),
            pl.BlockSpec((width, units), lambda i: (0, 0)),
            pl.BlockSpec((block, units), lambda i: (i, 0)),
        ],
        out_specs=[
            pl.BlockSpec((block, units), lambda i: (i, 0)),
            pl.BlockSpec((1, units), lambda i: (0, 0)),
        ],
        out_shape=[
            jax.ShapeDtypeStruct((count, units), BF16),
            jax.ShapeDtypeStruct((1, units), F32),
        ],
        compiler_params=params(),
        cost_estimate=cost(2 * count * width * units, 2 * (count * width + width * units + 3 * count * units)),
        name="hidden_back",
    )(grad, weight, slope)


def dgrad_sums(grad_ref, weight_ref, rows_ref, mean, inv, dot_ref, sum_ref, span):
    normed = nt(grad_ref[...], weight_ref[span])
    unit = (rows_ref[:, span].astype(F32) - mean) * inv
    dot_ref[:, span] += jnp.sum(normed * unit, axis=0, keepdims=True)
    sum_ref[:, span] += jnp.sum(normed, axis=0, keepdims=True)
    return normed


def dgrad_first_kernel(
    grad_ref, weight_ref, rows_ref, mean_ref, inv_ref, gain_ref, out_ref, dot_ref, sum_ref, *, chunk
):
    @pl.when(pl.program_id(0) == 0)
    def _():
        dot_ref[...] = jnp.zeros_like(dot_ref)
        sum_ref[...] = jnp.zeros_like(sum_ref)

    mean, inv = mean_ref[...], inv_ref[...]
    for at in range(0, weight_ref.shape[0], chunk):
        span = slice(at, at + chunk)
        normed = dgrad_sums(grad_ref, weight_ref, rows_ref, mean, inv, dot_ref, sum_ref, span)
        out_ref[:, span] = normed * gain_ref[:, span]


def dgrad_half_kernel(
    half_ref, grad_ref, weight_ref, rows_ref, mean_ref, inv_ref, gain_ref, before_ref,
    out_ref, dot_ref, sum_ref, *, chunk
):
    @pl.when(pl.program_id(0) == 0)
    def _():
        dot_ref[...] = jnp.zeros_like(dot_ref)
        sum_ref[...] = jnp.zeros_like(sum_ref)

    mean, inv = mean_ref[...], inv_ref[...]
    for at in range(0, weight_ref.shape[0], chunk):
        span = slice(at, at + chunk)
        normed = dgrad_sums(grad_ref, weight_ref, rows_ref, mean, inv, dot_ref, sum_ref, span)
        out_ref[:, span] = (normed * gain_ref[:, span] + before_ref[:, span]).astype(BF16)


def dgrad_first(grad, weight, rows, mean, inv, gain, block=256, chunk=256):
    count, width = rows.shape
    cols = grad.shape[1]
    wide = pl.BlockSpec((block, width), lambda i: (i, 0))
    thin = pl.BlockSpec((block, 1), lambda i: (i, 0))
    vector = pl.BlockSpec((1, width), lambda i: (0, 0))
    return pl.pallas_call(
        partial(dgrad_first_kernel, chunk=chunk),
        grid=(count // block,),
        in_specs=[
            pl.BlockSpec((block, cols), lambda i: (i, 0)),
            pl.BlockSpec((width, cols), lambda i: (0, 0)),
            wide,
            thin,
            thin,
            vector,
        ],
        out_specs=[wide, vector, vector],
        out_shape=[
            jax.ShapeDtypeStruct((count, width), F32),
            jax.ShapeDtypeStruct((1, width), F32),
            jax.ShapeDtypeStruct((1, width), F32),
        ],
        compiler_params=params(),
        cost_estimate=cost(2 * count * width * cols, 6 * count * width + 2 * width * cols),
        name="dgrad_first",
    )(grad, weight, rows, mean, inv, gain)


def dgrad_half(half, grad, weight, rows, mean, inv, gain, before, block=256, chunk=256):
    count, width = rows.shape
    cols = grad.shape[1]
    steps = count // block // 2
    wide = pl.BlockSpec((block, width), lambda i, h: (h[0] * steps + i, 0))
    thin = pl.BlockSpec((block, 1), lambda i, h: (h[0] * steps + i, 0))
    vector = pl.BlockSpec((1, width), lambda i, h: (0, 0))
    return pl.pallas_call(
        partial(dgrad_half_kernel, chunk=chunk),
        grid_spec=pltpu.PrefetchScalarGridSpec(
            num_scalar_prefetch=1,
            grid=(steps,),
            in_specs=[
                pl.BlockSpec((block, cols), lambda i, h: (h[0] * steps + i, 0)),
                pl.BlockSpec((width, cols), lambda i, h: (0, 0)),
                wide,
                thin,
                thin,
                vector,
                wide,
            ],
            out_specs=[pl.BlockSpec((block, width), lambda i, h: (i, 0)), vector, vector],
        ),
        out_shape=[
            jax.ShapeDtypeStruct((count // 2, width), BF16),
            jax.ShapeDtypeStruct((1, width), F32),
            jax.ShapeDtypeStruct((1, width), F32),
        ],
        compiler_params=params(),
        cost_estimate=cost(count * width * cols, 3 * count * width + 2 * width * cols),
        name="dgrad_half",
    )(half.reshape(1), grad, weight, rows, mean, inv, gain, before)


def branch_kernel(half_ref, heads_ref, out_ref_w, act_ref, down_ref, out_ref, *, chunk):
    heads, act = heads_ref[...], act_ref[...]
    for at in range(0, down_ref.shape[0], chunk):
        span = slice(at, at + chunk)
        out_ref[:, span] = (nt(heads, out_ref_w[span]) + nt(act, down_ref[span])).astype(BF16)


def branch_half(half, heads, pack, act, down, block=256, chunk=256):
    count = heads.shape[0]
    width, units = down.shape
    head_rows = heads.shape[1]
    last = pack.shape[1] // head_rows - 1
    steps = count // block // 2
    return pl.pallas_call(
        partial(branch_kernel, chunk=chunk),
        grid_spec=pltpu.PrefetchScalarGridSpec(
            num_scalar_prefetch=1,
            grid=(steps,),
            in_specs=[
                pl.BlockSpec((block, head_rows), lambda i, h: (h[0] * steps + i, 0)),
                pl.BlockSpec((width, head_rows), lambda i, h: (0, last)),
                pl.BlockSpec((block, units), lambda i, h: (h[0] * steps + i, 0)),
                pl.BlockSpec((width, units), lambda i, h: (0, 0)),
            ],
            out_specs=pl.BlockSpec((block, width), lambda i, h: (i, 0)),
        ),
        out_shape=jax.ShapeDtypeStruct((count // 2, width), BF16),
        compiler_params=params(),
        cost_estimate=cost(count * width * (units + head_rows), count * width + 2 * width * units + count * units),
        name="branch_half",
    )(half.reshape(1), heads, pack, act, down)


CORE = [(0, 1), (1, 0), (2, 3), (3, 2)]
YAX = [(0, 2), (2, 0), (1, 3), (3, 1)]
XAX = [(0, 1), (1, 0)]


def core_swap(block):
    return lax.ppermute(block, "tensor", CORE)


def y_swap(block):
    return lax.ppermute(block, "tensor", YAX)


def x_swap(block):
    return lax.ppermute(block, "branch", XAX)


def pick(array, index, size, axis=0):
    return lax.dynamic_slice_in_dim(array, index * size, size, axis)


def add16(first, second):
    return (first.astype(F32) + second.astype(F32)).astype(BF16)


def own_rows(array, core, why, ex):
    rows = array.shape[0]
    sixteenth = rows // 16
    first = core * 8 + why * 2 + ex
    second = core * 8 + 4 + ex * 2 + why
    return pick(array, first, sixteenth), pick(array, second, sixteenth)


def join(low_index, mine, other, axis=0):
    return jnp.where(
        low_index == 0,
        jnp.concatenate([mine, other], axis),
        jnp.concatenate([other, mine], axis),
    )


def plane_gather(first, second, core, why, ex):
    first_next, second_next = x_swap(first), y_swap(second)
    first, second = join(ex, first, first_next), join(why, second, second_next)
    first_next, second_next = y_swap(first), x_swap(second)
    first, second = join(why, first, first_next), join(ex, second, second_next)
    mine = jnp.concatenate([first, second], 0)
    return join(core, mine, core_swap(mine))


def after(value, *first):
    return lax.optimization_barrier((value,) + first)[0]


def reduce_sends(piece, place, count, step, got):
    right = piece(jnp.minimum(count - 1 - step + place, count - 1))
    left = piece(jnp.maximum(place - (count - 1 - step), 0))
    if got is None:
        return right, left
    return add16(right, got[0]), add16(left, got[1])


def reduce_hop(sends, count, step):
    return (
        lax.ppermute(sends[0], "dp", [(k, k + 1) for k in range(step + 1)]),
        lax.ppermute(sends[1], "dp", [(count - 1 - k, count - 2 - k) for k in range(step + 1)]),
    )


def reduced(piece, place, got):
    right, left = got
    return piece(place).astype(F32) + right.astype(F32) + left.astype(F32)


def halving_send(keep, got, why, ex):
    quarter = keep.shape[0] // 2
    eighth = quarter // 2
    first = add16(
        pick(keep[:quarter], 1 - why, eighth), pick(got[:quarter], 1 - why, eighth)
    )
    second = add16(pick(keep[quarter:], 1 - ex, eighth), pick(got[quarter:], 1 - ex, eighth))
    return first, second


def halving_rest(keep, got, two, why, ex):
    quarter = keep.shape[0] // 2
    eighth, sixteenth = quarter // 2, quarter // 4

    def mine(start, index, received):
        rows = slice(start, start + quarter)
        return (
            pick(keep[rows], index, eighth).astype(F32)
            + pick(got[rows], index, eighth).astype(F32)
            + received.astype(F32)
        )

    first, second = mine(0, why, two[0]), mine(quarter, ex, two[1])
    first_got = x_swap(pick(first, 1 - ex, sixteenth).astype(BF16))
    second_got = y_swap(pick(second, 1 - why, sixteenth).astype(BF16))
    return (
        pick(first, ex, sixteenth) + first_got.astype(F32),
        pick(second, why, sixteenth) + second_got.astype(F32),
    )


def weight_grad(rows, cols):
    return jnp.einsum("rd,rc->dc", rows, cols, preferred_element_type=F32).astype(BF16)


def local(
    tokens,
    lengths,
    valid_mask,
    ln1_gain,
    ln1_bias,
    qkv_weight,
    qkv_bias,
    out_weight,
    out_bias,
    ln2_gain,
    ln2_bias,
    up_weight,
    up_bias,
    down_weight,
    down_bias,
    out_grad,
    *,
    count,
):
    row_count, width = tokens.shape
    ex = lax.axis_index("branch")
    tensor_at = lax.axis_index("tensor")
    why, core = tensor_at // 2, tensor_at % 2
    place = lax.axis_index("dp")
    qkv_cols = qkv_bias.shape[0] // 2
    head_rows = out_weight.shape[0] // 2
    units = up_bias.shape[0] // 2
    chunk = width // (2 * count)

    heads_shard = jnp.concatenate(
        [pick(qkv_weight, ex, qkv_cols, 1), pick(out_weight, ex, head_rows, 0).T], axis=1
    )
    up_shard = pick(up_weight, ex, units, 1)
    down_shard = pick(down_weight, ex, units, 0).T
    heads_full = lax.all_gather(heads_shard, "dp", axis=0, tiled=True)
    up_full = lax.all_gather(up_shard, "dp", axis=0, tiled=True)
    down_full = lax.all_gather(down_shard, "dp", axis=0, tiled=True)

    positions = jnp.arange(row_count, dtype=jnp.int32)
    seq_valid = (valid_mask == 1) & (positions < lengths[0])
    validity = seq_valid.astype(F32)
    key_bias = jnp.broadcast_to(
        jnp.where(seq_valid, 0.0, masked_score)[:, None], (row_count, LANES)
    )
    rows_f32 = tokens.astype(F32)
    mean = jnp.mean(rows_f32, axis=-1, keepdims=True)
    centred = rows_f32 - mean
    inv_std = lax.rsqrt(jnp.mean(centred * centred, axis=-1, keepdims=True) + norm_eps)
    unit_rows = centred * inv_std
    grad_rows = out_grad * validity.astype(BF16)[:, None]
    normed1 = (unit_rows * ln1_gain + ln1_bias).astype(BF16)
    normed2 = (unit_rows * ln2_gain + ln2_bias).astype(BF16)
    cos_table, sin_table = rope_tables(row_count, ROT)
    gap = jnp.zeros((row_count, ROT // 2), F32)
    rest = jnp.zeros((row_count, LANES - ROT), F32)
    tables = (
        jnp.concatenate([cos_table, cos_table, rest + 1.0], axis=1),
        jnp.concatenate([-sin_table, gap, rest], axis=1),
        jnp.concatenate([gap, sin_table, rest], axis=1),
    )

    qkv = project(normed1, heads_full, pick(qkv_bias, ex, qkv_cols)[None], tables)
    attended, log_total = attend(qkv, key_bias)
    attended_grad = jnp.dot(
        grad_rows, heads_full[:, qkv_cols:], preferred_element_type=F32
    ).astype(BF16)
    out_partial = weight_grad(grad_rows, attended)
    attended_grad = after(attended_grad, out_partial)
    qkv_grad, qkv_bias_part = attend_back(
        qkv, attended_grad, log_total, key_bias, cos_table.T, sin_table.T
    )
    qkv_partial = weight_grad(normed1, qkv_grad)

    def split(partial_sum, at):
        return pick(partial_sum.reshape(2, count, chunk, -1), at, 1, 1)[:, 0]

    def heads_piece(at):
        return jnp.concatenate([split(qkv_partial, at), split(out_partial, at)], axis=-1)

    def run_hops(piece, got, first, last):
        for step in range(first, last):
            got = reduce_hop(reduce_sends(piece, place, count, step, got), count, step)
        return got

    hops_a, hops_b = (count - 1) // 3, 2 * (count - 1) // 3
    got = run_hops(heads_piece, None, 0, hops_a - 1)
    sends = reduce_sends(heads_piece, place, count, hops_a - 1, got)
    got = reduce_hop(sends, count, hops_a - 1)
    input_part, dot1, sum1 = dgrad_first(
        after(qkv_grad, *sends), heads_full, tokens, mean, inv_std, ln1_gain[None]
    )
    got = after(got, input_part)
    got = run_hops(heads_piece, got, hops_a, hops_b - 1)
    sends = reduce_sends(heads_piece, place, count, hops_b - 1, got)
    got = reduce_hop(sends, count, hops_b - 1)
    activated, slope = up_gelu(
        after(normed2, input_part, *sends), up_full, pick(up_bias, ex, units)[None]
    )
    got = after(got, activated)
    got = run_hops(heads_piece, got, hops_b, count - 2)
    sends = reduce_sends(heads_piece, place, count, count - 2, got)
    got = reduce_hop(sends, count, count - 2)
    down_partial = weight_grad(after(grad_rows, activated, *sends), activated)

    def scatter(partial_sum):
        return lax.psum_scatter(
            partial_sum.reshape(2, width // 2, -1), "dp", scatter_dimension=1, tiled=True
        )

    down_total = scatter(down_partial)
    got = after(got, down_partial)
    heads_total = reduced(heads_piece, place, got)

    branch_send = branch_half(
        1 - core, attended, heads_full, after(activated, down_partial, heads_total), down_full
    )
    branch_core = core_swap(branch_send)
    branch_keep = branch_half(core, attended, heads_full, after(activated, branch_send), down_full)
    branch_core = after(branch_core, branch_keep)
    branch_two = halving_send(branch_keep, branch_core, why, ex)
    branch_two_got = y_swap(branch_two[0]), x_swap(branch_two[1])
    hidden_grad, up_bias_part = hidden_back(
        after(grad_rows, branch_keep, *branch_two), down_full, slope
    )
    norm_rows = tokens, mean, inv_std, ln2_gain[None], input_part
    input_send, dot2, sum2 = dgrad_half(1 - core, hidden_grad, up_full, *norm_rows)
    input_core = core_swap(input_send)
    input_keep, dot3, sum3 = dgrad_half(core, after(hidden_grad, input_send), up_full, *norm_rows)
    dot2, sum2 = dot2 + dot3, sum2 + sum3
    input_core = after(input_core, input_keep)
    input_two = halving_send(input_keep, input_core, why, ex)
    input_two_got = y_swap(input_two[0]), x_swap(input_two[1])
    branch_two_got = after(branch_two_got, input_keep)
    up_partial = weight_grad(after(normed2, input_keep, *input_two), hidden_grad)
    up_total = scatter(up_partial)
    branch_first, branch_second = halving_rest(branch_keep, branch_core, branch_two_got, why, ex)
    input_first, input_second = halving_rest(input_keep, input_core, input_two_got, why, ex)

    shift_sum = out_bias + down_bias
    tokens_own = own_rows(tokens, core, why, ex)
    validity_own = own_rows(validity, core, why, ex)
    out_grad_own = own_rows(out_grad, core, why, ex)
    mean_own = own_rows(mean, core, why, ex)
    inv_own = own_rows(inv_std, core, why, ex)

    def output_of(at, total):
        return (
            tokens_own[at].astype(F32) + validity_own[at][:, None] * (total + shift_sum)
        ).astype(BF16)

    output_rows = plane_gather(
        output_of(0, branch_first), output_of(1, branch_second), core, why, ex
    )

    def input_of(at, total):
        unit = (tokens_own[at].astype(F32) - mean_own[at]) * inv_own[at]
        back = inv_own[at] * (
            total
            - jnp.mean(total, axis=-1, keepdims=True)
            - unit * jnp.mean(total * unit, axis=-1, keepdims=True)
        )
        return (out_grad_own[at].astype(F32) + back).astype(BF16)

    grad_input = plane_gather(
        input_of(0, input_first), input_of(1, input_second), core, why, ex
    )

    vectors = jnp.concatenate(
        [
            dot1[0],
            sum1[0],
            dot2[0],
            sum2[0],
            jnp.sum(grad_rows, axis=0, dtype=F32),
            qkv_bias_part[0],
            up_bias_part[0],
        ]
    ).reshape(-1, LANES)
    hops = [
        lax.ppermute(vectors, "dp", [(k, (k + hop) % count) for k in range(count)])
        for hop in range(1, count)
    ]
    vectors = sum(hops, vectors)
    norm_rows, bias_rows = 4 * width // LANES, width // LANES
    norms, bias_grad, biases = (
        vectors[:norm_rows],
        vectors[norm_rows : norm_rows + bias_rows].reshape(width),
        vectors[norm_rows + bias_rows :],
    )
    for swap in (core_swap, y_swap, x_swap):
        norms = norms + swap(norms)
    norms = norms.reshape(4, width)
    other = x_swap(biases).reshape(-1)
    biases = biases.reshape(-1)
    qkv_bias_grad = join(ex, biases[:qkv_cols], other[:qkv_cols])
    up_bias_grad = join(ex, biases[qkv_cols:], other[qkv_cols:])

    def share(total):
        mine = lax.dynamic_index_in_dim(total, ex, 0, keepdims=False)
        given = lax.dynamic_index_in_dim(total, 1 - ex, 0, keepdims=False)
        return mine.astype(F32), x_swap(given.astype(BF16)).astype(F32)

    mine, other = share(heads_total)
    qkv_out = join(ex, mine[:, :qkv_cols], other[:, :qkv_cols], 1)
    out_out = join(ex, mine[:, qkv_cols:].T, other[:, qkv_cols:].T, 0)
    mine, other = share(down_total)
    down_out = join(ex, mine.T, other.T, 0)
    mine, other = share(up_total)
    up_out = join(ex, mine, other, 1)

    return (
        output_rows,
        grad_input,
        norms[0],
        norms[1],
        qkv_out,
        qkv_bias_grad,
        out_out,
        bias_grad,
        norms[2],
        norms[3],
        up_out,
        up_bias_grad,
        down_out,
        bias_grad,
    )


def solution(mesh):
    return jax.shard_map(
        partial(local, count=mesh.shape["dp"]),
        mesh=mesh,
        in_specs=(
            P("dp", None),
            P("dp"),
            P("dp"),
            P(),
            P(),
            P("dp", "tensor"),
            P("tensor"),
            P("tensor", "dp"),
            P(),
            P(),
            P(),
            P("dp", "tensor"),
            P("tensor"),
            P("tensor", "dp"),
            P(),
            P("dp", None),
        ),
        out_specs=(
            P("dp", None),
            P("dp", None),
            P(),
            P(),
            P(("branch", "dp"), "tensor"),
            P("tensor"),
            P("tensor", ("branch", "dp")),
            P(),
            P(),
            P(),
            P(("branch", "dp"), "tensor"),
            P("tensor"),
            P("tensor", ("branch", "dp")),
            P(),
        ),
        check_vma=False,
    )
```

time: 818 us -> 630 us (0.77)
  matrix products: 182 us -> 47.6 us
  Pallas kernels: 0 us -> 131 us
  starting transfers between devices: 149 us -> 63.2 us
  waiting for transfers between devices: 252 us -> 193 us
  local copies, waits for them, and re-layouts: 113 us -> 59.3 us
  between operations: 3.78 us -> 15.7 us
  other arithmetic: 105 us -> 114 us
    dot_general x36 -> x5, matrix products: 182 us -> 47.6 us  [the longest x4 40.6 us: weight_grad(): jnp.einsum('rd,rc->dc', rows, cols, preferred_element_type=F32).astype(BF16)]
    pallas_call x0 -> x10, Pallas kernels: none -> 131 us  [the longest x2 24.6 us: dgrad_half(): pl.pallas_call(partial(dgrad_half_kernel, chunk=chunk), grid_spec=pltpu.P...]
    ppermute x48 -> x6, waiting for transfers between devices: 153 us -> 41 us  [the longest x3 35.8 us: reduce_hop(): lax.ppermute(sends[0], 'dp', [(k, k + 1) for k in range(step + 1)])]
    ppermute x48 -> x6, starting transfers between devices: 112 us -> 31.2 us  [the longest x3 26.5 us: reduce_hop(): lax.ppermute(sends[0], 'dp', [(k, k + 1) for k in range(step + 1)])]
    all_gather x0 -> x3, waiting for transfers between devices: none -> 38 us  [the longest x1 37.9 us: local(): heads_full = lax.all_gather(heads_shard, 'dp', axis=0, tiled=True)]
    dynamic_update_slice x28 -> x0, local copies, waits for them, and re-layouts: 36.2 us -> none  [the longest x12 18.4 us: chain_gather(): lax.dynamic_update_slice_in_dim(buffer, right[None], place - 1 - step + c...]
    ppermute x9, waiting for transfers between devices: 26.1 us -> 56 us  [y_swap(): return lax.ppermute(block, 'tensor', YAX)]
    ppermute x14 -> x13, waiting for transfers between devices: 71.7 us -> 57.9 us  [x_swap(): return lax.ppermute(block, 'branch', XAX)]
  transfers between devices with their start and end apart: 79 -> 41, of which waited for: 32 -> 20; matrix products, arithmetic and copies ran while one was open for 48% -> 33% of each run, Pallas kernels for 0% -> 15%
where the time goes in v2:
time: 630 us; the launch traced here: 624 us
  waiting for transfers between devices  193 us (31%)
  Pallas kernels  131 us (21%)
  other arithmetic  114 us (18%)
  starting transfers between devices  63.2 us (10%)
  local copies, waits for them, and re-layouts  59.3 us (9%)
  matrix products  47.6 us (8%)
  between operations  15.7 us (2%)
    ppermute x13, waiting for transfers between devices, x_swap(): return lax.ppermute(block, 'branch', XAX)  57.9 us
    ppermute x9, waiting for transfers between devices, y_swap(): return lax.ppermute(block, 'tensor', YAX)  56 us
    dot_general x4, matrix products, weight_grad(): jnp.einsum('rd,rc->dc', rows, cols, preferred_element_type=F32).astype(BF16)  40.6 us
    all_gather x1, waiting for transfers between devices, local(): heads_full = lax.all_gather(heads_shard, 'dp', axis=0, tiled=True)  37.9 us
    ppermute x3, waiting for transfers between devices, reduce_hop(): lax.ppermute(sends[0], 'dp', [(k, k + 1) for k in range(step + 1)])  35.8 us
    select_n x16, other arithmetic, join(): jnp.where(low_index == 0, jnp.concatenate([mine, other], axis), jnp.conca...  34.1 us
    ppermute x3, starting transfers between devices, reduce_hop(): lax.ppermute(sends[0], 'dp', [(k, k + 1) for k in range(step + 1)])  26.5 us
    pallas_call x2, Pallas kernels, dgrad_half(): pl.pallas_call(partial(dgrad_half_kernel, chunk=chunk), grid_spec=pltpu.P...  24.6 us
  transfers between devices with their start and end apart: 41, of which 20 were waited for; matrix products, arithmetic and copies ran while one was open for 33% of the time, Pallas kernels for 15%

profile of v2, /device:TPU:0, one launch (start us, length us, event | category | flops | bytes accessed | tf_op | source)
XLA Modules:
  0.0 623.7 jit_solution(12824102270320812435)
XLA Ops:
  15.5 3.9 fusion.28
  22.3 4.9 convert_reduce_fusion
  27.2 5.7 fusion.8
  32.9 9.4 %convert_reduce_fusion.1 = (f32[2048]{0:T(1024)}, bf16[2048,2048]{1,0:T(8,128)(2,1)}) fusion(bf16[2048,2048]{1,0:T(8,128)(2,1)} %param.31, bf16[2048]{0:T(1024)(128)(2,1)S(1)} %convert_convert_fusion), kind=kLoop, calls=%fused_computation.11 | loop fusion | flops 12580864 | bytes 16789504 | tf_op jit(solution)/shard_map/reduce_sum | solution.py:737
  42.3 11.6 %fusion.7 = (bf16[2048,2048]{1,0:T(8,128)(2,1)}, bf16[2048,2048]{1,0:T(8,128)(2,1)}) fusion(bf16[2048,2048]{1,0:T(8,128)(2,1)} %rows_ref.5, f32[2048]{0:T(1024)S(1)} %copy-done.34, f32[2048]{0:T(1024)S(1)} %copy-done.30, f32[2048]{0:T(1024)S(1)} %add_rsqrt_fusion, f32[2048]{0:T(1024)S(1)} %broadcast_multiply_fusion.1, f32[2048]{0:T(1024)S(1)} %copy-done.35, ...), kind=kLoop, calls=%fused_computation.9 | loop fusion | flops 37748736 | bytes 25214976 | tf_op jit(solution)/shard_map/convert_element_type | solution.py:615
  56.6 37.9 %all-gather.4.cloned.1.call-done.weight_ref.out_ref_w = bf16[2048,1024]{1,0:T(8,128)(2,1)} async-done(((bf16[512,1024]{1,0:T(8,128)(2,1)}), bf16[2048,1024]{1,0:T(8,128)(2,1)}) %all-gather.4.cloned.1.call-update) | async-done | bytes 4194320 | tf_op jit(solution)/shard_map/all_gather | solution.py:598
  94.5 11.8 %project.1.query_ref.key_ref.value_ref = bf16[2048,768]{1,0:T(8,128)(2,1)} custom-call(bf16[2048,2048]{1,0:T(8,128)(2,1)} %get-tuple-element.125.rows_ref, bf16[2048,1024]{1,0:T(8,128)(2,1)} %all-gather.4.cloned.1.call-done.weight_ref.out_ref_w, f32[1,768]{1,0:T(1,128)} %broadcast_in_dim.22.bias_ref, f32[2048,128]{1,0:T(8,128)} %get-tuple-element.171.cos_ref, ...), custom_call_target="tpu_custom_call" | custom-call | flops 6442450 | bytes 14680 | tf_op jit(solution)/shard_map/project/pallas_call | solution.py:77
  107.6 8.8 %attend.1 = (bf16[2048,256]{1,0:T(8,128)(2,1)}, f32[8,2048]{1,0:T(8,128)}) custom-call(bf16[2048,768]{1,0:T(8,128)(2,1)} %project.1.query_ref.key_ref.value_ref, bf16[2048,768]{1,0:T(8,128)(2,1)} %project.1.query_ref.key_ref.value_ref, bf16[2048,768]{1,0:T(8,128)(2,1)} %project.1.query_ref.key_ref.value_ref, f32[2048,128]{1,0:T(8,128)} %broadcast_in_dim.27.bias_ref), custom_call_target="tpu_custom_call" | custom-call | flops 2684354 | bytes 4194 | tf_op jit(solution)/shard_map/attend/pallas_call | solution.py:140
  116.4 6.1 convolution_convert_fusion.3
  122.5 7.0 %convolution_convert_fusion.4.grad_ref = bf16[2048,256]{1,0:T(8,128)(2,1)} fusion(bf16[2048,2048]{1,0:T(8,128)(2,1)} %get-tuple-element.68.grad_ref, bf16[2048,1024]{1,0:T(8,128)(2,1)} %all-gather.4.cloned.1.call-done.weight_ref.out_ref_w), kind=kOutput, calls=%fused_computation.21 | convolution fusion | flops 2148007936 | bytes 10485760 | tf_op jit(solution)/shard_map/dot_general | solution.py:627
  129.5 15.1 %attend_back.1 = (bf16[2048,768]{1,0:T(8,128)(2,1)}, f32[1,768]{1,0:T(1,128)}) custom-call(bf16[2048,768]{1,0:T(8,128)(2,1)} %project.1.query_ref.key_ref.value_ref, bf16[2048,768]{1,0:T(8,128)(2,1)} %project.1.query_ref.key_ref.value_ref, bf16[2048,768]{1,0:T(8,128)(2,1)} %project.1.query_ref.key_ref.value_ref, ...), custom_call_target="tpu_custom_call" | custom-call | flops 6710886 | bytes 8388 | tf_op jit(solution)/shard_map/attend_back/pallas_call | solution.py:213
  144.6 10.4 %convolution_convert_fusion.2 = bf16[2048,768]{1,0:T(8,128)(2,1)S(1)} fusion(bf16[2048,2048]{1,0:T(8,128)(2,1)} %get-tuple-element.125.rows_ref, bf16[2048,768]{1,0:T(8,128)(2,1)} %get-tuple-element.54.grad_ref), kind=kOutput, calls=%fused_computation.19 | convolution fusion | flops 6444023808 | bytes 14680064 | tf_op jit(solution)/shard_map/rd,rc->dc/dot_general | solution.py:560
  178.3 17.4 %dgrad_first.1 = (f32[2048,2048]{1,0:T(8,128)}, f32[1,2048]{1,0:T(1,128)}, f32[1,2048]{1,0:T(1,128)}) custom-call(bf16[2048,768]{1,0:T(8,128)(2,1)} %get-tuple-element.54.grad_ref, bf16[2048,1024]{1,0:T(8,128)(2,1)} %all-gather.4.cloned.1.call-done.weight_ref.out_ref_w, bf16[2048,2048]{1,0:T(8,128)(2,1)} %rows_ref.5, f32[2048,1]{1,0:T(8,128)} %copy.53.mean_ref, ...), custom_call_target="tpu_custom_call" | custom-call | flops 6442450 | bytes 28311 | tf_op jit(solution)/shard_map/dgrad_first/pallas_call | solution.py:364
  195.7 4.4 collective-permute-done
  206.8 5.1 collective-permute-start.2
  215.7 17.5 %up_gelu.1 = (bf16[2048,1024]{1,0:T(8,128)(2,1)}, f32[2048,1024]{1,0:T(8,128)}) custom-call(bf16[2048,2048]{1,0:T(8,128)(2,1)} %get-tuple-element.85.rows_ref, bf16[2048,1024]{1,0:T(8,128)(2,1)} %all-gather.6.cloned.1.call-done.weight_ref, f32[1,1024]{1,0:T(1,128)} %bitcast.117), custom_call_target="tpu_custom_call" | custom-call | flops 8589934 | bytes 25165 | tf_op jit(solution)/shard_map/up_gelu/pallas_call | solution.py:260
  233.2 23.2 %collective-permute-done.2 = bf16[2,256,1024]{1,2,0:T(8,128)(2,1)} collective-permute-done((bf16[2,256,1024]{1,2,0:T(8,128)(2,1)}, bf16[2,256,1024]{1,2,0:T(8,128)(2,1)}, u32[]{:S(2)}, u32[]{:S(2)}) %collective-permute-start.2) | collective-permute-done | bytes 1048608 | tf_op jit(solution)/shard_map/ppermute | solution.py:518
  260.8 19.0 %collective-permute-start.4 = (bf16[2,256,1024]{1,2,0:T(8,128)(2,1)S(1)}, bf16[2,256,1024]{1,2,0:T(8,128)(2,1)S(1)}, u32[]{:S(2)}, u32[]{:S(2)}) collective-permute-start(bf16[2,256,1024]{1,2,0:T(8,128)(2,1)S(1)} %add_convert_fusion.5), channel_id=1, source_target_pairs={{0,1},{1,2},{2,3},{4,5},{5,6},{6,7},{8,9},{9,10},{10,11},{12,13},{... | collective-permute-start | bytes 3145736 | tf_op jit(solution)/shard_map/ppermute | solution.py:518
  279.8 13.1 %convolution_convert_fusion.1 = bf16[2048,1024]{1,0:T(8,128)(2,1)} fusion(bf16[2048,2048]{1,0:T(8,128)(2,1)} %get-tuple-element.68.grad_ref, bf16[2048,1024]{1,0:T(8,128)(2,1)S(1)} %copy-done.7), kind=kOutput, calls=%fused_computation.18 | convolution fusion | flops 8592031744 | bytes 16777216 | tf_op jit(solution)/shard_map/rd,rc->dc/dot_general | solution.py:560
  292.9 5.2 collective-permute-done.5
  298.1 8.2 %collective-permute-done.4 = bf16[2,256,1024]{1,2,0:T(8,128)(2,1)S(1)} collective-permute-done((bf16[2,256,1024]{1,2,0:T(8,128)(2,1)S(1)}, bf16[2,256,1024]{1,2,0:T(8,128)(2,1)S(1)}, u32[]{:S(2)}, u32[]{:S(2)}) %collective-permute-start.4) | collective-permute-done | bytes 1048608 | tf_op jit(solution)/shard_map/ppermute | solution.py:518
  308.0 10.1 %branch_half.2 = bf16[1024,2048]{1,0:T(8,128)(2,1)} custom-call(s32[1]{0:T(128)} %bitcast.17.half_ref, bf16[2048,256]{1,0:T(8,128)(2,1)} %get-tuple-element.50.heads_ref, bf16[2048,1024]{1,0:T(8,128)(2,1)} %all-gather.4.cloned.1.call-done.weight_ref.out_ref_w, bf16[2048,1024]{1,0:T(8,128)(2,1)} %get-tuple-element.66.act_ref, ...), custom_call_target="tpu_custom_call" | custom-call | flops 5368709 | bytes 10485 | tf_op jit(solution)/shard_map/branch_half/pallas_call | solution.py:434
  318.0 10.1 %branch_half.3 = bf16[1024,2048]{1,0:T(8,128)(2,1)} custom-call(s32[1]{0:T(128)} %bitcast.1.half_ref, bf16[2048,256]{1,0:T(8,128)(2,1)} %get-tuple-element.50.heads_ref, bf16[2048,1024]{1,0:T(8,128)(2,1)} %all-gather.4.cloned.1.call-done.weight_ref.out_ref_w, bf16[2048,1024]{1,0:T(8,128)(2,1)} %get-tuple-element.66.act_ref, ...), custom_call_target="tpu_custom_call" | custom-call | flops 5368709 | bytes 10485 | tf_op jit(solution)/shard_map/branch_half/pallas_call | solution.py:434
  330.9 3.5 fusion.42
  337.6 15.5 %hidden_back.1 = (bf16[2048,1024]{1,0:T(8,128)(2,1)}, f32[1,1024]{1,0:T(1,128)}) custom-call(bf16[2048,2048]{1,0:T(8,128)(2,1)} %get-tuple-element.68.grad_ref, bf16[2048,1024]{1,0:T(8,128)(2,1)} %all-gather.8.cloned.1.call-done.down_ref.weight_ref, f32[2048,1024]{1,0:T(8,128)} %get-tuple-element.69.slope_ref), custom_call_target="tpu_custom_call" | custom-call | flops 8589934 | bytes 25165 | tf_op jit(solution)/shard_map/hidden_back/pallas_call | solution.py:297
  353.2 12.3 %dgrad_half.2 = (bf16[1024,2048]{1,0:T(8,128)(2,1)}, f32[1,2048]{1,0:T(1,128)}, f32[1,2048]{1,0:T(1,128)}) custom-call(s32[1]{0:T(128)} %bitcast.17.half_ref, bf16[2048,1024]{1,0:T(8,128)(2,1)} %get-tuple-element.72.grad_ref, bf16[2048,1024]{1,0:T(8,128)(2,1)} %all-gather.6.cloned.1.call-done.weight_ref, bf16[2048,2048]{1,0:T(8,128)(2,1)} %rows_ref.5, ...), custom_call_target="tpu_custom_call" | custom-call | flops 4294967 | bytes 16777 | tf_op jit(solution)/shard_map/dgrad_half/pallas_call | solution.py:394
  372.0 6.6 %copy.70 = bf16[2,1024,1024]{1,2,0:T(8,128)(2,1)} copy(bf16[2,1024,1024]{2,1,0:T(8,128)(2,1)} %bitcast.89) | data formatting | bytes 8388608 | tf_op jit(solution)/shard_map/reshape | solution.py:670
  380.0 22.7 %collective-permute-done.32 = bf16[256,1024]{0,1:T(8,128)(2,1)} collective-permute-done((bf16[256,1024]{0,1:T(8,128)(2,1)}, bf16[256,1024]{0,1:T(8,128)(2,1)}, u32[]{:S(2)}, u32[]{:S(2)}) %collective-permute-start.32) | collective-permute-done | bytes 524320 | tf_op jit(solution)/shard_map/ppermute | solution.py:468
  404.7 12.3 %dgrad_half.3 = (bf16[1024,2048]{1,0:T(8,128)(2,1)}, f32[1,2048]{1,0:T(1,128)}, f32[1,2048]{1,0:T(1,128)}) custom-call(s32[1]{0:T(128)} %bitcast.1.half_ref, bf16[2048,1024]{1,0:T(8,128)(2,1)} %get-tuple-element.72.grad_ref, bf16[2048,1024]{1,0:T(8,128)(2,1)} %all-gather.6.cloned.1.call-done.weight_ref, bf16[2048,2048]{1,0:T(8,128)(2,1)} %rows_ref.5, ...), custom_call_target="tpu_custom_call" | custom-call | flops 4294967 | bytes 16777 | tf_op jit(solution)/shard_map/dgrad_half/pallas_call | solution.py:394
  425.1 7.7 %collective-permute-done.12 = bf16[128,2048]{1,0:T(8,128)(2,1)S(1)} collective-permute-done((bf16[128,2048]{1,0:T(8,128)(2,1)S(1)}, bf16[128,2048]{1,0:T(8,128)(2,1)S(1)}, u32[]{:S(2)}, u32[]{:S(2)}) %collective-permute-start.12) | collective-permute-done | bytes 524320 | tf_op jit(solution)/shard_map/ppermute | solution.py:464
  432.8 3.3 collective-permute-done.9
  449.2 3.6 collective-permute-done.10
  454.6 6.2 collective-permute-done.13
  462.3 13.0 %collective-permute-done.21 = bf16[256,2048]{1,0:T(8,128)(2,1)S(1)} collective-permute-done((bf16[256,2048]{1,0:T(8,128)(2,1)S(1)}, bf16[256,2048]{1,0:T(8,128)(2,1)S(1)}, u32[]{:S(2)}, u32[]{:S(2)}) %collective-permute-start.21) | collective-permute-done | bytes 1048608 | tf_op jit(solution)/shard_map/ppermute | solution.py:468
  477.2 6.0 collective-permute-done.17
  487.1 11.1 %convolution_convert_fusion = bf16[2048,1024]{1,0:T(8,128)(2,1)} fusion(bf16[2048,2048]{1,0:T(8,128)(2,1)S(1)} %bitcast.86, bf16[2048,1024]{1,0:T(8,128)(2,1)S(1)} %copy-done.8), kind=kOutput, calls=%fused_computation.17 | convolution fusion | flops 8592031744 | bytes 16777216 | tf_op jit(solution)/shard_map/rd,rc->dc/dot_general | solution.py:560
  498.2 15.8 %collective-permute-done.22 = bf16[128,2048]{1,0:T(8,128)(2,1)} collective-permute-done((bf16[128,2048]{1,0:T(8,128)(2,1)}, bf16[128,2048]{1,0:T(8,128)(2,1)}, u32[]{:S(2)}, u32[]{:S(2)}) %collective-permute-start.22) | collective-permute-done | bytes 524320 | tf_op jit(solution)/shard_map/ppermute | solution.py:464
  516.8 2.8 fusion.17
  520.6 3.3 maximum_select_fusion.2
  526.8 3.8 collective-permute-done.19
  531.1 7.7 %collective-permute-done.23 = bf16[128,2048]{1,0:T(8,128)(2,1)S(1)} collective-permute-done((bf16[128,2048]{1,0:T(8,128)(2,1)S(1)}, bf16[128,2048]{1,0:T(8,128)(2,1)S(1)}, u32[]{:S(2)}, u32[]{:S(2)}) %collective-permute-start.23) | collective-permute-done | bytes 524320 | tf_op jit(solution)/shard_map/ppermute | solution.py:464
  547.3 9.5 %collective-permute-done.20 = bf16[256,2048]{1,0:T(8,128)(2,1)S(1)} collective-permute-done((bf16[256,2048]{1,0:T(8,128)(2,1)S(1)}, bf16[256,2048]{1,0:T(8,128)(2,1)S(1)}, u32[]{:S(2)}, u32[]{:S(2)}) %collective-permute-start.20) | collective-permute-done | bytes 1048608 | tf_op jit(solution)/shard_map/ppermute | solution.py:464
  556.8 3.5 collective-permute-start.28
  566.1 3.0 copy.71
  576.7 3.1 collective-permute-done.30
  580.9 7.7 %collective-permute-done.31 = f32[64,128]{1,0:T(8,128)S(1)} collective-permute-done((f32[64,128]{1,0:T(8,128)S(1)}, f32[64,128]{1,0:T(8,128)S(1)}, u32[]{:S(2)}, u32[]{:S(2)}) %collective-permute-start.31) | collective-permute-done | bytes 32800 | tf_op jit(solution)/shard_map/ppermute | solution.py:468
  591.6 8.6 %maximum_select_fusion = bf16[2048,2048]{1,0:T(8,128)(2,1)} fusion(bf16[1024,2048]{1,0:T(8,128)(2,1)} %collective-permute-done.15, bf16[512,2048]{1,0:T(8,128)(2,1)S(1)} %copy-done.3, bf16[512,2048]{1,0:T(8,128)(2,1)S(1)} %maximum_select_fusion.2, pred[]{:T(512)S(6)} %eq.12), kind=kLoop, calls=%fused_computation.12 | loop fusion | flops 54525952 | bytes 16777216 | tf_op jit(solution)/shard_map/jit(_where)/select_n | solution.py:488
  603.3 9.2 %maximum_select_fusion.1 = bf16[2048,2048]{1,0:T(8,128)(2,1)} fusion(bf16[1024,2048]{1,0:T(8,128)(2,1)} %collective-permute-done.25, bf16[512,2048]{1,0:T(8,128)(2,1)} %copy-done.6, bf16[512,2048]{1,0:T(8,128)(2,1)S(1)} %copy-done.5, pred[]{:T(512)S(6)} %eq.12), kind=kLoop, calls=%fused_computation.13 | loop fusion | flops 54525952 | bytes 16777216 | tf_op jit(solution)/shard_map/jit(_where)/select_n | solution.py:488
  (292 shorter events, 140.6 us)
Async XLA Ops:
  7.2 87.3 %all-gather.4.cloned.1.call-start = ((), (), s32[]{:S(2)}) async-start(), calls=%async_computation.2 | async-start | bytes 5242880 | tf_op jit(solution)/shard_map/all_gather | solution.py:598
  10.8 204.9 %all-gather.6.cloned.1.call-start = ((), (), s32[]{:S(2)}) async-start(), calls=%async_computation.3 | async-start | bytes 5242880 | tf_op jit(solution)/shard_map/all_gather | solution.py:599
  12.0 296.0 %all-gather.8.cloned.1.call-start = ((), (), s32[]{:S(2)}) async-start(), calls=%async_computation.4 | async-start | bytes 5242880 | tf_op jit(solution)/shard_map/all_gather | solution.py:600
  14.7 558.1 %reduce-scatter.5.cloned.1.call-start = ((), (), s32[]{:S(2)}) async-start(), calls=%async_computation.6 | async-start | bytes 5242880 | tf_op jit(solution)/shard_map/reduce_scatter | solution.py:669
  166.7 29.0 %collective-permute-start.1 = (bf16[2,256,1024]{1,2,0:T(8,128)(2,1)}, bf16[2,256,1024]{1,2,0:T(8,128)(2,1)}, u32[]{:S(2)}, u32[]{:S(2)}) collective-permute-start(bf16[2,256,1024]{1,2,0:T(8,128)(2,1)} %pad_maximum_fusion.4), channel_id=1, source_target_pairs={{3,2},{7,6},{11,10},{15,14},{19,18},{23,22},{27,26},{31,30}} | collective-permute-start | bytes 3145736 | tf_op jit(solution)/shard_map/ppermute | solution.py:519
  169.3 30.8 %collective-permute-start = (bf16[2,256,1024]{1,2,0:T(8,128)(2,1)}, bf16[2,256,1024]{1,2,0:T(8,128)(2,1)}, u32[]{:S(2)}, u32[]{:S(2)}) collective-permute-start(bf16[2,256,1024]{1,2,0:T(8,128)(2,1)} %pad_maximum_fusion.3), channel_id=1, source_target_pairs={{0,1},{4,5},{8,9},{12,13},{16,17},{20,21},{24,25},{28,29}} | collective-permute-start | bytes 3145736 | tf_op jit(solution)/shard_map/ppermute | solution.py:518
  202.6 30.6 %collective-permute-start.3 = (bf16[2,256,1024]{1,2,0:T(8,128)(2,1)}, bf16[2,256,1024]{1,2,0:T(8,128)(2,1)}, u32[]{:S(2)}, u32[]{:S(2)}) collective-permute-start(bf16[2,256,1024]{1,2,0:T(8,128)(2,1)} %add_convert_fusion.6), channel_id=1, source_target_pairs={{3,2},{2,1},{7,6},{6,5},{11,10},{10,9},{15,14},{14,13},{19,18},{18... | collective-permute-start | bytes 3145736 | tf_op jit(solution)/shard_map/ppermute | solution.py:519
  206.8 49.5 %collective-permute-start.2 = (bf16[2,256,1024]{1,2,0:T(8,128)(2,1)}, bf16[2,256,1024]{1,2,0:T(8,128)(2,1)}, u32[]{:S(2)}, u32[]{:S(2)}) collective-permute-start(bf16[2,256,1024]{1,2,0:T(8,128)(2,1)} %add_convert_fusion.7), channel_id=1, source_target_pairs={{0,1},{1,2},{4,5},{5,6},{8,9},{9,10},{12,13},{13,14},{16,17},{17,1... | collective-permute-start | bytes 3145736 | tf_op jit(solution)/shard_map/ppermute | solution.py:518
  215.7 40.7 %copy-start.20 = (bf16[2,1,256,768]{2,3,0,1:T(8,128)(2,1)S(1)}, bf16[2,1,256,768]{2,3,0,1:T(8,128)(2,1)}, u32[]{:S(2)}) copy-start(bf16[2,1,256,768]{2,3,0,1:T(8,128)(2,1)} %copy.61) | copy-start | bytes 2359300
  233.2 26.1 %copy-start.19 = (bf16[2,1,256,768]{2,3,0,1:T(8,128)(2,1)S(1)}, bf16[2,1,256,768]{2,3,0,1:T(8,128)(2,1)}, u32[]{:S(2)}) copy-start(bf16[2,1,256,768]{2,3,0,1:T(8,128)(2,1)} %copy.59) | copy-start | bytes 2359300
  256.4 23.4 %copy-start.7 = (bf16[2048,1024]{1,0:T(8,128)(2,1)S(1)}, bf16[2048,1024]{1,0:T(8,128)(2,1)}, u32[]{:S(2)}) copy-start(bf16[2048,1024]{1,0:T(8,128)(2,1)} %get-tuple-element.66.act_ref) | copy-start | bytes 12582916
  258.0 40.1 %collective-permute-start.5 = (bf16[2,256,1024]{1,2,0:T(8,128)(2,1)S(1)}, bf16[2,256,1024]{1,2,0:T(8,128)(2,1)S(1)}, u32[]{:S(2)}, u32[]{:S(2)}) collective-permute-start(bf16[2,256,1024]{1,2,0:T(8,128)(2,1)S(1)} %add_convert_fusion.4), channel_id=1, source_target_pairs={{3,2},{2,1},{1,0},{7,6},{6,5},{5,4},{11,10},{10,9},{9,8},{15,14},{... | collective-permute-start | bytes 3145736 | tf_op jit(solution)/shard_map/ppermute | solution.py:519
  260.8 45.5 %collective-permute-start.4 = (bf16[2,256,1024]{1,2,0:T(8,128)(2,1)S(1)}, bf16[2,256,1024]{1,2,0:T(8,128)(2,1)S(1)}, u32[]{:S(2)}, u32[]{:S(2)}) collective-permute-start(bf16[2,256,1024]{1,2,0:T(8,128)(2,1)S(1)} %add_convert_fusion.5), channel_id=1, source_target_pairs={{0,1},{1,2},{2,3},{4,5},{5,6},{6,7},{8,9},{9,10},{10,11},{12,13},{... | collective-permute-start | bytes 3145736 | tf_op jit(solution)/shard_map/ppermute | solution.py:518
  318.0 12.9 %collective-permute-start.6 = (bf16[1024,2048]{1,0:T(8,128)(2,1)}, bf16[1024,2048]{1,0:T(8,128)(2,1)}, u32[]{:S(2)}, u32[]{:S(2)}) collective-permute-start(bf16[1024,2048]{1,0:T(8,128)(2,1)} %branch_half.2), channel_id=1, source_target_pairs={{0,4},{4,0},{8,12},{12,8},{1,5},{5,1},{9,13},{13,9},{2,6},{6,2},{1... | collective-permute-start | bytes 12582920 | tf_op jit(solution)/shard_map/ppermute | solution.py:460
  365.4 74.1 %collective-permute-start.16 = (bf16[1024,2048]{1,0:T(8,128)(2,1)}, bf16[1024,2048]{1,0:T(8,128)(2,1)}, u32[]{:S(2)}, u32[]{:S(2)}) collective-permute-start(bf16[1024,2048]{1,0:T(8,128)(2,1)} %get-tuple-element.71), channel_id=1, source_target_pairs={{0,4},{4,0},{8,12},{12,8},{1,5},{5,1},{9,13},{13,9},{2,6},{6,2},{1... | collective-permute-start | bytes 12582920 | tf_op jit(solution)/shard_map/ppermute | solution.py:460
  366.0 51.0 %collective-permute-start.8 = (bf16[256,2048]{1,0:T(8,128)(2,1)}, bf16[256,2048]{1,0:T(8,128)(2,1)}, u32[]{:S(2)}, u32[]{:S(2)}) collective-permute-start(bf16[256,2048]{1,0:T(8,128)(2,1)} %add_convert_fusion.2), channel_id=1, source_target_pairs={{0,16},{16,0},{1,17},{17,1},{2,18},{18,2},{3,19},{19,3},{4,20},{20... | collective-permute-start | bytes 3145736 | tf_op jit(solution)/shard_map/ppermute | solution.py:468
  367.6 49.4 %collective-permute-start.7 = (bf16[256,2048]{1,0:T(8,128)(2,1)}, bf16[256,2048]{1,0:T(8,128)(2,1)}, u32[]{:S(2)}, u32[]{:S(2)}) collective-permute-start(bf16[256,2048]{1,0:T(8,128)(2,1)} %add_convert_fusion.3), channel_id=1, source_target_pairs={{0,8},{8,0},{4,12},{12,4},{1,9},{9,1},{5,13},{13,5},{2,10},{10,2},... | collective-permute-start | bytes 3145736 | tf_op jit(solution)/shard_map/ppermute | solution.py:464
  371.4 31.3 %collective-permute-start.32 = (bf16[256,1024]{0,1:T(8,128)(2,1)}, bf16[256,1024]{0,1:T(8,128)(2,1)}, u32[]{:S(2)}, u32[]{:S(2)}) collective-permute-start(bf16[256,1024]{0,1:T(8,128)(2,1)} %fusion.30), channel_id=1, source_target_pairs={{0,16},{16,0},{1,17},{17,1},{2,18},{18,2},{3,19},{19,3},{4,20},{20... | collective-permute-start | bytes 1572872 | tf_op jit(solution)/shard_map/ppermute | solution.py:468
  378.6 221.6 %reduce-scatter.3.cloned.1.call-start = ((), (), s32[]{:S(2)}) async-start(), calls=%async_computation.5 | async-start | bytes 5242880 | tf_op jit(solution)/shard_map/reduce_scatter | solution.py:669
  380.0 37.0 %copy-start.15 = (f32[256,1024]{0,1:T(8,128)}, f32[256,1024]{0,1:T(8,128)S(1)}, u32[]{:S(2)}) copy-start(f32[256,1024]{0,1:T(8,128)S(1)} %dynamic-slice_bitcast_fusion) | copy-start | bytes 3145732
  419.7 13.1 %collective-permute-start.12 = (bf16[128,2048]{1,0:T(8,128)(2,1)S(1)}, bf16[128,2048]{1,0:T(8,128)(2,1)S(1)}, u32[]{:S(2)}, u32[]{:S(2)}) collective-permute-start(bf16[128,2048]{1,0:T(8,128)(2,1)S(1)} %dynamic-slice_convert_fusion.3), channel_id=1, source_target_pairs={{0,8},{8,0},{4,12},{12,4},{1,9},{9,1},{5,13},{13,5},{2,10},{10,2},... | collective-permute-start | bytes 1572872 | tf_op jit(solution)/shard_map/ppermute | solution.py:464
  423.3 12.8 %collective-permute-start.9 = (bf16[128,2048]{1,0:T(8,128)(2,1)S(1)}, bf16[128,2048]{1,0:T(8,128)(2,1)S(1)}, u32[]{:S(2)}, u32[]{:S(2)}) collective-permute-start(bf16[128,2048]{1,0:T(8,128)(2,1)S(1)} %dynamic-slice_convert_fusion.4), channel_id=1, source_target_pairs={{0,16},{16,0},{1,17},{17,1},{2,18},{18,2},{3,19},{19,3},{4,20},{20... | collective-permute-start | bytes 1572872 | tf_op jit(solution)/shard_map/ppermute | solution.py:468
  437.9 14.9 %collective-permute-start.10 = (bf16[128,2048]{1,0:T(8,128)(2,1)S(1)}, bf16[128,2048]{1,0:T(8,128)(2,1)S(1)}, u32[]{:S(2)}, u32[]{:S(2)}) collective-permute-start(bf16[128,2048]{1,0:T(8,128)(2,1)S(1)} %get-tuple-element.126), channel_id=1, source_target_pairs={{0,16},{16,0},{1,17},{17,1},{2,18},{18,2},{3,19},{19,3},{4,20},{20... | collective-permute-start | bytes 1572872 | tf_op jit(solution)/shard_map/ppermute | solution.py:468
  442.6 32.7 %collective-permute-start.21 = (bf16[256,2048]{1,0:T(8,128)(2,1)S(1)}, bf16[256,2048]{1,0:T(8,128)(2,1)S(1)}, u32[]{:S(2)}, u32[]{:S(2)}) collective-permute-start(bf16[256,2048]{1,0:T(8,128)(2,1)S(1)} %add_convert_fusion), channel_id=1, source_target_pairs={{0,16},{16,0},{1,17},{17,1},{2,18},{18,2},{3,19},{19,3},{4,20},{20... | collective-permute-start | bytes 3145736 | tf_op jit(solution)/shard_map/ppermute | solution.py:468
  445.9 14.9 %collective-permute-start.13 = (bf16[128,2048]{1,0:T(8,128)(2,1)S(1)}, bf16[128,2048]{1,0:T(8,128)(2,1)S(1)}, u32[]{:S(2)}, u32[]{:S(2)}) collective-permute-start(bf16[128,2048]{1,0:T(8,128)(2,1)S(1)} %get-tuple-element.127), channel_id=1, source_target_pairs={{0,8},{8,0},{4,12},{12,4},{1,9},{9,1},{5,13},{13,5},{2,10},{10,2},... | collective-permute-start | bytes 1572872 | tf_op jit(solution)/shard_map/ppermute | solution.py:464
  447.4 39.7 %slice-start = ((s8[8388608]{0:T(1024)(128)(4,1)}), s8[4194304]{0:T(1024)(128)(4,1)S(1)}, s32[]{:S(2)}) async-start(s8[8388608]{0:T(1024)(128)(4,1)} %bitcast.85), calls=%async_computation.7 | async-start | bytes 8388608
  447.8 35.4 %collective-permute-start.17 = (bf16[256,2048]{1,0:T(8,128)(2,1)S(1)}, bf16[256,2048]{1,0:T(8,128)(2,1)S(1)}, u32[]{:S(2)}, u32[]{:S(2)}) collective-permute-start(bf16[256,2048]{1,0:T(8,128)(2,1)S(1)} %add_convert_fusion.1), channel_id=1, source_target_pairs={{0,8},{8,0},{4,12},{12,4},{1,9},{9,1},{5,13},{13,5},{2,10},{10,2},... | collective-permute-start | bytes 3145736 | tf_op jit(solution)/shard_map/ppermute | solution.py:464
  454.0 66.6 %collective-permute-start.11 = (bf16[256,2048]{1,0:T(8,128)(2,1)}, bf16[256,2048]{1,0:T(8,128)(2,1)}, u32[]{:S(2)}, u32[]{:S(2)}) collective-permute-start(bf16[256,2048]{1,0:T(8,128)(2,1)} %maximum_select_fusion.9), channel_id=1, source_target_pairs={{0,8},{8,0},{4,12},{12,4},{1,9},{9,1},{5,13},{13,5},{2,10},{10,2},... | collective-permute-start | bytes 3145736 | tf_op jit(solution)/shard_map/ppermute | solution.py:464
  461.0 26.1 %slice-start.1 = ((s8[8388608]{0:T(1024)(128)(4,1)}), s8[4194304]{0:T(1024)(128)(4,1)S(1)}, s32[]{:S(2)}) async-start(s8[8388608]{0:T(1024)(128)(4,1)} %bitcast.85), calls=%async_computation.8 | async-start | bytes 8388608
  461.0 63.3 %collective-permute-start.14 = (bf16[256,2048]{1,0:T(8,128)(2,1)S(1)}, bf16[256,2048]{1,0:T(8,128)(2,1)}, u32[]{:S(2)}, u32[]{:S(2)}) collective-permute-start(bf16[256,2048]{1,0:T(8,128)(2,1)S(1)} %maximum_select_fusion.10), channel_id=1, source_target_pairs={{0,16},{16,0},{1,17},{17,1},{2,18},{18,2},{3,19},{19,3},{4,20},{20... | collective-permute-start | bytes 3145736 | tf_op jit(solution)/shard_map/ppermute | solution.py:468
  476.7 37.3 %collective-permute-start.22 = (bf16[128,2048]{1,0:T(8,128)(2,1)}, bf16[128,2048]{1,0:T(8,128)(2,1)}, u32[]{:S(2)}, u32[]{:S(2)}) collective-permute-start(bf16[128,2048]{1,0:T(8,128)(2,1)} %dynamic-slice_convert_fusion.1), channel_id=1, source_target_pairs={{0,8},{8,0},{4,12},{12,4},{1,9},{9,1},{5,13},{13,5},{2,10},{10,2},... | collective-permute-start | bytes 1572872 | tf_op jit(solution)/shard_map/ppermute | solution.py:464
  485.9 28.1 %collective-permute-start.18 = (bf16[128,2048]{1,0:T(8,128)(2,1)}, bf16[128,2048]{1,0:T(8,128)(2,1)}, u32[]{:S(2)}, u32[]{:S(2)}) collective-permute-start(bf16[128,2048]{1,0:T(8,128)(2,1)} %dynamic-slice_convert_fusion.2), channel_id=1, source_target_pairs={{0,16},{16,0},{1,17},{17,1},{2,18},{18,2},{3,19},{19,3},{4,20},{20... | collective-permute-start | bytes 1572872 | tf_op jit(solution)/shard_map/ppermute | solution.py:468
  519.6 11.0 %collective-permute-start.19 = (bf16[128,2048]{1,0:T(8,128)(2,1)S(1)}, bf16[128,2048]{1,0:T(8,128)(2,1)S(1)}, u32[]{:S(2)}, u32[]{:S(2)}) collective-permute-start(bf16[128,2048]{1,0:T(8,128)(2,1)S(1)} %get-tuple-element.122), channel_id=1, source_target_pairs={{0,16},{16,0},{1,17},{17,1},{2,18},{18,2},{3,19},{19,3},{4,20},{20... | collective-permute-start | bytes 1572872 | tf_op jit(solution)/shard_map/ppermute | solution.py:468
  523.9 14.9 %collective-permute-start.23 = (bf16[128,2048]{1,0:T(8,128)(2,1)S(1)}, bf16[128,2048]{1,0:T(8,128)(2,1)S(1)}, u32[]{:S(2)}, u32[]{:S(2)}) collective-permute-start(bf16[128,2048]{1,0:T(8,128)(2,1)S(1)} %get-tuple-element.123), channel_id=1, source_target_pairs={{0,8},{8,0},{4,12},{12,4},{1,9},{9,1},{5,13},{13,5},{2,10},{10,2},... | collective-permute-start | bytes 1572872 | tf_op jit(solution)/shard_map/ppermute | solution.py:464
  530.9 25.9 %collective-permute-start.20 = (bf16[256,2048]{1,0:T(8,128)(2,1)S(1)}, bf16[256,2048]{1,0:T(8,128)(2,1)S(1)}, u32[]{:S(2)}, u32[]{:S(2)}) collective-permute-start(bf16[256,2048]{1,0:T(8,128)(2,1)S(1)} %maximum_select_fusion.11), channel_id=1, source_target_pairs={{0,8},{8,0},{4,12},{12,4},{1,9},{9,1},{5,13},{13,5},{2,10},{10,2},... | collective-permute-start | bytes 3145736 | tf_op jit(solution)/shard_map/ppermute | solution.py:464
  539.1 22.2 %collective-permute-start.24 = (bf16[256,2048]{1,0:T(8,128)(2,1)S(1)}, bf16[256,2048]{1,0:T(8,128)(2,1)S(1)}, u32[]{:S(2)}, u32[]{:S(2)}) collective-permute-start(bf16[256,2048]{1,0:T(8,128)(2,1)S(1)} %maximum_select_fusion.12), channel_id=1, source_target_pairs={{0,16},{16,0},{1,17},{17,1},{2,18},{18,2},{3,19},{19,3},{4,20},{20... | collective-permute-start | bytes 3145736 | tf_op jit(solution)/shard_map/ppermute | solution.py:468
  542.8 48.1 %collective-permute-start.15 = (bf16[1024,2048]{1,0:T(8,128)(2,1)}, bf16[1024,2048]{1,0:T(8,128)(2,1)}, u32[]{:S(2)}, u32[]{:S(2)}) collective-permute-start(bf16[1024,2048]{1,0:T(8,128)(2,1)} %pad_maximum_fusion), channel_id=1, source_target_pairs={{0,4},{4,0},{8,12},{12,8},{1,5},{5,1},{9,13},{13,9},{2,6},{6,2},{1... | collective-permute-start | bytes 12582920 | tf_op jit(solution)/shard_map/ppermute | solution.py:460
  542.9 26.2 %collective-permute-start.26 = (f32[94,128]{1,0:T(8,128)S(1)}, f32[94,128]{1,0:T(8,128)S(1)}, u32[]{:S(2)}, u32[]{:S(2)}) collective-permute-start(f32[94,128]{1,0:T(8,128)S(1)} %bitcast.111), channel_id=1, source_target_pairs={{0,1},{1,2},{2,3},{3,0},{4,5},{5,6},{6,7},{7,4},{8,9},{9,10},{10,1... | collective-permute-start | bytes 144392 | tf_op jit(solution)/shard_map/ppermute | solution.py:743
  545.3 23.8 %collective-permute-start.27 = (f32[94,128]{1,0:T(8,128)S(1)}, f32[94,128]{1,0:T(8,128)S(1)}, u32[]{:S(2)}, u32[]{:S(2)}) collective-permute-start(f32[94,128]{1,0:T(8,128)S(1)} %bitcast.112), channel_id=1, source_target_pairs={{0,2},{1,3},{2,0},{3,1},{4,6},{5,7},{6,4},{7,5},{8,10},{9,11},{10,... | collective-permute-start | bytes 144392 | tf_op jit(solution)/shard_map/ppermute | solution.py:743
  556.8 12.3 %collective-permute-start.28 = (f32[94,128]{1,0:T(8,128)S(1)}, f32[94,128]{1,0:T(8,128)S(1)}, u32[]{:S(2)}, u32[]{:S(2)}) collective-permute-start(f32[94,128]{1,0:T(8,128)S(1)} %bitcast.113), channel_id=1, source_target_pairs={{0,3},{1,0},{2,1},{3,2},{4,7},{5,4},{6,5},{7,6},{8,11},{9,8},{10,9... | collective-permute-start | bytes 144392 | tf_op jit(solution)/shard_map/ppermute | solution.py:743
  565.2 38.1 %collective-permute-start.25 = (bf16[1024,2048]{1,0:T(8,128)(2,1)}, bf16[1024,2048]{1,0:T(8,128)(2,1)}, u32[]{:S(2)}, u32[]{:S(2)}) collective-permute-start(bf16[1024,2048]{1,0:T(8,128)(2,1)} %pad_maximum_fusion.1), channel_id=1, source_target_pairs={{0,4},{4,0},{8,12},{12,8},{1,5},{5,1},{9,13},{13,9},{2,6},{6,2},{1... | collective-permute-start | bytes 12582920 | tf_op jit(solution)/shard_map/ppermute | solution.py:460
  569.1 3.7 collective-permute-start.33
  570.7 45.6 %copy-start.33 = (f32[2048]{0:T(1024)}, f32[2048]{0:T(1024)S(1)}, u32[]{:S(2)}) copy-start(f32[2048]{0:T(1024)S(1)} %slice_bitcast_fusion.4) | copy-start | bytes 24580
  570.7 5.1 collective-permute-start.29
  574.2 15.0 %collective-permute-start.35 = (bf16[256,1024]{0,1:T(8,128)(2,1)S(1)}, bf16[256,1024]{0,1:T(8,128)(2,1)S(1)}, u32[]{:S(2)}, u32[]{:S(2)}) collective-permute-start(bf16[256,1024]{0,1:T(8,128)(2,1)S(1)} %get-tuple-element.146), channel_id=1, source_target_pairs={{0,16},{16,0},{1,17},{17,1},{2,18},{18,2},{3,19},{19,3},{4,20},{20... | collective-permute-start | bytes 1572872 | tf_op jit(solution)/shard_map/ppermute | solution.py:468
  575.8 4.0 collective-permute-start.30
  579.8 8.8 %collective-permute-start.31 = (f32[64,128]{1,0:T(8,128)S(1)}, f32[64,128]{1,0:T(8,128)S(1)}, u32[]{:S(2)}, u32[]{:S(2)}) collective-permute-start(f32[64,128]{1,0:T(8,128)S(1)} %add.377), channel_id=1, source_target_pairs={{0,16},{16,0},{1,17},{17,1},{2,18},{18,2},{3,19},{19,3},{4,20},{20... | collective-permute-start | bytes 98312 | tf_op jit(solution)/shard_map/ppermute | solution.py:468
  601.7 12.8 %collective-permute-start.34 = (bf16[256,1024]{1,0:T(8,128)(2,1)S(1)}, bf16[256,1024]{1,0:T(8,128)(2,1)S(1)}, u32[]{:S(2)}, u32[]{:S(2)}) collective-permute-start(bf16[256,1024]{1,0:T(8,128)(2,1)S(1)} %get-tuple-element.148), channel_id=1, source_target_pairs={{0,16},{16,0},{1,17},{17,1},{2,18},{18,2},{3,19},{19,3},{4,20},{20... | collective-permute-start | bytes 1572872 | tf_op jit(solution)/shard_map/ppermute | solution.py:468
  (45 other events, 308.3 us)
Sparse Core Ops, SparseCore 0:
  11.0 83.5 all-gather.3
  96.1 79.1 all-gather.5
  176.9 113.2 all-gather.7
  378.8 77.7 reduce-scatter.4
  498.3 80.3 reduce-scatter.2

commit v3 on v2

--- a/solution.py
+++ b/solution.py
@@ -451,6 +451,72 @@
     )(half.reshape(1), heads, pack, act, down)
 
 
+def weight_grad_kernel(*refs, pairs):
+    out_ref = refs[-1]
+    at = 0
+    for pair in range(pairs):
+        rows_ref, cols_ref = refs[2 * pair], refs[2 * pair + 1]
+        span = slice(at, at + cols_ref.shape[1])
+        out_ref[:, span] = lax.dot_general(
+            rows_ref[...], cols_ref[...], (((0,), (0,)), ((), ())), preferred_element_type=F32
+        ).astype(BF16)
+        at += cols_ref.shape[1]
+
+
+def weight_grad(pairs, count):
+    width = pairs[0][0].shape[1]
+    block = width // (2 * count)
+    total = sum(cols.shape[1] for _, cols in pairs)
+    tokens = pairs[0][0].shape[0]
+    if block % LANES:
+        grads = [
+            jnp.einsum("rd,rc->dc", rows, cols, preferred_element_type=F32) for rows, cols in pairs
+        ]
+        grads = jnp.concatenate(grads, axis=1).astype(BF16).reshape(2, count, block, total)
+        return grads.transpose(1, 0, 2, 3).reshape(width, total)
+    specs = []
+    for rows, cols in pairs:
+        specs.append(pl.BlockSpec((tokens, block), lambda i: (0, (i % 2) * count + i // 2)))
+        specs.append(pl.BlockSpec(cols.shape, lambda i: (0, 0)))
+    return pl.pallas_call(
+        partial(weight_grad_kernel, pairs=len(pairs)),
+        grid=(2 * count,),
+        in_specs=specs,
+        out_specs=pl.BlockSpec((block, total), lambda i: (i, 0)),
+        out_shape=jax.ShapeDtypeStruct((width, total), BF16),
+        compiler_params=params(),
+        cost_estimate=cost(2 * tokens * width * total, 2 * (tokens * (width + total) + width * total)),
+        name="weight_grad",
+    )(*[array for pair in pairs for array in pair])
+
+
+def place_kernel(core_ref, rows_ref, *refs):
+    refs[-1][...] = rows_ref[...]
+
+
+def place_half(half, rows, before=None, block=256):
+    count, width = rows.shape
+    steps = count // block
+    operands, specs = [rows], [pl.BlockSpec((block, width), lambda i, h: (i, 0))]
+    if before is not None:
+        operands.append(before)
+        specs.append(pl.BlockSpec(memory_space=pl.ANY))
+    return pl.pallas_call(
+        place_kernel,
+        grid_spec=pltpu.PrefetchScalarGridSpec(
+            num_scalar_prefetch=1,
+            grid=(steps,),
+            in_specs=specs,
+            out_specs=pl.BlockSpec((block, width), lambda i, h: (h[0] * steps + i, 0)),
+        ),
+        out_shape=jax.ShapeDtypeStruct((2 * count, width), rows.dtype),
+        input_output_aliases={} if before is None else {2: 0},
+        compiler_params=params(),
+        cost_estimate=cost(0, 4 * count * width),
+        name="place_half",
+    )(half.reshape(1), *operands)
+
+
 CORE = [(0, 1), (1, 0), (2, 3), (3, 2)]
 YAX = [(0, 2), (2, 0), (1, 3), (3, 1)]
 XAX = [(0, 1), (1, 0)]
@@ -492,72 +558,57 @@
     )
 
 
-def plane_gather(first, second, core, why, ex):
-    first_next, second_next = x_swap(first), y_swap(second)
-    first, second = join(ex, first, first_next), join(why, second, second_next)
-    first_next, second_next = y_swap(first), x_swap(second)
-    first, second = join(why, first, first_next), join(ex, second, second_next)
-    mine = jnp.concatenate([first, second], 0)
-    return join(core, mine, core_swap(mine))
-
-
 def after(value, *first):
     return lax.optimization_barrier((value,) + first)[0]
 
 
-def reduce_sends(piece, place, count, step, got):
-    right = piece(jnp.minimum(count - 1 - step + place, count - 1))
-    left = piece(jnp.maximum(place - (count - 1 - step), 0))
-    if got is None:
-        return right, left
-    return add16(right, got[0]), add16(left, got[1])
-
-
-def reduce_hop(sends, count, step):
-    return (
-        lax.ppermute(sends[0], "dp", [(k, k + 1) for k in range(step + 1)]),
-        lax.ppermute(sends[1], "dp", [(count - 1 - k, count - 2 - k) for k in range(step + 1)]),
-    )
-
-
-def reduced(piece, place, got):
-    right, left = got
-    return piece(place).astype(F32) + right.astype(F32) + left.astype(F32)
+def rows_at(array, start, index, size):
+    return lax.dynamic_slice_in_dim(array, start + index * size, size, 0)
 
 
 def halving_send(keep, got, why, ex):
     quarter = keep.shape[0] // 2
     eighth = quarter // 2
-    first = add16(
-        pick(keep[:quarter], 1 - why, eighth), pick(got[:quarter], 1 - why, eighth)
-    )
-    second = add16(pick(keep[quarter:], 1 - ex, eighth), pick(got[quarter:], 1 - ex, eighth))
-    return first, second
-
-
-def halving_rest(keep, got, two, why, ex):
+
+    def send(start, index):
+        return add16(rows_at(keep, start, index, eighth), rows_at(got, start, index, eighth))
+
+    return send(0, 1 - why), send(quarter, 1 - ex)
+
+
+def halving_more(keep, got, two, why, ex):
     quarter = keep.shape[0] // 2
     eighth, sixteenth = quarter // 2, quarter // 4
 
-    def mine(start, index, received):
-        rows = slice(start, start + quarter)
+    def mine(start, index, received, part):
+        at = start + index * eighth
         return (
-            pick(keep[rows], index, eighth).astype(F32)
-            + pick(got[rows], index, eighth).astype(F32)
-            + received.astype(F32)
+            rows_at(keep, at, part, sixteenth).astype(F32)
+            + rows_at(got, at, part, sixteenth).astype(F32)
+            + rows_at(received, 0, part, sixteenth).astype(F32)
         )
 
-    first, second = mine(0, why, two[0]), mine(quarter, ex, two[1])
-    first_got = x_swap(pick(first, 1 - ex, sixteenth).astype(BF16))
-    second_got = y_swap(pick(second, 1 - why, sixteenth).astype(BF16))
-    return (
-        pick(first, ex, sixteenth) + first_got.astype(F32),
-        pick(second, why, sixteenth) + second_got.astype(F32),
-    )
-
-
-def weight_grad(rows, cols):
-    return jnp.einsum("rd,rc->dc", rows, cols, preferred_element_type=F32).astype(BF16)
+    kept = mine(0, why, two[0], ex), mine(quarter, ex, two[1], why)
+    sent = (
+        mine(0, why, two[0], 1 - ex).astype(BF16),
+        mine(quarter, ex, two[1], 1 - why).astype(BF16),
+    )
+    return kept, sent
+
+
+def gather_one(first, second):
+    return x_swap(first), y_swap(second)
+
+
+def gather_two(first, second, got, why, ex):
+    first, second = join(ex, first, got[0]), join(why, second, got[1])
+    return (first, second), (y_swap(first), x_swap(second))
+
+
+def gather_last(two, got, core, why, ex):
+    first, second = join(why, two[0], got[0]), join(ex, two[1], got[1])
+    mine = jnp.concatenate([first, second], 0)
+    return mine, core_swap(mine)
 
 
 def local(
@@ -627,77 +678,23 @@
     attended_grad = jnp.dot(
         grad_rows, heads_full[:, qkv_cols:], preferred_element_type=F32
     ).astype(BF16)
-    out_partial = weight_grad(grad_rows, attended)
-    attended_grad = after(attended_grad, out_partial)
     qkv_grad, qkv_bias_part = attend_back(
         qkv, attended_grad, log_total, key_bias, cos_table.T, sin_table.T
     )
-    qkv_partial = weight_grad(normed1, qkv_grad)
-
-    def split(partial_sum, at):
-        return pick(partial_sum.reshape(2, count, chunk, -1), at, 1, 1)[:, 0]
-
-    def heads_piece(at):
-        return jnp.concatenate([split(qkv_partial, at), split(out_partial, at)], axis=-1)
-
-    def run_hops(piece, got, first, last):
-        for step in range(first, last):
-            got = reduce_hop(reduce_sends(piece, place, count, step, got), count, step)
-        return got
-
-    hops_a, hops_b = (count - 1) // 3, 2 * (count - 1) // 3
-    got = run_hops(heads_piece, None, 0, hops_a - 1)
-    sends = reduce_sends(heads_piece, place, count, hops_a - 1, got)
-    got = reduce_hop(sends, count, hops_a - 1)
+    heads_partial = weight_grad([(normed1, qkv_grad), (grad_rows, attended)], count)
+
+    def scatter(partial_sum):
+        return lax.psum_scatter(partial_sum, "dp", scatter_dimension=0, tiled=True)
+
+    heads_total = scatter(heads_partial)
     input_part, dot1, sum1 = dgrad_first(
-        after(qkv_grad, *sends), heads_full, tokens, mean, inv_std, ln1_gain[None]
-    )
-    got = after(got, input_part)
-    got = run_hops(heads_piece, got, hops_a, hops_b - 1)
-    sends = reduce_sends(heads_piece, place, count, hops_b - 1, got)
-    got = reduce_hop(sends, count, hops_b - 1)
+        after(qkv_grad, heads_partial), heads_full, tokens, mean, inv_std, ln1_gain[None]
+    )
     activated, slope = up_gelu(
-        after(normed2, input_part, *sends), up_full, pick(up_bias, ex, units)[None]
-    )
-    got = after(got, activated)
-    got = run_hops(heads_piece, got, hops_b, count - 2)
-    sends = reduce_sends(heads_piece, place, count, count - 2, got)
-    got = reduce_hop(sends, count, count - 2)
-    down_partial = weight_grad(after(grad_rows, activated, *sends), activated)
-
-    def scatter(partial_sum):
-        return lax.psum_scatter(
-            partial_sum.reshape(2, width // 2, -1), "dp", scatter_dimension=1, tiled=True
-        )
-
+        after(normed2, input_part), up_full, pick(up_bias, ex, units)[None]
+    )
+    down_partial = weight_grad([(after(grad_rows, activated), activated)], count)
     down_total = scatter(down_partial)
-    got = after(got, down_partial)
-    heads_total = reduced(heads_piece, place, got)
-
-    branch_send = branch_half(
-        1 - core, attended, heads_full, after(activated, down_partial, heads_total), down_full
-    )
-    branch_core = core_swap(branch_send)
-    branch_keep = branch_half(core, attended, heads_full, after(activated, branch_send), down_full)
-    branch_core = after(branch_core, branch_keep)
-    branch_two = halving_send(branch_keep, branch_core, why, ex)
-    branch_two_got = y_swap(branch_two[0]), x_swap(branch_two[1])
-    hidden_grad, up_bias_part = hidden_back(
-        after(grad_rows, branch_keep, *branch_two), down_full, slope
-    )
-    norm_rows = tokens, mean, inv_std, ln2_gain[None], input_part
-    input_send, dot2, sum2 = dgrad_half(1 - core, hidden_grad, up_full, *norm_rows)
-    input_core = core_swap(input_send)
-    input_keep, dot3, sum3 = dgrad_half(core, after(hidden_grad, input_send), up_full, *norm_rows)
-    dot2, sum2 = dot2 + dot3, sum2 + sum3
-    input_core = after(input_core, input_keep)
-    input_two = halving_send(input_keep, input_core, why, ex)
-    input_two_got = y_swap(input_two[0]), x_swap(input_two[1])
-    branch_two_got = after(branch_two_got, input_keep)
-    up_partial = weight_grad(after(normed2, input_keep, *input_two), hidden_grad)
-    up_total = scatter(up_partial)
-    branch_first, branch_second = halving_rest(branch_keep, branch_core, branch_two_got, why, ex)
-    input_first, input_second = halving_rest(input_keep, input_core, input_two_got, why, ex)
 
     shift_sum = out_bias + down_bias
     tokens_own = own_rows(tokens, core, why, ex)
@@ -710,10 +707,6 @@
         return (
             tokens_own[at].astype(F32) + validity_own[at][:, None] * (total + shift_sum)
         ).astype(BF16)
-
-    output_rows = plane_gather(
-        output_of(0, branch_first), output_of(1, branch_second), core, why, ex
-    )
 
     def input_of(at, total):
         unit = (tokens_own[at].astype(F32) - mean_own[at]) * inv_own[at]
@@ -724,10 +717,35 @@
         )
         return (out_grad_own[at].astype(F32) + back).astype(BF16)
 
-    grad_input = plane_gather(
-        input_of(0, input_first), input_of(1, input_second), core, why, ex
-    )
-
+    branch_send = branch_half(
+        1 - core, attended, heads_full, after(activated, down_partial), down_full
+    )
+    branch_core = core_swap(branch_send)
+    branch_keep = branch_half(core, attended, heads_full, after(activated, branch_send), down_full)
+    branch_core = after(branch_core, branch_keep)
+    branch_two = halving_send(branch_keep, branch_core, why, ex)
+    branch_two_got = y_swap(branch_two[0]), x_swap(branch_two[1])
+    hidden_grad, up_bias_part = hidden_back(
+        after(grad_rows, branch_keep, *branch_two), down_full, slope
+    )
+    norm_rows = tokens, mean, inv_std, ln2_gain[None], input_part
+    branch_two_got = after(branch_two_got, hidden_grad)
+    branch_mine, branch_three = halving_more(branch_keep, branch_core, branch_two_got, why, ex)
+    branch_three_got = x_swap(branch_three[0]), y_swap(branch_three[1])
+    input_send, dot2, sum2 = dgrad_half(
+        1 - core, after(hidden_grad, *branch_three), up_full, *norm_rows
+    )
+    input_core = core_swap(input_send)
+    input_keep, dot3, sum3 = dgrad_half(core, after(hidden_grad, input_send), up_full, *norm_rows)
+    input_core = after(input_core, input_keep)
+    input_two = halving_send(input_keep, input_core, why, ex)
+    input_two_got = y_swap(input_two[0]), x_swap(input_two[1])
+    branch_three_got = after(branch_three_got, *input_two)
+    output_one = [
+        output_of(at, branch_mine[at] + branch_three_got[at].astype(F32)) for at in range(2)
+    ]
+    output_got = gather_one(*output_one)
+    dot2, sum2 = dot2 + dot3, sum2 + sum3
     vectors = jnp.concatenate(
         [
             dot1[0],
@@ -743,33 +761,63 @@
         lax.ppermute(vectors, "dp", [(k, (k + hop) % count) for k in range(count)])
         for hop in range(1, count)
     ]
+    up_partial = weight_grad([(after(normed2, vectors, *output_one), hidden_grad)], count)
+    up_total = scatter(up_partial)
+    hops = after(hops, up_partial)
     vectors = sum(hops, vectors)
-    norm_rows, bias_rows = 4 * width // LANES, width // LANES
+    norm_count, bias_rows = 4 * width // LANES, width // LANES
     norms, bias_grad, biases = (
-        vectors[:norm_rows],
-        vectors[norm_rows : norm_rows + bias_rows].reshape(width),
-        vectors[norm_rows + bias_rows :],
-    )
-    for swap in (core_swap, y_swap, x_swap):
-        norms = norms + swap(norms)
-    norms = norms.reshape(4, width)
-    other = x_swap(biases).reshape(-1)
-    biases = biases.reshape(-1)
+        vectors[:norm_count],
+        vectors[norm_count : norm_count + bias_rows].reshape(width),
+        vectors[norm_count + bias_rows :],
+    )
+
+    def share(total):
+        mine, given = pick(total, ex, chunk), pick(total, 1 - ex, chunk)
+        return mine.astype(F32), x_swap(given.astype(BF16))
+
+    heads_mine, heads_other = share(after(heads_total, up_partial))
+    norms_other, biases_other = core_swap(norms), x_swap(biases)
+    input_two_got = after(input_two_got, up_partial, norms)
+    input_mine, input_three = halving_more(input_keep, input_core, input_two_got, why, ex)
+    input_three_got = x_swap(input_three[0]), y_swap(input_three[1])
+    output_got, norms_other, biases_other, heads_other = after(
+        (output_got, norms_other, biases_other, heads_other), *input_three
+    )
+    output_two, output_got = gather_two(*output_one, output_got, why, ex)
+    norms = norms + norms_other
+    norms_other = y_swap(norms)
+    input_three_got, norms_other = after(
+        (input_three_got, norms_other), norms, *output_two
+    )
+    input_one = [input_of(at, input_mine[at] + input_three_got[at].astype(F32)) for at in range(2)]
+    input_got = gather_one(*input_one)
+    norms = norms + norms_other
+    norms_other = x_swap(norms)
+    output_got, norms_other, down_total = after(
+        (output_got, norms_other, down_total), norms, *input_one
+    )
+    output_mine, output_other = gather_last(output_two, output_got, core, why, ex)
+    down_mine, down_other = share(down_total)
+    input_got = after(input_got, output_mine)
+    input_two, input_got = gather_two(*input_one, input_got, why, ex)
+    norms = (norms + norms_other).reshape(4, width)
+    biases, other = biases.reshape(-1), biases_other.reshape(-1)
     qkv_bias_grad = join(ex, biases[:qkv_cols], other[:qkv_cols])
     up_bias_grad = join(ex, biases[qkv_cols:], other[qkv_cols:])
-
-    def share(total):
-        mine = lax.dynamic_index_in_dim(total, ex, 0, keepdims=False)
-        given = lax.dynamic_index_in_dim(total, 1 - ex, 0, keepdims=False)
-        return mine.astype(F32), x_swap(given.astype(BF16)).astype(F32)
-
-    mine, other = share(heads_total)
-    qkv_out = join(ex, mine[:, :qkv_cols], other[:, :qkv_cols], 1)
-    out_out = join(ex, mine[:, qkv_cols:].T, other[:, qkv_cols:].T, 0)
-    mine, other = share(down_total)
-    down_out = join(ex, mine.T, other.T, 0)
-    mine, other = share(up_total)
-    up_out = join(ex, mine, other, 1)
+    other = heads_other.astype(F32)
+    qkv_out = join(ex, heads_mine[:, :qkv_cols], other[:, :qkv_cols], 1)
+    out_out = join(ex, heads_mine[:, qkv_cols:].T, other[:, qkv_cols:].T, 0)
+    down_out = join(ex, down_mine.T, down_other.T.astype(F32), 0)
+    output_rows = place_half(
+        1 - core, output_other, place_half(core, after(output_mine, *input_two))
+    )
+    input_got = after(input_got, output_rows, norms, qkv_out, out_out, down_out)
+    input_mine, input_other = gather_last(input_two, input_got, core, why, ex)
+    up_mine, up_other = share(after(up_total, input_mine))
+    grad_half = place_half(core, input_mine)
+    up_out = join(ex, up_mine, up_other.astype(F32), 1)
+    grad_input = place_half(1 - core, after(input_other, up_out), grad_half)
 
     return (
         output_rows,

time: 630 us -> 543 us (0.86)
  Pallas kernels: 131 us -> 194 us
  local copies, waits for them, and re-layouts: 59.3 us -> 16.8 us
  matrix products: 47.6 us -> 6.94 us
  starting transfers between devices: 63.2 us -> 25.6 us
  other arithmetic: 114 us -> 99 us
  waiting for transfers between devices: 193 us -> 179 us
    pallas_call x0 -> x7, Pallas kernels: none -> 63.4 us  [the longest x3 44.3 us: weight_grad(): pl.pallas_call(partial(weight_grad_kernel, pairs=len(pairs)), grid=(2 * c...]
    all_gather x1, waiting for transfers between devices: 0.01 us -> 49.2 us  [local(): down_full = lax.all_gather(down_shard, 'dp', axis=0, tiled=True)]
    ppermute x6 -> x0, waiting for transfers between devices: 41 us -> none  [the longest x3 35.8 us: reduce_hop(): lax.ppermute(sends[0], 'dp', [(k, k + 1) for k in range(step + 1)])]
    dot_general x4 -> x0, matrix products: 40.6 us -> none  [weight_grad(): jnp.einsum('rd,rc->dc', rows, cols, preferred_element_type=F32).astype(BF16)]
    ppermute x9, waiting for transfers between devices: 56 us -> 22 us  [y_swap(): return lax.ppermute(block, 'tensor', YAX)]
    ppermute x6 -> x0, starting transfers between devices: 31.2 us -> none  [the longest x3 26.5 us: reduce_hop(): lax.ppermute(sends[0], 'dp', [(k, k + 1) for k in range(step + 1)])]
    dynamic_slice x23 -> x7, local copies, waits for them, and re-layouts: 21.8 us -> 5.44 us  [pick(): return lax.dynamic_slice_in_dim(array, index * size, size, axis)]
    select_n x16 -> x14, other arithmetic: 34.1 us -> 21.9 us  [join(): jnp.where(low_index == 0, jnp.concatenate([mine, other], axis), jnp.conca...]
  transfers between devices with their start and end apart: 41 -> 36, of which waited for: 20 -> 13; matrix products, arithmetic and copies ran while one was open for 33% -> 22% of each run, Pallas kernels for 15% -> 35%
where the time goes in v3:
time: 543 us; the launch traced here: 537 us
  Pallas kernels  194 us (36%)
  waiting for transfers between devices  179 us (33%)
  other arithmetic  99 us (18%)
  starting transfers between devices  25.6 us (5%)
  local copies, waits for them, and re-layouts  16.8 us (3%)
  between operations  15.8 us (3%)
  matrix products  6.94 us (1%)
    ppermute x13, waiting for transfers between devices, x_swap(): return lax.ppermute(block, 'branch', XAX)  66.7 us
    all_gather x1, waiting for transfers between devices, local(): down_full = lax.all_gather(down_shard, 'dp', axis=0, tiled=True)  49.2 us
    pallas_call x3, Pallas kernels, weight_grad(): pl.pallas_call(partial(weight_grad_kernel, pairs=len(pairs)), grid=(2 * c...  44.3 us
    all_gather x1, waiting for transfers between devices, local(): heads_full = lax.all_gather(heads_shard, 'dp', axis=0, tiled=True)  38.3 us
    pallas_call x2, Pallas kernels, dgrad_half(): pl.pallas_call(partial(dgrad_half_kernel, chunk=chunk), grid_spec=pltpu.P...  24.7 us
    ppermute x9, waiting for transfers between devices, y_swap(): return lax.ppermute(block, 'tensor', YAX)  22 us
    select_n x14, other arithmetic, join(): jnp.where(low_index == 0, jnp.concatenate([mine, other], axis), jnp.conca...  21.9 us
    pallas_call x2, Pallas kernels, branch_half(): pl.pallas_call(partial(branch_kernel, chunk=chunk), grid_spec=pltpu.Prefe...  20.2 us
  transfers between devices with their start and end apart: 36, of which 13 were waited for; matrix products, arithmetic and copies ran while one was open for 22% of the time, Pallas kernels for 35%

profile of v3, /device:TPU:0, one launch (start us, length us, event | category | flops | bytes accessed | tf_op | source)
XLA Modules:
  0.0 536.6 jit_solution(2547992751934261764)
XLA Ops:
  16.3 4.5 convert_reduce_fusion
  20.9 6.3 %fusion.8 = f32[2048]{0:T(1024)S(1)} fusion(bf16[2048,2048]{1,0:T(8,128)(2,1)} %rows_ref.5, f32[2048]{0:T(1024)S(1)} %broadcast_multiply_fusion.1), kind=kLoop, calls=%fused_computation.10 | loop fusion | flops 16775168 | bytes 8404992 | tf_op jit(solution)/shard_map/reduce_sum | solution.py:662
  29.2 3.9 fusion.28
  33.2 2.6 maximum_maximum_fusion.2
  35.8 8.7 %convert_reduce_fusion.1 = (f32[2048]{0:T(1024)S(1)}, bf16[2048,2048]{1,0:T(8,128)(2,1)}) fusion(bf16[2048,2048]{1,0:T(8,128)(2,1)} %param.31, bf16[2048]{0:T(1024)(128)(2,1)S(1)} %convert_convert_fusion), kind=kLoop, calls=%fused_computation.11 | loop fusion | flops 12580864 | bytes 16789504 | tf_op jit(solution)/shard_map/reduce_sum | solution.py:755
  44.5 11.7 %fusion.7 = (bf16[2048,2048]{1,0:T(8,128)(2,1)}, bf16[2048,2048]{1,0:T(8,128)(2,1)}) fusion(bf16[2048,2048]{1,0:T(8,128)(2,1)} %rows_ref.5, f32[2048]{0:T(1024)S(1)} %copy-done.16, f32[2048]{0:T(1024)S(1)} %copy-done.13, f32[2048]{0:T(1024)S(1)} %add_rsqrt_fusion, f32[2048]{0:T(1024)S(1)} %broadcast_multiply_fusion.1, f32[2048]{0:T(1024)S(1)} %copy-done.17, ...), kind=kLoop, calls=%fused_computation.9 | loop fusion | flops 37748736 | bytes 25214976 | tf_op jit(solution)/shard_map/convert_element_type | solution.py:666
  56.2 38.3 %all-gather.4.cloned.1.call-done.weight_ref.out_ref_w = bf16[2048,1024]{1,0:T(8,128)(2,1)} async-done(((bf16[512,1024]{1,0:T(8,128)(2,1)}), bf16[2048,1024]{1,0:T(8,128)(2,1)}) %all-gather.4.cloned.1.call-update) | async-done | bytes 4194320 | tf_op jit(solution)/shard_map/all_gather | solution.py:649
  94.5 11.8 %project.1.query_ref.key_ref.value_ref = bf16[2048,768]{1,0:T(8,128)(2,1)} custom-call(bf16[2048,2048]{1,0:T(8,128)(2,1)} %get-tuple-element.171.rows_ref.refs_0_, bf16[2048,1024]{1,0:T(8,128)(2,1)} %all-gather.4.cloned.1.call-done.weight_ref.out_ref_w, f32[1,768]{1,0:T(1,128)} %broadcast_in_dim.22.bias_ref, f32[2048,128]{1,0:T(8,128)} %get-tuple-element.205.cos_ref, ...), custom_call_target="tpu_custom_call" | custom-call | flops 6442450 | bytes 14680 | tf_op jit(solution)/shard_map/project/pallas_call | solution.py:77
  107.5 8.7 %attend.1 = (bf16[2048,256]{1,0:T(8,128)(2,1)}, f32[8,2048]{1,0:T(8,128)}) custom-call(bf16[2048,768]{1,0:T(8,128)(2,1)} %project.1.query_ref.key_ref.value_ref, bf16[2048,768]{1,0:T(8,128)(2,1)} %project.1.query_ref.key_ref.value_ref, bf16[2048,768]{1,0:T(8,128)(2,1)} %project.1.query_ref.key_ref.value_ref, f32[2048,128]{1,0:T(8,128)} %broadcast_in_dim.27.bias_ref), custom_call_target="tpu_custom_call" | custom-call | flops 2684354 | bytes 4194 | tf_op jit(solution)/shard_map/attend/pallas_call | solution.py:140
  116.3 6.9 %convolution_convert_fusion.grad_ref = bf16[2048,256]{1,0:T(8,128)(2,1)} fusion(bf16[2048,2048]{1,0:T(8,128)(2,1)} %get-tuple-element.82.refs_2_.refs_0_.grad_ref, bf16[2048,1024]{1,0:T(8,128)(2,1)} %all-gather.4.cloned.1.call-done.weight_ref.out_ref_w), kind=kOutput, calls=%fused_computation.15 | convolution fusion | flops 2148007936 | bytes 10485760 | tf_op jit(solution)/shard_map/dot_general | solution.py:678
  123.2 14.9 %attend_back.1 = (bf16[2048,768]{1,0:T(8,128)(2,1)}, f32[1,768]{1,0:T(1,128)}) custom-call(bf16[2048,768]{1,0:T(8,128)(2,1)} %project.1.query_ref.key_ref.value_ref, bf16[2048,768]{1,0:T(8,128)(2,1)} %project.1.query_ref.key_ref.value_ref, bf16[2048,768]{1,0:T(8,128)(2,1)} %project.1.query_ref.key_ref.value_ref, ...), custom_call_target="tpu_custom_call" | custom-call | flops 6710886 | bytes 8388 | tf_op jit(solution)/shard_map/attend_back/pallas_call | solution.py:213
  138.1 15.7 %weight_grad.3 = bf16[2048,1024]{1,0:T(8,128)(2,1)} custom-call(bf16[2048,2048]{1,0:T(8,128)(2,1)} %get-tuple-element.171.rows_ref.refs_0_, bf16[2048,768]{1,0:T(8,128)(2,1)} %get-tuple-element.74.refs_1_.grad_ref, bf16[2048,2048]{1,0:T(8,128)(2,1)} %get-tuple-element.82.refs_2_.refs_0_.grad_ref, bf16[2048,256]{1,0:T(8,128)(2,1)} %get-tuple-element.71.refs_3_.heads_ref), custom_call_target="tpu_custom_call" | custom-call | flops 8589934 | bytes 16777 | tf_op jit(solution)/shard_map/weight_grad/pallas_call | solution.py:481
  157.8 17.2 %dgrad_first.1 = (f32[2048,2048]{1,0:T(8,128)}, f32[1,2048]{1,0:T(1,128)}, f32[1,2048]{1,0:T(1,128)}) custom-call(bf16[2048,768]{1,0:T(8,128)(2,1)} %get-tuple-element.74.refs_1_.grad_ref, bf16[2048,1024]{1,0:T(8,128)(2,1)} %all-gather.4.cloned.1.call-done.weight_ref.out_ref_w, bf16[2048,2048]{1,0:T(8,128)(2,1)} %rows_ref.5, f32[2048,1]{1,0:T(8,128)} %copy.37.mean_ref, ...), custom_call_target="tpu_custom_call" | custom-call | flops 6442450 | bytes 28311 | tf_op jit(solution)/shard_map/dgrad_first/pallas_call | solution.py:364
  175.3 17.4 %up_gelu.1 = (bf16[2048,1024]{1,0:T(8,128)(2,1)}, f32[2048,1024]{1,0:T(8,128)}) custom-call(bf16[2048,2048]{1,0:T(8,128)(2,1)} %get-tuple-element.102.rows_ref.refs_0_, bf16[2048,1024]{1,0:T(8,128)(2,1)} %all-gather.6.cloned.1.call-done.weight_ref, f32[1,1024]{1,0:T(1,128)} %bitcast.57), custom_call_target="tpu_custom_call" | custom-call | flops 8589934 | bytes 25165 | tf_op jit(solution)/shard_map/up_gelu/pallas_call | solution.py:260
  192.7 14.2 %weight_grad.4 = bf16[2048,1024]{1,0:T(8,128)(2,1)} custom-call(bf16[2048,2048]{1,0:T(8,128)(2,1)} %get-tuple-element.82.refs_2_.refs_0_.grad_ref, bf16[2048,1024]{1,0:T(8,128)(2,1)} %get-tuple-element.80.refs_1_.act_ref), custom_call_target="tpu_custom_call" | custom-call | flops 8589934 | bytes 16777 | tf_op jit(solution)/shard_map/weight_grad/pallas_call | solution.py:481
  206.9 49.2 %all-gather.8.cloned.1.call-done.down_ref.weight_ref = bf16[2048,1024]{1,0:T(8,128)(2,1)} async-done(((bf16[512,1024]{1,0:T(8,128)(2,1)}), bf16[2048,1024]{1,0:T(8,128)(2,1)}) %all-gather.8.cloned.1.call-update) | async-done | bytes 4194320 | tf_op jit(solution)/shard_map/all_gather | solution.py:651
  256.1 10.0 %branch_half.2 = bf16[1024,2048]{1,0:T(8,128)(2,1)} custom-call(s32[1]{0:T(128)} %bitcast.half_ref.core_ref, bf16[2048,256]{1,0:T(8,128)(2,1)} %get-tuple-element.71.refs_3_.heads_ref, bf16[2048,1024]{1,0:T(8,128)(2,1)} %all-gather.4.cloned.1.call-done.weight_ref.out_ref_w, bf16[2048,1024]{1,0:T(8,128)(2,1)} %get-tuple-element.80.refs_1_.act_ref, ...), custom_call_target="tpu_custom_call" | custom-call | flops 5368709 | bytes 10485 | tf_op jit(solution)/shard_map/branch_half/pallas_call | solution.py:434
  266.3 10.1 %branch_half.3 = bf16[1024,2048]{1,0:T(8,128)(2,1)} custom-call(s32[1]{0:T(128)} %bitcast.2.half_ref.core_ref, bf16[2048,256]{1,0:T(8,128)(2,1)} %get-tuple-element.71.refs_3_.heads_ref, bf16[2048,1024]{1,0:T(8,128)(2,1)} %all-gather.4.cloned.1.call-done.weight_ref.out_ref_w, bf16[2048,1024]{1,0:T(8,128)(2,1)} %get-tuple-element.80.refs_1_.act_ref, ...), custom_call_target="tpu_custom_call" | custom-call | flops 5368709 | bytes 10485 | tf_op jit(solution)/shard_map/branch_half/pallas_call | solution.py:434
  276.4 3.1 add_convert_fusion.2
  282.5 15.6 %hidden_back.1 = (bf16[2048,1024]{1,0:T(8,128)(2,1)}, f32[1,1024]{1,0:T(1,128)}) custom-call(bf16[2048,2048]{1,0:T(8,128)(2,1)} %get-tuple-element.82.refs_2_.refs_0_.grad_ref, bf16[2048,1024]{1,0:T(8,128)(2,1)} %all-gather.8.cloned.1.call-done.down_ref.weight_ref, f32[2048,1024]{1,0:T(8,128)} %get-tuple-element.83.slope_ref), custom_call_target="tpu_custom_call" | custom-call | flops 8589934 | bytes 25165 | tf_op jit(solution)/shard_map/hidden_back/pallas_call | solution.py:297
  298.1 7.0 %collective-permute-done.2 = bf16[256,2048]{1,0:T(8,128)(2,1)S(1)} collective-permute-done((bf16[256,2048]{1,0:T(8,128)(2,1)S(1)}, bf16[256,2048]{1,0:T(8,128)(2,1)S(1)}, u32[]{:S(2)}, u32[]{:S(2)}) %collective-permute-start.2) | collective-permute-done | bytes 1048608 | tf_op jit(solution)/shard_map/ppermute | solution.py:534
  306.4 2.2 add_convert_fusion.6
  308.7 12.4 %dgrad_half.2 = (bf16[1024,2048]{1,0:T(8,128)(2,1)}, f32[1,2048]{1,0:T(1,128)}, f32[1,2048]{1,0:T(1,128)}) custom-call(s32[1]{0:T(128)} %bitcast.half_ref.core_ref, bf16[2048,1024]{1,0:T(8,128)(2,1)} %get-tuple-element.89.grad_ref.refs_1_, bf16[2048,1024]{1,0:T(8,128)(2,1)} %all-gather.6.cloned.1.call-done.weight_ref, bf16[2048,2048]{1,0:T(8,128)(2,1)} %rows_ref.5, ...), custom_call_target="tpu_custom_call" | custom-call | flops 4294967 | bytes 16777 | tf_op jit(solution)/shard_map/dgrad_half/pallas_call | solution.py:394
  323.6 12.3 %dgrad_half.3 = (bf16[1024,2048]{1,0:T(8,128)(2,1)}, f32[1,2048]{1,0:T(1,128)}, f32[1,2048]{1,0:T(1,128)}) custom-call(s32[1]{0:T(128)} %bitcast.2.half_ref.core_ref, bf16[2048,1024]{1,0:T(8,128)(2,1)} %get-tuple-element.89.grad_ref.refs_1_, bf16[2048,1024]{1,0:T(8,128)(2,1)} %all-gather.6.cloned.1.call-done.weight_ref, bf16[2048,2048]{1,0:T(8,128)(2,1)} %rows_ref.5, ...), custom_call_target="tpu_custom_call" | custom-call | flops 4294967 | bytes 16777 | tf_op jit(solution)/shard_map/dgrad_half/pallas_call | solution.py:394
  337.5 4.0 add_convert_fusion
  346.5 3.2 fusion.18
  349.7 14.4 %weight_grad.5 = bf16[2048,1024]{1,0:T(8,128)(2,1)} custom-call(bf16[2048,2048]{1,0:T(8,128)(2,1)} %get-tuple-element.102.rows_ref.refs_0_, bf16[2048,1024]{1,0:T(8,128)(2,1)} %get-tuple-element.89.grad_ref.refs_1_), custom_call_target="tpu_custom_call" | custom-call | flops 8589934 | bytes 16777 | tf_op jit(solution)/shard_map/weight_grad/pallas_call | solution.py:481
  364.1 2.5 dynamic-slice_convert_fusion.1
  370.9 2.4 add_convert_fusion.4
  373.3 18.2 %collective-permute-done.12 = f32[14,128]{1,0:T(8,128)S(1)} collective-permute-done((f32[14,128]{1,0:T(8,128)S(1)}, f32[14,128]{1,0:T(8,128)S(1)}, u32[]{:S(2)}, u32[]{:S(2)}) %collective-permute-start.12) | collective-permute-done | bytes 7200 | tf_op jit(solution)/shard_map/ppermute | solution.py:534
  398.2 8.7 %collective-permute-done.20 = f32[64,128]{1,0:T(8,128)S(1)} collective-permute-done((f32[64,128]{1,0:T(8,128)S(1)}, f32[64,128]{1,0:T(8,128)S(1)}, u32[]{:S(2)}, u32[]{:S(2)}) %collective-permute-start.20) | collective-permute-done | bytes 32800 | tf_op jit(solution)/shard_map/ppermute | solution.py:530
  407.0 3.2 fusion.22
  410.8 3.3 fusion.26
  416.2 10.1 %collective-permute-done.21 = f32[64,128]{1,0:T(8,128)S(1)} collective-permute-done((f32[64,128]{1,0:T(8,128)S(1)}, f32[64,128]{1,0:T(8,128)S(1)}, u32[]{:S(2)}, u32[]{:S(2)}) %collective-permute-start.21) | collective-permute-done | bytes 32800 | tf_op jit(solution)/shard_map/ppermute | solution.py:534
  426.3 3.3 maximum_select_fusion
  429.6 2.5 maximum_select_fusion.1
  432.2 2.6 pad_maximum_fusion.rows_ref
  437.1 12.0 %collective-permute-done.24 = bf16[128,2048]{1,0:T(8,128)(2,1)S(1)} collective-permute-done((bf16[128,2048]{1,0:T(8,128)(2,1)S(1)}, bf16[128,2048]{1,0:T(8,128)(2,1)S(1)}, u32[]{:S(2)}, u32[]{:S(2)}) %collective-permute-start.24) | collective-permute-done | bytes 524320 | tf_op jit(solution)/shard_map/ppermute | solution.py:530
  458.5 4.8 place_half.4.refs_0_
  463.3 24.2 %collective-permute-done.27 = bf16[256,1024]{1,0:T(8,128)(2,1)} collective-permute-done((bf16[256,1024]{1,0:T(8,128)(2,1)}, bf16[256,1024]{1,0:T(8,128)(2,1)}, u32[]{:S(2)}, u32[]{:S(2)}) %collective-permute-start.27) | collective-permute-done | bytes 524320 | tf_op jit(solution)/shard_map/ppermute | solution.py:534
  488.9 4.8 place_half.5
  493.7 3.3 maximum_select_fusion.3
  496.9 3.2 maximum_select_fusion.4
  500.2 2.6 pad_maximum_fusion.1.rows_ref
  504.5 2.1 dynamic-slice_convert_fusion
  510.3 4.7 place_half.6.refs_0_
  515.0 6.2 %collective-permute-done.29 = bf16[256,1024]{1,0:T(8,128)(2,1)} collective-permute-done((bf16[256,1024]{1,0:T(8,128)(2,1)}, bf16[256,1024]{1,0:T(8,128)(2,1)}, u32[]{:S(2)}, u32[]{:S(2)}) %collective-permute-start.29) | collective-permute-done | bytes 524320 | tf_op jit(solution)/shard_map/ppermute | solution.py:534
  524.0 4.9 place_half.7
  (202 shorter events, 64.7 us)
Async XLA Ops:
  7.2 87.3 %all-gather.4.cloned.1.call-start = ((), (), s32[]{:S(2)}) async-start(), calls=%async_computation.3 | async-start | bytes 5242880 | tf_op jit(solution)/shard_map/all_gather | solution.py:649
  10.8 164.4 %all-gather.6.cloned.1.call-start = ((), (), s32[]{:S(2)}) async-start(), calls=%async_computation.4 | async-start | bytes 5242880 | tf_op jit(solution)/shard_map/all_gather | solution.py:650
  12.0 244.1 %all-gather.8.cloned.1.call-start = ((), (), s32[]{:S(2)}) async-start(), calls=%async_computation.5 | async-start | bytes 5242880 | tf_op jit(solution)/shard_map/all_gather | solution.py:651
  14.7 349.4 %reduce-scatter.4.cloned.1.call-start = ((), (), s32[]{:S(2)}) async-start(), calls=%async_computation.6 | async-start | bytes 5242880 | tf_op jit(solution)/shard_map/reduce_scatter | solution.py:687
  153.8 262.3 %reduce-scatter.6.cloned.1.call-start = ((), (), s32[]{:S(2)}) async-start(), calls=%async_computation.7 | async-start | bytes 5242880 | tf_op jit(solution)/shard_map/reduce_scatter | solution.py:687
  266.2 10.2 %collective-permute-start = (bf16[1024,2048]{1,0:T(8,128)(2,1)}, bf16[1024,2048]{1,0:T(8,128)(2,1)}, u32[]{:S(2)}, u32[]{:S(2)}) collective-permute-start(bf16[1024,2048]{1,0:T(8,128)(2,1)} %branch_half.2), channel_id=1, source_target_pairs={{0,4},{4,0},{8,12},{12,8},{1,5},{5,1},{9,13},{13,9},{2,6},{6,2},{1... | collective-permute-start | bytes 12582920 | tf_op jit(solution)/shard_map/ppermute | solution.py:526
  266.2 238.3 %reduce-scatter.8.cloned.1.call-start = ((), (), s32[]{:S(2)}) async-start(), calls=%async_computation.8 | async-start | bytes 5242880 | tf_op jit(solution)/shard_map/reduce_scatter | solution.py:687
  279.5 25.6 %collective-permute-start.2 = (bf16[256,2048]{1,0:T(8,128)(2,1)S(1)}, bf16[256,2048]{1,0:T(8,128)(2,1)S(1)}, u32[]{:S(2)}, u32[]{:S(2)}) collective-permute-start(bf16[256,2048]{1,0:T(8,128)(2,1)S(1)} %get-tuple-element.178), channel_id=1, source_target_pairs={{0,16},{16,0},{1,17},{17,1},{2,18},{18,2},{3,19},{19,3},{4,20},{20... | collective-permute-start | bytes 3145736 | tf_op jit(solution)/shard_map/ppermute | solution.py:534
  281.1 25.4 %collective-permute-start.1 = (bf16[256,2048]{1,0:T(8,128)(2,1)S(1)}, bf16[256,2048]{1,0:T(8,128)(2,1)}, u32[]{:S(2)}, u32[]{:S(2)}) collective-permute-start(bf16[256,2048]{1,0:T(8,128)(2,1)S(1)} %get-tuple-element.179), channel_id=1, source_target_pairs={{0,8},{8,0},{4,12},{12,4},{1,9},{9,1},{5,13},{13,5},{2,10},{10,2},... | collective-permute-start | bytes 3145736 | tf_op jit(solution)/shard_map/ppermute | solution.py:530
  305.1 15.9 %copy-start.10 = (bf16[256,2048]{1,0:T(8,128)(2,1)}, bf16[256,2048]{1,0:T(8,128)(2,1)S(1)}, u32[]{:S(2)}) copy-start(bf16[256,2048]{1,0:T(8,128)(2,1)S(1)} %collective-permute-done.2) | copy-start | bytes 3145732
  308.6 12.5 %copy-start.18 = (f32[2048]{0:T(1024)S(1)}, f32[2048]{0:T(1024)}, u32[]{:S(2)}) copy-start(f32[2048]{0:T(1024)} %param.24) | copy-start | bytes 24580
  308.7 12.5 %copy-start.19 = (f32[2048]{0:T(1024)S(1)}, f32[2048]{0:T(1024)}, u32[]{:S(2)}) copy-start(f32[2048]{0:T(1024)} %param.30) | copy-start | bytes 24580
  308.7 12.6 %copy-start.26 = (f32[1,768]{1,0:T(1,128)S(1)}, f32[1,768]{1,0:T(1,128)}, u32[]{:S(2)}) copy-start(f32[1,768]{1,0:T(1,128)} %get-tuple-element.100) | copy-start | bytes 9220
  308.7 12.6 %copy-start.24 = (f32[1,2048]{1,0:T(1,128)S(1)}, f32[1,2048]{1,0:T(1,128)}, u32[]{:S(2)}) copy-start(f32[1,2048]{1,0:T(1,128)} %get-tuple-element.94) | copy-start | bytes 24580
  308.7 12.7 %copy-start.23 = (f32[1,2048]{1,0:T(1,128)S(1)}, f32[1,2048]{1,0:T(1,128)}, u32[]{:S(2)}) copy-start(f32[1,2048]{1,0:T(1,128)} %get-tuple-element.95) | copy-start | bytes 24580
  321.1 16.4 %collective-permute-start.5 = (bf16[1024,2048]{1,0:T(8,128)(2,1)}, bf16[1024,2048]{1,0:T(8,128)(2,1)}, u32[]{:S(2)}, u32[]{:S(2)}) collective-permute-start(bf16[1024,2048]{1,0:T(8,128)(2,1)} %get-tuple-element.88), channel_id=1, source_target_pairs={{0,4},{4,0},{8,12},{12,8},{1,5},{5,1},{9,13},{13,9},{2,6},{6,2},{1... | collective-permute-start | bytes 12582920 | tf_op jit(solution)/shard_map/ppermute | solution.py:526
  321.4 14.5 %copy-start.21 = (f32[1,2048]{1,0:T(1,128)S(1)}, f32[1,2048]{1,0:T(1,128)}, u32[]{:S(2)}) copy-start(f32[1,2048]{1,0:T(1,128)} %get-tuple-element.96) | copy-start | bytes 24580
  321.4 15.3 %copy-start.20 = (f32[1,2048]{1,0:T(1,128)S(1)}, f32[1,2048]{1,0:T(1,128)}, u32[]{:S(2)}) copy-start(f32[1,2048]{1,0:T(1,128)} %get-tuple-element.98) | copy-start | bytes 24580
  321.4 23.0 %collective-permute-start.4 = (bf16[128,2048]{1,0:T(8,128)(2,1)S(1)}, bf16[128,2048]{1,0:T(8,128)(2,1)S(1)}, u32[]{:S(2)}, u32[]{:S(2)}) collective-permute-start(bf16[128,2048]{1,0:T(8,128)(2,1)S(1)} %get-tuple-element.176), channel_id=1, source_target_pairs={{0,8},{8,0},{4,12},{12,4},{1,9},{9,1},{5,13},{13,5},{2,10},{10,2},... | collective-permute-start | bytes 1572872 | tf_op jit(solution)/shard_map/ppermute | solution.py:530
  323.0 21.6 %collective-permute-start.3 = (bf16[128,2048]{1,0:T(8,128)(2,1)S(1)}, bf16[128,2048]{1,0:T(8,128)(2,1)S(1)}, u32[]{:S(2)}, u32[]{:S(2)}) collective-permute-start(bf16[128,2048]{1,0:T(8,128)(2,1)S(1)} %get-tuple-element.177), channel_id=1, source_target_pairs={{0,16},{16,0},{1,17},{17,1},{2,18},{18,2},{3,19},{19,3},{4,20},{20... | collective-permute-start | bytes 1572872 | tf_op jit(solution)/shard_map/ppermute | solution.py:534
  335.9 10.6 %copy-start.11 = (bf16[256,2048]{1,0:T(8,128)(2,1)S(1)}, bf16[256,2048]{1,0:T(8,128)(2,1)}, u32[]{:S(2)}) copy-start(bf16[256,2048]{1,0:T(8,128)(2,1)} %copy-done.10) | copy-start | bytes 3145732
  341.5 28.8 %collective-permute-start.15 = (bf16[256,2048]{1,0:T(8,128)(2,1)}, bf16[256,2048]{1,0:T(8,128)(2,1)}, u32[]{:S(2)}, u32[]{:S(2)}) collective-permute-start(bf16[256,2048]{1,0:T(8,128)(2,1)} %get-tuple-element.174), channel_id=1, source_target_pairs={{0,16},{16,0},{1,17},{17,1},{2,18},{18,2},{3,19},{19,3},{4,20},{20... | collective-permute-start | bytes 3145736 | tf_op jit(solution)/shard_map/ppermute | solution.py:534
  342.9 28.0 %collective-permute-start.14 = (bf16[256,2048]{1,0:T(8,128)(2,1)S(1)}, bf16[256,2048]{1,0:T(8,128)(2,1)}, u32[]{:S(2)}, u32[]{:S(2)}) collective-permute-start(bf16[256,2048]{1,0:T(8,128)(2,1)S(1)} %get-tuple-element.175), channel_id=1, source_target_pairs={{0,8},{8,0},{4,12},{12,4},{1,9},{9,1},{5,13},{13,5},{2,10},{10,2},... | collective-permute-start | bytes 3145736 | tf_op jit(solution)/shard_map/ppermute | solution.py:530
  343.4 23.1 %collective-permute-start.10 = (f32[94,128]{1,0:T(8,128)S(1)}, f32[94,128]{1,0:T(8,128)S(1)}, u32[]{:S(2)}, u32[]{:S(2)}) collective-permute-start(f32[94,128]{1,0:T(8,128)S(1)} %bitcast.51), channel_id=1, source_target_pairs={{0,3},{1,0},{2,1},{3,2},{4,7},{5,4},{6,5},{7,6},{8,11},{9,8},{10,9... | collective-permute-start | bytes 144392 | tf_op jit(solution)/shard_map/ppermute | solution.py:761
  344.4 23.7 %collective-permute-start.9 = (f32[94,128]{1,0:T(8,128)S(1)}, f32[94,128]{1,0:T(8,128)S(1)}, u32[]{:S(2)}, u32[]{:S(2)}) collective-permute-start(f32[94,128]{1,0:T(8,128)S(1)} %bitcast.52), channel_id=1, source_target_pairs={{0,2},{1,3},{2,0},{3,1},{4,6},{5,7},{6,4},{7,5},{8,10},{9,11},{10,... | collective-permute-start | bytes 144392 | tf_op jit(solution)/shard_map/ppermute | solution.py:761
  344.5 24.1 %collective-permute-start.8 = (f32[94,128]{1,0:T(8,128)S(1)}, f32[94,128]{1,0:T(8,128)S(1)}, u32[]{:S(2)}, u32[]{:S(2)}) collective-permute-start(f32[94,128]{1,0:T(8,128)S(1)} %bitcast.53), channel_id=1, source_target_pairs={{0,1},{1,2},{2,3},{3,0},{4,5},{5,6},{6,7},{7,4},{8,9},{9,10},{10,1... | collective-permute-start | bytes 144392 | tf_op jit(solution)/shard_map/ppermute | solution.py:761
  366.6 26.0 %collective-permute-start.7 = (bf16[128,2048]{1,0:T(8,128)(2,1)S(1)}, bf16[128,2048]{1,0:T(8,128)(2,1)S(1)}, u32[]{:S(2)}, u32[]{:S(2)}) collective-permute-start(bf16[128,2048]{1,0:T(8,128)(2,1)S(1)} %get-tuple-element.166), channel_id=1, source_target_pairs={{0,8},{8,0},{4,12},{12,4},{1,9},{9,1},{5,13},{13,5},{2,10},{10,2},... | collective-permute-start | bytes 1572872 | tf_op jit(solution)/shard_map/ppermute | solution.py:530
  368.1 24.6 %collective-permute-start.6 = (bf16[128,2048]{1,0:T(8,128)(2,1)S(1)}, bf16[128,2048]{1,0:T(8,128)(2,1)}, u32[]{:S(2)}, u32[]{:S(2)}) collective-permute-start(bf16[128,2048]{1,0:T(8,128)(2,1)S(1)} %get-tuple-element.167), channel_id=1, source_target_pairs={{0,16},{16,0},{1,17},{17,1},{2,18},{18,2},{3,19},{19,3},{4,20},{20... | collective-permute-start | bytes 1572872 | tf_op jit(solution)/shard_map/ppermute | solution.py:534
  368.7 24.0 %collective-permute-start.13 = (bf16[256,1024]{1,0:T(8,128)(2,1)}, bf16[256,1024]{1,0:T(8,128)(2,1)S(1)}, u32[]{:S(2)}, u32[]{:S(2)}) collective-permute-start(bf16[256,1024]{1,0:T(8,128)(2,1)} %get-tuple-element.187), channel_id=1, source_target_pairs={{0,16},{16,0},{1,17},{17,1},{2,18},{18,2},{3,19},{19,3},{4,20},{20... | collective-permute-start | bytes 1572872 | tf_op jit(solution)/shard_map/ppermute | solution.py:534
  370.2 21.2 %collective-permute-start.12 = (f32[14,128]{1,0:T(8,128)S(1)}, f32[14,128]{1,0:T(8,128)S(1)}, u32[]{:S(2)}, u32[]{:S(2)}) collective-permute-start(f32[14,128]{1,0:T(8,128)S(1)} %slice.88), channel_id=1, source_target_pairs={{0,16},{16,0},{1,17},{17,1},{2,18},{18,2},{3,19},{19,3},{4,20},{20... | collective-permute-start | bytes 21512 | tf_op jit(solution)/shard_map/ppermute | solution.py:534
  370.9 21.2 %collective-permute-start.11 = (f32[64,128]{1,0:T(8,128)S(1)}, f32[64,128]{1,0:T(8,128)S(1)}, u32[]{:S(2)}, u32[]{:S(2)}) collective-permute-start(f32[64,128]{1,0:T(8,128)S(1)} %slice.87), channel_id=1, source_target_pairs={{0,4},{4,0},{8,12},{12,8},{1,5},{5,1},{9,13},{13,9},{2,6},{6,2},{1... | collective-permute-start | bytes 98312 | tf_op jit(solution)/shard_map/ppermute | solution.py:526
  391.5 15.5 %collective-permute-start.19 = (bf16[128,2048]{1,0:T(8,128)(2,1)S(1)}, bf16[128,2048]{1,0:T(8,128)(2,1)S(1)}, u32[]{:S(2)}, u32[]{:S(2)}) collective-permute-start(bf16[128,2048]{1,0:T(8,128)(2,1)S(1)} %get-tuple-element.172), channel_id=1, source_target_pairs={{0,8},{8,0},{4,12},{12,4},{1,9},{9,1},{5,13},{13,5},{2,10},{10,2},... | collective-permute-start | bytes 1572872 | tf_op jit(solution)/shard_map/ppermute | solution.py:530
  392.1 14.9 %collective-permute-start.18 = (bf16[128,2048]{1,0:T(8,128)(2,1)S(1)}, bf16[128,2048]{1,0:T(8,128)(2,1)S(1)}, u32[]{:S(2)}, u32[]{:S(2)}) collective-permute-start(bf16[128,2048]{1,0:T(8,128)(2,1)S(1)} %get-tuple-element.173), channel_id=1, source_target_pairs={{0,16},{16,0},{1,17},{17,1},{2,18},{18,2},{3,19},{19,3},{4,20},{20... | collective-permute-start | bytes 1572872 | tf_op jit(solution)/shard_map/ppermute | solution.py:534
  392.7 14.3 %collective-permute-start.20 = (f32[64,128]{1,0:T(8,128)S(1)}, f32[64,128]{1,0:T(8,128)S(1)}, u32[]{:S(2)}, u32[]{:S(2)}) collective-permute-start(f32[64,128]{1,0:T(8,128)S(1)} %slice_add_fusion), channel_id=1, source_target_pairs={{0,8},{8,0},{4,12},{12,4},{1,9},{9,1},{5,13},{13,5},{2,10},{10,2},... | collective-permute-start | bytes 98312 | tf_op jit(solution)/shard_map/ppermute | solution.py:530
  394.4 31.9 %collective-permute-start.17 = (bf16[256,2048]{1,0:T(8,128)(2,1)S(1)}, bf16[256,2048]{1,0:T(8,128)(2,1)}, u32[]{:S(2)}, u32[]{:S(2)}) collective-permute-start(bf16[256,2048]{1,0:T(8,128)(2,1)S(1)} %maximum_select_fusion.8), channel_id=1, source_target_pairs={{0,16},{16,0},{1,17},{17,1},{2,18},{18,2},{3,19},{19,3},{4,20},{20... | collective-permute-start | bytes 3145736 | tf_op jit(solution)/shard_map/ppermute | solution.py:534
  397.5 16.6 %copy-start.2 = (bf16[256,2048]{1,0:T(8,128)(2,1)}, bf16[256,2048]{1,0:T(8,128)(2,1)S(1)}, u32[]{:S(2)}) copy-start(bf16[256,2048]{1,0:T(8,128)(2,1)S(1)} %maximum_select_fusion.7) | copy-start | bytes 3145732
  397.6 28.7 %collective-permute-start.16 = (bf16[256,2048]{1,0:T(8,128)(2,1)S(1)}, bf16[256,2048]{1,0:T(8,128)(2,1)}, u32[]{:S(2)}, u32[]{:S(2)}) collective-permute-start(bf16[256,2048]{1,0:T(8,128)(2,1)S(1)} %maximum_select_fusion.7), channel_id=1, source_target_pairs={{0,8},{8,0},{4,12},{12,4},{1,9},{9,1},{5,13},{13,5},{2,10},{10,2},... | collective-permute-start | bytes 3145736 | tf_op jit(solution)/shard_map/ppermute | solution.py:530
  410.2 16.0 %collective-permute-start.21 = (f32[64,128]{1,0:T(8,128)S(1)}, f32[64,128]{1,0:T(8,128)S(1)}, u32[]{:S(2)}, u32[]{:S(2)}) collective-permute-start(f32[64,128]{1,0:T(8,128)S(1)} %add.389), channel_id=1, source_target_pairs={{0,16},{16,0},{1,17},{17,1},{2,18},{18,2},{3,19},{19,3},{4,20},{20... | collective-permute-start | bytes 98312 | tf_op jit(solution)/shard_map/ppermute | solution.py:534
  434.8 19.2 %copy-start.9 = (bf16[512,1024]{1,0:T(8,128)(2,1)S(1)}, bf16[512,1024]{1,0:T(8,128)(2,1)}, u32[]{:S(2)}) copy-start(bf16[512,1024]{1,0:T(8,128)(2,1)} %reduce-scatter.6.cloned.1.call-done) | copy-start | bytes 3145732
  434.8 54.1 %collective-permute-start.22 = (bf16[1024,2048]{1,0:T(8,128)(2,1)}, bf16[1024,2048]{1,0:T(8,128)(2,1)}, u32[]{:S(2)}, u32[]{:S(2)}) collective-permute-start(bf16[1024,2048]{1,0:T(8,128)(2,1)} %pad_maximum_fusion.rows_ref), channel_id=1, source_target_pairs={{0,4},{4,0},{8,12},{12,8},{1,5},{5,1},{9,13},{13,9},{2,6},{6,2},{1... | collective-permute-start | bytes 12582920 | tf_op jit(solution)/shard_map/ppermute | solution.py:526
  434.8 14.3 %collective-permute-start.24 = (bf16[128,2048]{1,0:T(8,128)(2,1)S(1)}, bf16[128,2048]{1,0:T(8,128)(2,1)S(1)}, u32[]{:S(2)}, u32[]{:S(2)}) collective-permute-start(bf16[128,2048]{1,0:T(8,128)(2,1)S(1)} %copy-done.7), channel_id=1, source_target_pairs={{0,8},{8,0},{4,12},{12,4},{1,9},{9,1},{5,13},{13,5},{2,10},{10,2},... | collective-permute-start | bytes 1572872 | tf_op jit(solution)/shard_map/ppermute | solution.py:530
  436.2 14.0 %collective-permute-start.23 = (bf16[128,2048]{1,0:T(8,128)(2,1)S(1)}, bf16[128,2048]{1,0:T(8,128)(2,1)S(1)}, u32[]{:S(2)}, u32[]{:S(2)}) collective-permute-start(bf16[128,2048]{1,0:T(8,128)(2,1)S(1)} %copy-done.6), channel_id=1, source_target_pairs={{0,16},{16,0},{1,17},{17,1},{2,18},{18,2},{3,19},{19,3},{4,20},{20... | collective-permute-start | bytes 1572872 | tf_op jit(solution)/shard_map/ppermute | solution.py:534
  451.4 42.2 %collective-permute-start.26 = (bf16[256,2048]{1,0:T(8,128)(2,1)}, bf16[256,2048]{1,0:T(8,128)(2,1)}, u32[]{:S(2)}, u32[]{:S(2)}) collective-permute-start(bf16[256,2048]{1,0:T(8,128)(2,1)} %maximum_select_fusion.10), channel_id=1, source_target_pairs={{0,16},{16,0},{1,17},{17,1},{2,18},{18,2},{3,19},{19,3},{4,20},{20... | collective-permute-start | bytes 3145736 | tf_op jit(solution)/shard_map/ppermute | solution.py:534
  453.4 40.3 %collective-permute-start.25 = (bf16[256,2048]{1,0:T(8,128)(2,1)}, bf16[256,2048]{1,0:T(8,128)(2,1)}, u32[]{:S(2)}, u32[]{:S(2)}) collective-permute-start(bf16[256,2048]{1,0:T(8,128)(2,1)} %maximum_select_fusion.9), channel_id=1, source_target_pairs={{0,8},{8,0},{4,12},{12,4},{1,9},{9,1},{5,13},{13,5},{2,10},{10,2},... | collective-permute-start | bytes 3145736 | tf_op jit(solution)/shard_map/ppermute | solution.py:530
  454.9 32.6 %collective-permute-start.27 = (bf16[256,1024]{1,0:T(8,128)(2,1)}, bf16[256,1024]{1,0:T(8,128)(2,1)}, u32[]{:S(2)}, u32[]{:S(2)}) collective-permute-start(bf16[256,1024]{1,0:T(8,128)(2,1)} %get-tuple-element.185), channel_id=1, source_target_pairs={{0,16},{16,0},{1,17},{17,1},{2,18},{18,2},{3,19},{19,3},{4,20},{20... | collective-permute-start | bytes 1572872 | tf_op jit(solution)/shard_map/ppermute | solution.py:534
  502.8 21.2 %collective-permute-start.28 = (bf16[1024,2048]{1,0:T(8,128)(2,1)}, bf16[1024,2048]{1,0:T(8,128)(2,1)}, u32[]{:S(2)}, u32[]{:S(2)}) collective-permute-start(bf16[1024,2048]{1,0:T(8,128)(2,1)} %pad_maximum_fusion.1.rows_ref), channel_id=1, source_target_pairs={{0,4},{4,0},{8,12},{12,8},{1,5},{5,1},{9,13},{13,9},{2,6},{6,2},{1... | collective-permute-start | bytes 12582920 | tf_op jit(solution)/shard_map/ppermute | solution.py:526
  502.8 26.0 %copy-start.15 = (f32[2048]{0:T(1024)}, f32[2048]{0:T(1024)S(1)}, u32[]{:S(2)}) copy-start(f32[2048]{0:T(1024)S(1)} %slice_bitcast_fusion.4) | copy-start | bytes 24580
  506.6 14.6 %collective-permute-start.29 = (bf16[256,1024]{1,0:T(8,128)(2,1)}, bf16[256,1024]{1,0:T(8,128)(2,1)}, u32[]{:S(2)}, u32[]{:S(2)}) collective-permute-start(bf16[256,1024]{1,0:T(8,128)(2,1)} %get-tuple-element.183), channel_id=1, source_target_pairs={{0,16},{16,0},{1,17},{17,1},{2,18},{18,2},{3,19},{19,3},{4,20},{20... | collective-permute-start | bytes 1572872 | tf_op jit(solution)/shard_map/ppermute | solution.py:534
  (17 other events, 84.3 us)
Sparse Core Ops, SparseCore 0:
  11.0 83.4 all-gather.3
  96.0 79.2 all-gather.5
  176.9 79.2 all-gather.7
  258.3 75.2 reduce-scatter.3
  335.7 80.4 reduce-scatter.5
  418.3 77.2 reduce-scatter.7

commit v4 on v3

--- a/solution.py
+++ b/solution.py
@@ -681,20 +681,24 @@
     qkv_grad, qkv_bias_part = attend_back(
         qkv, attended_grad, log_total, key_bias, cos_table.T, sin_table.T
     )
-    heads_partial = weight_grad([(normed1, qkv_grad), (grad_rows, attended)], count)
-
     def scatter(partial_sum):
         return lax.psum_scatter(partial_sum, "dp", scatter_dimension=0, tiled=True)
 
-    heads_total = scatter(heads_partial)
     input_part, dot1, sum1 = dgrad_first(
-        after(qkv_grad, heads_partial), heads_full, tokens, mean, inv_std, ln1_gain[None]
+        qkv_grad, heads_full, tokens, mean, inv_std, ln1_gain[None]
     )
     activated, slope = up_gelu(
         after(normed2, input_part), up_full, pick(up_bias, ex, units)[None]
     )
-    down_partial = weight_grad([(after(grad_rows, activated), activated)], count)
-    down_total = scatter(down_partial)
+    down_partial = weight_grad(
+        [
+            (normed1, after(qkv_grad, activated)),
+            (grad_rows, attended),
+            (after(grad_rows, activated), activated),
+        ],
+        count,
+    )
+    first_total = scatter(down_partial)
 
     shift_sum = out_bias + down_bias
     tokens_own = own_rows(tokens, core, why, ex)
@@ -763,61 +767,59 @@
     ]
     up_partial = weight_grad([(after(normed2, vectors, *output_one), hidden_grad)], count)
     up_total = scatter(up_partial)
-    hops = after(hops, up_partial)
-    vectors = sum(hops, vectors)
+    input_two_got = after(input_two_got, up_partial)
+    input_mine, input_three = halving_more(input_keep, input_core, input_two_got, why, ex)
+    input_three_got = x_swap(input_three[0]), y_swap(input_three[1])
+    output_got, hops = after((output_got, hops), *input_three)
+    output_two, output_got = gather_two(*output_one, output_got, why, ex)
+    vectors = sum(after(hops, *output_two), vectors)
     norm_count, bias_rows = 4 * width // LANES, width // LANES
     norms, bias_grad, biases = (
         vectors[:norm_count],
         vectors[norm_count : norm_count + bias_rows].reshape(width),
         vectors[norm_count + bias_rows :],
     )
-
-    def share(total):
-        mine, given = pick(total, ex, chunk), pick(total, 1 - ex, chunk)
-        return mine.astype(F32), x_swap(given.astype(BF16))
-
-    heads_mine, heads_other = share(after(heads_total, up_partial))
     norms_other, biases_other = core_swap(norms), x_swap(biases)
-    input_two_got = after(input_two_got, up_partial, norms)
-    input_mine, input_three = halving_more(input_keep, input_core, input_two_got, why, ex)
-    input_three_got = x_swap(input_three[0]), y_swap(input_three[1])
-    output_got, norms_other, biases_other, heads_other = after(
-        (output_got, norms_other, biases_other, heads_other), *input_three
-    )
-    output_two, output_got = gather_two(*output_one, output_got, why, ex)
-    norms = norms + norms_other
-    norms_other = y_swap(norms)
-    input_three_got, norms_other = after(
-        (input_three_got, norms_other), norms, *output_two
-    )
+    input_three_got = after(input_three_got, norms, *output_two)
     input_one = [input_of(at, input_mine[at] + input_three_got[at].astype(F32)) for at in range(2)]
     input_got = gather_one(*input_one)
+    norms, biases_other = after((norms + norms_other, biases_other), *input_one)
+    norms_other = y_swap(norms)
+    output_got = after(output_got, norms, *input_one)
+    output_mine, output_other = gather_last(output_two, output_got, core, why, ex)
+    input_got, norms_other = after((input_got, norms_other), output_mine)
     norms = norms + norms_other
     norms_other = x_swap(norms)
-    output_got, norms_other, down_total = after(
-        (output_got, norms_other, down_total), norms, *input_one
-    )
-    output_mine, output_other = gather_last(output_two, output_got, core, why, ex)
-    down_mine, down_other = share(down_total)
-    input_got = after(input_got, output_mine)
+    input_got = after(input_got, norms)
     input_two, input_got = gather_two(*input_one, input_got, why, ex)
-    norms = (norms + norms_other).reshape(4, width)
+    def halves(total):
+        return pick(total, ex, chunk).astype(F32), pick(total, 1 - ex, chunk)
+
+    def share(total):
+        mine, given = halves(total)
+        return mine, x_swap(given)
+
+    first_mine, first_other = share(after(first_total, *input_two))
+    output_half = place_half(core, after(output_mine, *input_two))
+    output_rows = place_half(1 - core, after(output_other, output_half), output_half)
     biases, other = biases.reshape(-1), biases_other.reshape(-1)
     qkv_bias_grad = join(ex, biases[:qkv_cols], other[:qkv_cols])
     up_bias_grad = join(ex, biases[qkv_cols:], other[qkv_cols:])
-    other = heads_other.astype(F32)
+    input_got, norms_other = after((input_got, norms_other), output_rows)
+    norms = (norms + norms_other).reshape(4, width)
+    input_mine, input_other = gather_last(input_two, input_got, core, why, ex)
+    up_mine, up_given = halves(after(up_total, input_mine))
+    up_other = x_swap(up_given)
+    first_other = after(first_other, up_given)
+    heads_mine, down_mine = first_mine[:, :-units], first_mine[:, -units:]
+    other, down_other = first_other[:, :-units].astype(F32), first_other[:, -units:].astype(F32)
     qkv_out = join(ex, heads_mine[:, :qkv_cols], other[:, :qkv_cols], 1)
     out_out = join(ex, heads_mine[:, qkv_cols:].T, other[:, qkv_cols:].T, 0)
-    down_out = join(ex, down_mine.T, down_other.T.astype(F32), 0)
-    output_rows = place_half(
-        1 - core, output_other, place_half(core, after(output_mine, *input_two))
-    )
-    input_got = after(input_got, output_rows, norms, qkv_out, out_out, down_out)
-    input_mine, input_other = gather_last(input_two, input_got, core, why, ex)
-    up_mine, up_other = share(after(up_total, input_mine))
-    grad_half = place_half(core, input_mine)
+    down_out = join(ex, down_mine.T, down_other.T, 0)
+    grad_half = place_half(core, after(input_mine, norms, up_given))
+    grad_input = place_half(1 - core, after(input_other, grad_half), grad_half)
+    up_other = after(up_other, qkv_out, out_out, down_out, grad_input)
     up_out = join(ex, up_mine, up_other.astype(F32), 1)
-    grad_input = place_half(1 - core, after(input_other, up_out), grad_half)
 
     return (
         output_rows,

time: 543 us -> 524 us (0.965)
  other arithmetic: 99 us -> 86.9 us
  waiting for transfers between devices: 179 us -> 173 us
    ppermute x13 -> x12, waiting for transfers between devices: 66.7 us -> 41.4 us  [x_swap(): return lax.ppermute(block, 'branch', XAX)]
    all_gather x1, waiting for transfers between devices: 0.22 us -> 19.9 us  [local(): up_full = lax.all_gather(up_shard, 'dp', axis=0, tiled=True)]
    all_gather x1, waiting for transfers between devices: 49.2 us -> 38.2 us  [local(): down_full = lax.all_gather(down_shard, 'dp', axis=0, tiled=True)]
    reduce_sum x1 -> x0, other arithmetic: 8.71 us -> none  [local(): jnp.sum(grad_rows, axis=0, dtype=F32)]
    reduce_scatter x3 -> x2, waiting for transfers between devices: 2.04 us -> 10.1 us  [scatter(): return lax.psum_scatter(partial_sum, 'dp', scatter_dimension=0, tiled=True)]
    select_n x14, other arithmetic: 21.9 us -> 14.4 us  [join(): jnp.where(low_index == 0, jnp.concatenate([mine, other], axis), jnp.conca...]
    pallas_call x3 -> x2, Pallas kernels: 44.3 us -> 39.4 us  [weight_grad(): pl.pallas_call(partial(weight_grad_kernel, pairs=len(pairs)), grid=(2 * c...]
    ppermute x13 -> x12, starting transfers between devices: 12.3 us -> 13.3 us  [x_swap(): return lax.ppermute(block, 'branch', XAX)]
  transfers between devices with their start and end apart: 36 -> 34, of which waited for: 13 -> 16; matrix products, arithmetic and copies ran while one was open for 22% -> 21% of each run, Pallas kernels for 35% -> 37%
where the time goes in v4:
time: 524 us; the launch traced here: 518 us
  Pallas kernels  189 us (36%)
  waiting for transfers between devices  173 us (33%)
  other arithmetic  86.9 us (17%)
  starting transfers between devices  25.1 us (5%)
  local copies, waits for them, and re-layouts  21.3 us (4%)
  between operations  15.4 us (3%)
  matrix products  6.97 us (1%)
    ppermute x12, waiting for transfers between devices, x_swap(): return lax.ppermute(block, 'branch', XAX)  41.4 us
    pallas_call x2, Pallas kernels, weight_grad(): pl.pallas_call(partial(weight_grad_kernel, pairs=len(pairs)), grid=(2 * c...  39.4 us
    all_gather x1, waiting for transfers between devices, local(): heads_full = lax.all_gather(heads_shard, 'dp', axis=0, tiled=True)  38.8 us
    all_gather x1, waiting for transfers between devices, local(): down_full = lax.all_gather(down_shard, 'dp', axis=0, tiled=True)  38.2 us
    pallas_call x2, Pallas kernels, dgrad_half(): pl.pallas_call(partial(dgrad_half_kernel, chunk=chunk), grid_spec=pltpu.P...  24.8 us
    ppermute x9, waiting for transfers between devices, y_swap(): return lax.ppermute(block, 'tensor', YAX)  22.8 us
    pallas_call x2, Pallas kernels, branch_half(): pl.pallas_call(partial(branch_kernel, chunk=chunk), grid_spec=pltpu.Prefe...  20.3 us
    all_gather x1, waiting for transfers between devices, local(): up_full = lax.all_gather(up_shard, 'dp', axis=0, tiled=True)  19.9 us
  transfers between devices with their start and end apart: 34, of which 16 were waited for; matrix products, arithmetic and copies ran while one was open for 21% of the time, Pallas kernels for 37%

profile of v4, /device:TPU:0, one launch (start us, length us, event | category | flops | bytes accessed | tf_op | source)
XLA Modules:
  0.0 518.1 jit_solution(17633516654400519542)
XLA Ops:
  16.2 4.5 convert_reduce_fusion
  20.8 6.4 %fusion.8 = f32[2048]{0:T(1024)S(1)} fusion(bf16[2048,2048]{1,0:T(8,128)(2,1)} %rows_ref.5, f32[2048]{0:T(1024)S(1)} %broadcast_multiply_fusion.1), kind=kLoop, calls=%fused_computation.10 | loop fusion | flops 16775168 | bytes 8404992 | tf_op jit(solution)/shard_map/reduce_sum | solution.py:662
  30.5 2.0 fusion.31
  32.5 3.9 fusion.28
  36.5 2.5 maximum_maximum_fusion.2
  39.1 16.5 %fusion.7 = (bf16[2048,2048]{1,0:T(8,128)(2,1)}, bf16[2048,2048]{1,0:T(8,128)(2,1)}, f32[2048]{0:T(1024)S(1)}, bf16[2048,2048]{1,0:T(8,128)(2,1)}) fusion(bf16[2048,2048]{1,0:T(8,128)(2,1)} %rows_ref.5, f32[2048]{0:T(1024)S(1)} %copy-done.16, f32[2048]{0:T(1024)S(1)} %copy-done.13, f32[2048]{0:T(1024)S(1)} %add_rsqrt_fusion, ...), kind=kLoop, calls=%fused_computation.9 | loop fusion | flops 50329600 | bytes 42004480 | tf_op jit(solution)/shard_map/convert_element_type | solution.py:666
  55.6 38.8 %all-gather.4.cloned.1.call-done.weight_ref.out_ref_w = bf16[2048,1024]{1,0:T(8,128)(2,1)} async-done(((bf16[512,1024]{1,0:T(8,128)(2,1)}), bf16[2048,1024]{1,0:T(8,128)(2,1)}) %all-gather.4.cloned.1.call-update) | async-done | bytes 4194320 | tf_op jit(solution)/shard_map/all_gather | solution.py:649
  94.4 11.8 %project.1.query_ref.key_ref.value_ref = bf16[2048,768]{1,0:T(8,128)(2,1)} custom-call(bf16[2048,2048]{1,0:T(8,128)(2,1)} %get-tuple-element.185.rows_ref.refs_0_, bf16[2048,1024]{1,0:T(8,128)(2,1)} %all-gather.4.cloned.1.call-done.weight_ref.out_ref_w, f32[1,768]{1,0:T(1,128)} %broadcast_in_dim.22.bias_ref, f32[2048,128]{1,0:T(8,128)} %get-tuple-element.219.cos_ref, ...), custom_call_target="tpu_custom_call" | custom-call | flops 6442450 | bytes 14680 | tf_op jit(solution)/shard_map/project/pallas_call | solution.py:77
  107.6 8.7 %attend.1 = (bf16[2048,256]{1,0:T(8,128)(2,1)}, f32[8,2048]{1,0:T(8,128)}) custom-call(bf16[2048,768]{1,0:T(8,128)(2,1)} %project.1.query_ref.key_ref.value_ref, bf16[2048,768]{1,0:T(8,128)(2,1)} %project.1.query_ref.key_ref.value_ref, bf16[2048,768]{1,0:T(8,128)(2,1)} %project.1.query_ref.key_ref.value_ref, f32[2048,128]{1,0:T(8,128)} %broadcast_in_dim.27.bias_ref), custom_call_target="tpu_custom_call" | custom-call | flops 2684354 | bytes 4194 | tf_op jit(solution)/shard_map/attend/pallas_call | solution.py:140
  116.3 7.0 %convolution_convert_fusion.grad_ref = bf16[2048,256]{1,0:T(8,128)(2,1)} fusion(bf16[2048,2048]{1,0:T(8,128)(2,1)} %get-tuple-element.89.refs_2_.refs_4_.grad_ref, bf16[2048,1024]{1,0:T(8,128)(2,1)} %all-gather.4.cloned.1.call-done.weight_ref.out_ref_w), kind=kOutput, calls=%fused_computation.15 | convolution fusion | flops 2148007936 | bytes 10485760 | tf_op jit(solution)/shard_map/dot_general | solution.py:678
  123.3 14.9 %attend_back.1 = (bf16[2048,768]{1,0:T(8,128)(2,1)}, f32[1,768]{1,0:T(1,128)}) custom-call(bf16[2048,768]{1,0:T(8,128)(2,1)} %project.1.query_ref.key_ref.value_ref, bf16[2048,768]{1,0:T(8,128)(2,1)} %project.1.query_ref.key_ref.value_ref, bf16[2048,768]{1,0:T(8,128)(2,1)} %project.1.query_ref.key_ref.value_ref, ...), custom_call_target="tpu_custom_call" | custom-call | flops 6710886 | bytes 8388 | tf_op jit(solution)/shard_map/attend_back/pallas_call | solution.py:213
  138.2 17.2 %dgrad_first.1 = (f32[2048,2048]{1,0:T(8,128)}, f32[1,2048]{1,0:T(1,128)}, f32[1,2048]{1,0:T(1,128)}) custom-call(bf16[2048,768]{1,0:T(8,128)(2,1)} %get-tuple-element.84.grad_ref.refs_1_, bf16[2048,1024]{1,0:T(8,128)(2,1)} %all-gather.4.cloned.1.call-done.weight_ref.out_ref_w, bf16[2048,2048]{1,0:T(8,128)(2,1)} %rows_ref.5, f32[2048,1]{1,0:T(8,128)} %copy.37.mean_ref, ...), custom_call_target="tpu_custom_call" | custom-call | flops 6442450 | bytes 28311 | tf_op jit(solution)/shard_map/dgrad_first/pallas_call | solution.py:364
  155.4 19.9 %all-gather.6.cloned.1.call-done.weight_ref = bf16[2048,1024]{1,0:T(8,128)(2,1)} async-done(((bf16[512,1024]{1,0:T(8,128)(2,1)}), bf16[2048,1024]{1,0:T(8,128)(2,1)}) %all-gather.6.cloned.1.call-update) | async-done | bytes 4194320 | tf_op jit(solution)/shard_map/all_gather | solution.py:650
  175.3 17.4 %up_gelu.1 = (bf16[2048,1024]{1,0:T(8,128)(2,1)}, f32[2048,1024]{1,0:T(8,128)}) custom-call(bf16[2048,2048]{1,0:T(8,128)(2,1)} %get-tuple-element.109.rows_ref.refs_0_, bf16[2048,1024]{1,0:T(8,128)(2,1)} %all-gather.6.cloned.1.call-done.weight_ref, f32[1,1024]{1,0:T(1,128)} %bitcast.57), custom_call_target="tpu_custom_call" | custom-call | flops 8589934 | bytes 25165 | tf_op jit(solution)/shard_map/up_gelu/pallas_call | solution.py:260
  192.7 25.1 %weight_grad.2 = bf16[2048,2048]{1,0:T(8,128)(2,1)} custom-call(bf16[2048,2048]{1,0:T(8,128)(2,1)} %get-tuple-element.185.rows_ref.refs_0_, bf16[2048,768]{1,0:T(8,128)(2,1)} %get-tuple-element.84.grad_ref.refs_1_, bf16[2048,2048]{1,0:T(8,128)(2,1)} %get-tuple-element.89.refs_2_.refs_4_.grad_ref, bf16[2048,256]{1,0:T(8,128)(2,1)} %get-tuple-element.78.refs_3_.heads_ref, ...), custom_call_target="tpu_custom_call" | custom-call | flops 17179868 | bytes 25165 | tf_op jit(solution)/shard_map/weight_grad/pallas_call | solution.py:481
  217.9 38.2 %all-gather.8.cloned.1.call-done.down_ref.weight_ref = bf16[2048,1024]{1,0:T(8,128)(2,1)} async-done(((bf16[512,1024]{1,0:T(8,128)(2,1)}), bf16[2048,1024]{1,0:T(8,128)(2,1)}) %all-gather.8.cloned.1.call-update) | async-done | bytes 4194320 | tf_op jit(solution)/shard_map/all_gather | solution.py:651
  256.1 10.2 %branch_half.2 = bf16[1024,2048]{1,0:T(8,128)(2,1)} custom-call(s32[1]{0:T(128)} %bitcast.half_ref.core_ref, bf16[2048,256]{1,0:T(8,128)(2,1)} %get-tuple-element.78.refs_3_.heads_ref, bf16[2048,1024]{1,0:T(8,128)(2,1)} %all-gather.4.cloned.1.call-done.weight_ref.out_ref_w, bf16[2048,1024]{1,0:T(8,128)(2,1)} %get-tuple-element.87.refs_5_.act_ref, ...), custom_call_target="tpu_custom_call" | custom-call | flops 5368709 | bytes 10485 | tf_op jit(solution)/shard_map/branch_half/pallas_call | solution.py:434
  266.4 10.1 %branch_half.3 = bf16[1024,2048]{1,0:T(8,128)(2,1)} custom-call(s32[1]{0:T(128)} %bitcast.2.half_ref.core_ref, bf16[2048,256]{1,0:T(8,128)(2,1)} %get-tuple-element.78.refs_3_.heads_ref, bf16[2048,1024]{1,0:T(8,128)(2,1)} %all-gather.4.cloned.1.call-done.weight_ref.out_ref_w, bf16[2048,1024]{1,0:T(8,128)(2,1)} %get-tuple-element.87.refs_5_.act_ref, ...), custom_call_target="tpu_custom_call" | custom-call | flops 5368709 | bytes 10485 | tf_op jit(solution)/shard_map/branch_half/pallas_call | solution.py:434
  276.4 3.1 add_convert_fusion.2
  282.6 15.6 %hidden_back.1 = (bf16[2048,1024]{1,0:T(8,128)(2,1)}, f32[1,1024]{1,0:T(1,128)}) custom-call(bf16[2048,2048]{1,0:T(8,128)(2,1)} %get-tuple-element.89.refs_2_.refs_4_.grad_ref, bf16[2048,1024]{1,0:T(8,128)(2,1)} %all-gather.8.cloned.1.call-done.down_ref.weight_ref, f32[2048,1024]{1,0:T(8,128)} %get-tuple-element.90.slope_ref), custom_call_target="tpu_custom_call" | custom-call | flops 8589934 | bytes 25165 | tf_op jit(solution)/shard_map/hidden_back/pallas_call | solution.py:297
  298.2 7.0 %collective-permute-done.1 = bf16[256,2048]{1,0:T(8,128)(2,1)S(1)} collective-permute-done((bf16[256,2048]{1,0:T(8,128)(2,1)S(1)}, bf16[256,2048]{1,0:T(8,128)(2,1)S(1)}, u32[]{:S(2)}, u32[]{:S(2)}) %collective-permute-start.1) | collective-permute-done | bytes 1048608 | tf_op jit(solution)/shard_map/ppermute | solution.py:530
  306.4 2.2 add_convert_fusion.6
  308.7 12.5 %dgrad_half.2 = (bf16[1024,2048]{1,0:T(8,128)(2,1)}, f32[1,2048]{1,0:T(1,128)}, f32[1,2048]{1,0:T(1,128)}) custom-call(s32[1]{0:T(128)} %bitcast.half_ref.core_ref, bf16[2048,1024]{1,0:T(8,128)(2,1)} %get-tuple-element.96.grad_ref.refs_1_, bf16[2048,1024]{1,0:T(8,128)(2,1)} %all-gather.6.cloned.1.call-done.weight_ref, bf16[2048,2048]{1,0:T(8,128)(2,1)} %rows_ref.5, ...), custom_call_target="tpu_custom_call" | custom-call | flops 4294967 | bytes 16777 | tf_op jit(solution)/shard_map/dgrad_half/pallas_call | solution.py:394
  323.6 12.3 %dgrad_half.3 = (bf16[1024,2048]{1,0:T(8,128)(2,1)}, f32[1,2048]{1,0:T(1,128)}, f32[1,2048]{1,0:T(1,128)}) custom-call(s32[1]{0:T(128)} %bitcast.2.half_ref.core_ref, bf16[2048,1024]{1,0:T(8,128)(2,1)} %get-tuple-element.96.grad_ref.refs_1_, bf16[2048,1024]{1,0:T(8,128)(2,1)} %all-gather.6.cloned.1.call-done.weight_ref, bf16[2048,2048]{1,0:T(8,128)(2,1)} %rows_ref.5, ...), custom_call_target="tpu_custom_call" | custom-call | flops 4294967 | bytes 16777 | tf_op jit(solution)/shard_map/dgrad_half/pallas_call | solution.py:394
  337.3 3.1 add_convert_fusion
  342.6 3.4 fusion.18
  349.2 14.3 %weight_grad.3 = bf16[2048,1024]{1,0:T(8,128)(2,1)} custom-call(bf16[2048,2048]{1,0:T(8,128)(2,1)} %get-tuple-element.109.rows_ref.refs_0_, bf16[2048,1024]{1,0:T(8,128)(2,1)} %get-tuple-element.96.grad_ref.refs_1_), custom_call_target="tpu_custom_call" | custom-call | flops 8589934 | bytes 16777 | tf_op jit(solution)/shard_map/weight_grad/pallas_call | solution.py:481
  363.5 3.1 collective-permute-done.11
  369.5 3.4 add_convert_fusion.4
  376.5 2.9 collective-permute-done.6
  385.4 5.2 %collective-permute-done.17 = bf16[128,2048]{1,0:T(8,128)(2,1)} collective-permute-done((bf16[128,2048]{1,0:T(8,128)(2,1)}, bf16[128,2048]{1,0:T(8,128)(2,1)}, u32[]{:S(2)}, u32[]{:S(2)}) %collective-permute-start.17) | collective-permute-done | bytes 524320 | tf_op jit(solution)/shard_map/ppermute | solution.py:534
  390.6 3.5 fusion.22
  394.2 2.4 fusion.26
  396.6 15.2 %collective-permute-done.16 = f32[14,128]{1,0:T(8,128)S(1)} collective-permute-done((f32[14,128]{1,0:T(8,128)S(1)}, f32[14,128]{1,0:T(8,128)S(1)}, u32[]{:S(2)}, u32[]{:S(2)}) %collective-permute-start.16) | collective-permute-done | bytes 7200 | tf_op jit(solution)/shard_map/ppermute | solution.py:534
  413.9 2.6 pad_maximum_fusion.rows_ref
  419.0 12.7 %collective-permute-done.22 = f32[64,128]{1,0:T(8,128)S(1)} collective-permute-done((f32[64,128]{1,0:T(8,128)S(1)}, f32[64,128]{1,0:T(8,128)S(1)}, u32[]{:S(2)}, u32[]{:S(2)}) %collective-permute-start.22) | collective-permute-done | bytes 32800 | tf_op jit(solution)/shard_map/ppermute | solution.py:530
  435.1 4.7 place_half.4.refs_0_
  439.8 4.8 place_half.5
  444.6 13.0 %collective-permute-done.25 = f32[64,128]{1,0:T(8,128)S(1)} collective-permute-done((f32[64,128]{1,0:T(8,128)S(1)}, f32[64,128]{1,0:T(8,128)S(1)}, u32[]{:S(2)}, u32[]{:S(2)}) %collective-permute-start.25) | collective-permute-done | bytes 32800 | tf_op jit(solution)/shard_map/ppermute | solution.py:534
  458.6 3.4 maximum_select_fusion.2
  462.9 2.7 pad_maximum_fusion.1.rows_ref
  465.7 2.8 dynamic-slice_convert_fusion
  474.0 10.1 %reduce-scatter.3.cloned.1.call-done = bf16[512,1024]{1,0:T(8,128)(2,1)} async-done(((bf16[2048,1024]{1,0:T(8,128)(2,1)}), bf16[512,1024]{1,0:T(8,128)(2,1)}) %reduce-scatter.3.cloned.1.call-update) | async-done | bytes 1048592 | tf_op jit(solution)/shard_map/reduce_scatter | solution.py:685
  484.1 2.2 dynamic-slice_convert_fusion.1
  487.7 4.7 place_half.6.refs_0_
  492.5 2.4 collective-permute-done.27
  497.8 1.8 copy.45
  503.1 4.9 place_half.7
  (194 shorter events, 65.3 us)
Async XLA Ops:
  7.2 87.3 %all-gather.4.cloned.1.call-start = ((), (), s32[]{:S(2)}) async-start(), calls=%async_computation.2 | async-start | bytes 5242880 | tf_op jit(solution)/shard_map/all_gather | solution.py:649
  10.8 164.4 %all-gather.6.cloned.1.call-start = ((), (), s32[]{:S(2)}) async-start(), calls=%async_computation.3 | async-start | bytes 5242880 | tf_op jit(solution)/shard_map/all_gather | solution.py:650
  12.0 244.1 %all-gather.8.cloned.1.call-start = ((), (), s32[]{:S(2)}) async-start(), calls=%async_computation.4 | async-start | bytes 5242880 | tf_op jit(solution)/shard_map/all_gather | solution.py:651
  14.7 451.0 %reduce-scatter.5.cloned.1.call-start = ((), (), s32[]{:S(2)}) async-start(), calls=%async_computation.6 | async-start | bytes 10485760 | tf_op jit(solution)/shard_map/reduce_scatter | solution.py:685
  20.8 9.1 %copy-start.28 = (f32[2048]{0:T(1024)S(1)}, f32[2048]{0:T(1024)}, u32[]{:S(2)}) copy-start(f32[2048]{0:T(1024)} %param.28) | copy-start | bytes 24580
  20.8 9.7 %copy-start.22 = (s32[2048]{0:T(1024)S(1)}, s32[2048]{0:T(1024)}, u32[]{:S(2)}) copy-start(s32[2048]{0:T(1024)} %param.18) | copy-start | bytes 24580
  217.8 266.3 %reduce-scatter.3.cloned.1.call-start = ((), (), s32[]{:S(2)}) async-start(), calls=%async_computation.5 | async-start | bytes 5242880 | tf_op jit(solution)/shard_map/reduce_scatter | solution.py:685
  266.4 10.1 %collective-permute-start = (bf16[1024,2048]{1,0:T(8,128)(2,1)}, bf16[1024,2048]{1,0:T(8,128)(2,1)}, u32[]{:S(2)}, u32[]{:S(2)}) collective-permute-start(bf16[1024,2048]{1,0:T(8,128)(2,1)} %branch_half.2), channel_id=1, source_target_pairs={{0,4},{4,0},{8,12},{12,8},{1,5},{5,1},{9,13},{13,9},{2,6},{6,2},{1... | collective-permute-start | bytes 12582920 | tf_op jit(solution)/shard_map/ppermute | solution.py:526
  279.6 25.6 %collective-permute-start.1 = (bf16[256,2048]{1,0:T(8,128)(2,1)S(1)}, bf16[256,2048]{1,0:T(8,128)(2,1)S(1)}, u32[]{:S(2)}, u32[]{:S(2)}) collective-permute-start(bf16[256,2048]{1,0:T(8,128)(2,1)S(1)} %get-tuple-element.193), channel_id=1, source_target_pairs={{0,8},{8,0},{4,12},{12,4},{1,9},{9,1},{5,13},{13,5},{2,10},{10,2},... | collective-permute-start | bytes 3145736 | tf_op jit(solution)/shard_map/ppermute | solution.py:530
  281.1 25.3 %collective-permute-start.2 = (bf16[256,2048]{1,0:T(8,128)(2,1)S(1)}, bf16[256,2048]{1,0:T(8,128)(2,1)}, u32[]{:S(2)}, u32[]{:S(2)}) collective-permute-start(bf16[256,2048]{1,0:T(8,128)(2,1)S(1)} %get-tuple-element.192), channel_id=1, source_target_pairs={{0,16},{16,0},{1,17},{17,1},{2,18},{18,2},{3,19},{19,3},{4,20},{20... | collective-permute-start | bytes 3145736 | tf_op jit(solution)/shard_map/ppermute | solution.py:534
  305.2 16.1 %copy-start.11 = (bf16[256,2048]{1,0:T(8,128)(2,1)}, bf16[256,2048]{1,0:T(8,128)(2,1)S(1)}, u32[]{:S(2)}) copy-start(bf16[256,2048]{1,0:T(8,128)(2,1)S(1)} %collective-permute-done.1) | copy-start | bytes 3145732
  308.7 12.7 %copy-start.18 = (f32[2048]{0:T(1024)S(1)}, f32[2048]{0:T(1024)}, u32[]{:S(2)}) copy-start(f32[2048]{0:T(1024)} %param.24) | copy-start | bytes 24580
  308.7 12.7 %copy-start.19 = (f32[2048]{0:T(1024)S(1)}, f32[2048]{0:T(1024)}, u32[]{:S(2)}) copy-start(f32[2048]{0:T(1024)} %param.30) | copy-start | bytes 24580
  308.7 12.8 %copy-start.24 = (f32[1,2048]{1,0:T(1,128)S(1)}, f32[1,2048]{1,0:T(1,128)}, u32[]{:S(2)}) copy-start(f32[1,2048]{1,0:T(1,128)} %get-tuple-element.101) | copy-start | bytes 24580
  308.7 14.8 %copy-start.23 = (f32[1,2048]{1,0:T(1,128)S(1)}, f32[1,2048]{1,0:T(1,128)}, u32[]{:S(2)}) copy-start(f32[1,2048]{1,0:T(1,128)} %get-tuple-element.102) | copy-start | bytes 24580
  308.7 14.8 %copy-start.26 = (f32[1,768]{1,0:T(1,128)S(1)}, f32[1,768]{1,0:T(1,128)}, u32[]{:S(2)}) copy-start(f32[1,768]{1,0:T(1,128)} %get-tuple-element.107) | copy-start | bytes 9220
  321.3 16.0 %collective-permute-start.5 = (bf16[1024,2048]{1,0:T(8,128)(2,1)}, bf16[1024,2048]{1,0:T(8,128)(2,1)}, u32[]{:S(2)}, u32[]{:S(2)}) collective-permute-start(bf16[1024,2048]{1,0:T(8,128)(2,1)} %get-tuple-element.95), channel_id=1, source_target_pairs={{0,4},{4,0},{8,12},{12,8},{1,5},{5,1},{9,13},{13,9},{2,6},{6,2},{1... | collective-permute-start | bytes 12582920 | tf_op jit(solution)/shard_map/ppermute | solution.py:526
  321.5 21.1 %collective-permute-start.3 = (bf16[128,2048]{1,0:T(8,128)(2,1)S(1)}, bf16[128,2048]{1,0:T(8,128)(2,1)}, u32[]{:S(2)}, u32[]{:S(2)}) collective-permute-start(bf16[128,2048]{1,0:T(8,128)(2,1)S(1)} %get-tuple-element.191), channel_id=1, source_target_pairs={{0,16},{16,0},{1,17},{17,1},{2,18},{18,2},{3,19},{19,3},{4,20},{20... | collective-permute-start | bytes 1572872 | tf_op jit(solution)/shard_map/ppermute | solution.py:534
  323.0 19.6 %collective-permute-start.4 = (bf16[128,2048]{1,0:T(8,128)(2,1)S(1)}, bf16[128,2048]{1,0:T(8,128)(2,1)}, u32[]{:S(2)}, u32[]{:S(2)}) collective-permute-start(bf16[128,2048]{1,0:T(8,128)(2,1)S(1)} %get-tuple-element.190), channel_id=1, source_target_pairs={{0,8},{8,0},{4,12},{12,4},{1,9},{9,1},{5,13},{13,5},{2,10},{10,2},... | collective-permute-start | bytes 1572872 | tf_op jit(solution)/shard_map/ppermute | solution.py:530
  323.5 12.3 %copy-start.21 = (f32[1,2048]{1,0:T(1,128)S(1)}, f32[1,2048]{1,0:T(1,128)}, u32[]{:S(2)}) copy-start(f32[1,2048]{1,0:T(1,128)} %get-tuple-element.105) | copy-start | bytes 24580
  323.6 13.0 %copy-start.20 = (f32[1,2048]{1,0:T(1,128)S(1)}, f32[1,2048]{1,0:T(1,128)}, u32[]{:S(2)}) copy-start(f32[1,2048]{1,0:T(1,128)} %get-tuple-element.103) | copy-start | bytes 24580
  340.4 26.2 %collective-permute-start.11 = (bf16[256,2048]{1,0:T(8,128)(2,1)S(1)}, bf16[256,2048]{1,0:T(8,128)(2,1)}, u32[]{:S(2)}, u32[]{:S(2)}) collective-permute-start(bf16[256,2048]{1,0:T(8,128)(2,1)S(1)} %get-tuple-element.189), channel_id=1, source_target_pairs={{0,8},{8,0},{4,12},{12,4},{1,9},{9,1},{5,13},{13,5},{2,10},{10,2},... | collective-permute-start | bytes 3145736 | tf_op jit(solution)/shard_map/ppermute | solution.py:530
  342.0 26.1 %collective-permute-start.12 = (bf16[256,2048]{1,0:T(8,128)(2,1)S(1)}, bf16[256,2048]{1,0:T(8,128)(2,1)}, u32[]{:S(2)}, u32[]{:S(2)}) collective-permute-start(bf16[256,2048]{1,0:T(8,128)(2,1)S(1)} %get-tuple-element.188), channel_id=1, source_target_pairs={{0,16},{16,0},{1,17},{17,1},{2,18},{18,2},{3,19},{19,3},{4,20},{20... | collective-permute-start | bytes 3145736 | tf_op jit(solution)/shard_map/ppermute | solution.py:534
  346.0 33.4 %collective-permute-start.6 = (bf16[128,2048]{1,0:T(8,128)(2,1)S(1)}, bf16[128,2048]{1,0:T(8,128)(2,1)}, u32[]{:S(2)}, u32[]{:S(2)}) collective-permute-start(bf16[128,2048]{1,0:T(8,128)(2,1)S(1)} %get-tuple-element.181), channel_id=1, source_target_pairs={{0,16},{16,0},{1,17},{17,1},{2,18},{18,2},{3,19},{19,3},{4,20},{20... | collective-permute-start | bytes 1572872 | tf_op jit(solution)/shard_map/ppermute | solution.py:534
  347.6 31.8 %collective-permute-start.7 = (bf16[128,2048]{1,0:T(8,128)(2,1)S(1)}, bf16[128,2048]{1,0:T(8,128)(2,1)}, u32[]{:S(2)}, u32[]{:S(2)}) collective-permute-start(bf16[128,2048]{1,0:T(8,128)(2,1)S(1)} %get-tuple-element.180), channel_id=1, source_target_pairs={{0,8},{8,0},{4,12},{12,4},{1,9},{9,1},{5,13},{13,5},{2,10},{10,2},... | collective-permute-start | bytes 1572872 | tf_op jit(solution)/shard_map/ppermute | solution.py:530
  348.1 24.8 %collective-permute-start.10 = (f32[94,128]{1,0:T(8,128)S(1)}, f32[94,128]{1,0:T(8,128)S(1)}, u32[]{:S(2)}, u32[]{:S(2)}) collective-permute-start(f32[94,128]{1,0:T(8,128)S(1)} %bitcast.51), channel_id=1, source_target_pairs={{0,3},{1,0},{2,1},{3,2},{4,7},{5,4},{6,5},{7,6},{8,11},{9,8},{10,9... | collective-permute-start | bytes 144392 | tf_op jit(solution)/shard_map/ppermute | solution.py:765
  366.6 7.2 %collective-permute-start.8 = (f32[94,128]{1,0:T(8,128)S(1)}, f32[94,128]{1,0:T(8,128)S(1)}, u32[]{:S(2)}, u32[]{:S(2)}) collective-permute-start(f32[94,128]{1,0:T(8,128)S(1)} %bitcast.52), channel_id=1, source_target_pairs={{0,1},{1,2},{2,3},{3,0},{4,5},{5,6},{6,7},{7,4},{8,9},{9,10},{10,1... | collective-permute-start | bytes 144392 | tf_op jit(solution)/shard_map/ppermute | solution.py:765
  368.2 8.3 %collective-permute-start.9 = (f32[94,128]{1,0:T(8,128)S(1)}, f32[94,128]{1,0:T(8,128)S(1)}, u32[]{:S(2)}, u32[]{:S(2)}) collective-permute-start(f32[94,128]{1,0:T(8,128)S(1)} %bitcast.53), channel_id=1, source_target_pairs={{0,2},{1,3},{2,0},{3,1},{4,6},{5,7},{6,4},{7,5},{8,10},{9,11},{10,... | collective-permute-start | bytes 144392 | tf_op jit(solution)/shard_map/ppermute | solution.py:765
  372.9 17.7 %collective-permute-start.17 = (bf16[128,2048]{1,0:T(8,128)(2,1)}, bf16[128,2048]{1,0:T(8,128)(2,1)}, u32[]{:S(2)}, u32[]{:S(2)}) collective-permute-start(bf16[128,2048]{1,0:T(8,128)(2,1)} %get-tuple-element.187), channel_id=1, source_target_pairs={{0,16},{16,0},{1,17},{17,1},{2,18},{18,2},{3,19},{19,3},{4,20},{20... | collective-permute-start | bytes 1572872 | tf_op jit(solution)/shard_map/ppermute | solution.py:534
  373.9 16.8 %collective-permute-start.18 = (bf16[128,2048]{1,0:T(8,128)(2,1)}, bf16[128,2048]{1,0:T(8,128)(2,1)}, u32[]{:S(2)}, u32[]{:S(2)}) collective-permute-start(bf16[128,2048]{1,0:T(8,128)(2,1)} %get-tuple-element.186), channel_id=1, source_target_pairs={{0,8},{8,0},{4,12},{12,4},{1,9},{9,1},{5,13},{13,5},{2,10},{10,2},... | collective-permute-start | bytes 1572872 | tf_op jit(solution)/shard_map/ppermute | solution.py:530
  382.6 11.6 %copy-start.2 = (bf16[256,2048]{1,0:T(8,128)(2,1)}, bf16[256,2048]{1,0:T(8,128)(2,1)S(1)}, u32[]{:S(2)}) copy-start(bf16[256,2048]{1,0:T(8,128)(2,1)S(1)} %maximum_select_fusion.7) | copy-start | bytes 3145732
  382.6 1.4 collective-permute-start.15
  382.8 29.1 %collective-permute-start.14 = (bf16[256,2048]{1,0:T(8,128)(2,1)S(1)}, bf16[256,2048]{1,0:T(8,128)(2,1)S(1)}, u32[]{:S(2)}, u32[]{:S(2)}) collective-permute-start(bf16[256,2048]{1,0:T(8,128)(2,1)S(1)} %maximum_select_fusion.8), channel_id=1, source_target_pairs={{0,16},{16,0},{1,17},{17,1},{2,18},{18,2},{3,19},{19,3},{4,20},{20... | collective-permute-start | bytes 3145736 | tf_op jit(solution)/shard_map/ppermute | solution.py:534
  383.5 28.4 %collective-permute-start.13 = (bf16[256,2048]{1,0:T(8,128)(2,1)S(1)}, bf16[256,2048]{1,0:T(8,128)(2,1)S(1)}, u32[]{:S(2)}, u32[]{:S(2)}) collective-permute-start(bf16[256,2048]{1,0:T(8,128)(2,1)S(1)} %maximum_select_fusion.7), channel_id=1, source_target_pairs={{0,8},{8,0},{4,12},{12,4},{1,9},{9,1},{5,13},{13,5},{2,10},{10,2},... | collective-permute-start | bytes 3145736 | tf_op jit(solution)/shard_map/ppermute | solution.py:530
  384.0 27.9 %collective-permute-start.16 = (f32[14,128]{1,0:T(8,128)S(1)}, f32[14,128]{1,0:T(8,128)S(1)}, u32[]{:S(2)}, u32[]{:S(2)}) collective-permute-start(f32[14,128]{1,0:T(8,128)S(1)} %slice.103), channel_id=1, source_target_pairs={{0,16},{16,0},{1,17},{17,1},{2,18},{18,2},{3,19},{19,3},{4,20},{20... | collective-permute-start | bytes 21512 | tf_op jit(solution)/shard_map/ppermute | solution.py:534
  394.1 17.7 %copy-start.3 = (bf16[256,2048]{1,0:T(8,128)(2,1)S(1)}, bf16[256,2048]{1,0:T(8,128)(2,1)}, u32[]{:S(2)}) copy-start(bf16[256,2048]{1,0:T(8,128)(2,1)} %copy-done.2) | copy-start | bytes 3145732
  416.5 23.3 %collective-permute-start.19 = (bf16[1024,2048]{1,0:T(8,128)(2,1)}, bf16[1024,2048]{1,0:T(8,128)(2,1)}, u32[]{:S(2)}, u32[]{:S(2)}) collective-permute-start(bf16[1024,2048]{1,0:T(8,128)(2,1)} %pad_maximum_fusion.rows_ref), channel_id=1, source_target_pairs={{0,4},{4,0},{8,12},{12,8},{1,5},{5,1},{9,13},{13,9},{2,6},{6,2},{1... | collective-permute-start | bytes 12582920 | tf_op jit(solution)/shard_map/ppermute | solution.py:526
  416.5 15.2 %collective-permute-start.20 = (bf16[128,2048]{1,0:T(8,128)(2,1)S(1)}, bf16[128,2048]{1,0:T(8,128)(2,1)S(1)}, u32[]{:S(2)}, u32[]{:S(2)}) collective-permute-start(bf16[128,2048]{1,0:T(8,128)(2,1)S(1)} %get-tuple-element.183), channel_id=1, source_target_pairs={{0,16},{16,0},{1,17},{17,1},{2,18},{18,2},{3,19},{19,3},{4,20},{20... | collective-permute-start | bytes 1572872 | tf_op jit(solution)/shard_map/ppermute | solution.py:534
  417.0 14.8 %collective-permute-start.21 = (bf16[128,2048]{1,0:T(8,128)(2,1)S(1)}, bf16[128,2048]{1,0:T(8,128)(2,1)S(1)}, u32[]{:S(2)}, u32[]{:S(2)}) collective-permute-start(bf16[128,2048]{1,0:T(8,128)(2,1)S(1)} %get-tuple-element.182), channel_id=1, source_target_pairs={{0,8},{8,0},{4,12},{12,4},{1,9},{9,1},{5,13},{13,5},{2,10},{10,2},... | collective-permute-start | bytes 1572872 | tf_op jit(solution)/shard_map/ppermute | solution.py:530
  417.7 14.1 %collective-permute-start.22 = (f32[64,128]{1,0:T(8,128)S(1)}, f32[64,128]{1,0:T(8,128)S(1)}, u32[]{:S(2)}, u32[]{:S(2)}) collective-permute-start(f32[64,128]{1,0:T(8,128)S(1)} %slice_add_fusion), channel_id=1, source_target_pairs={{0,8},{8,0},{4,12},{12,4},{1,9},{9,1},{5,13},{13,5},{2,10},{10,2},... | collective-permute-start | bytes 98312 | tf_op jit(solution)/shard_map/ppermute | solution.py:530
  432.3 25.3 %collective-permute-start.24 = (bf16[256,2048]{1,0:T(8,128)(2,1)S(1)}, bf16[256,2048]{1,0:T(8,128)(2,1)S(1)}, u32[]{:S(2)}, u32[]{:S(2)}) collective-permute-start(bf16[256,2048]{1,0:T(8,128)(2,1)S(1)} %maximum_select_fusion.10), channel_id=1, source_target_pairs={{0,16},{16,0},{1,17},{17,1},{2,18},{18,2},{3,19},{19,3},{4,20},{20... | collective-permute-start | bytes 3145736 | tf_op jit(solution)/shard_map/ppermute | solution.py:534
  433.9 24.6 %collective-permute-start.23 = (bf16[256,2048]{1,0:T(8,128)(2,1)S(1)}, bf16[256,2048]{1,0:T(8,128)(2,1)}, u32[]{:S(2)}, u32[]{:S(2)}) collective-permute-start(bf16[256,2048]{1,0:T(8,128)(2,1)S(1)} %maximum_select_fusion.9), channel_id=1, source_target_pairs={{0,8},{8,0},{4,12},{12,4},{1,9},{9,1},{5,13},{13,5},{2,10},{10,2},... | collective-permute-start | bytes 3145736 | tf_op jit(solution)/shard_map/ppermute | solution.py:530
  434.4 23.2 %collective-permute-start.25 = (f32[64,128]{1,0:T(8,128)S(1)}, f32[64,128]{1,0:T(8,128)S(1)}, u32[]{:S(2)}, u32[]{:S(2)}) collective-permute-start(f32[64,128]{1,0:T(8,128)S(1)} %add.393), channel_id=1, source_target_pairs={{0,16},{16,0},{1,17},{17,1},{2,18},{18,2},{3,19},{19,3},{4,20},{20... | collective-permute-start | bytes 98312 | tf_op jit(solution)/shard_map/ppermute | solution.py:534
  465.6 37.5 %collective-permute-start.26 = (bf16[1024,2048]{1,0:T(8,128)(2,1)}, bf16[1024,2048]{1,0:T(8,128)(2,1)}, u32[]{:S(2)}, u32[]{:S(2)}) collective-permute-start(bf16[1024,2048]{1,0:T(8,128)(2,1)} %pad_maximum_fusion.1.rows_ref), channel_id=1, source_target_pairs={{0,4},{4,0},{8,12},{12,8},{1,5},{5,1},{9,13},{13,9},{2,6},{6,2},{1... | collective-permute-start | bytes 12582920 | tf_op jit(solution)/shard_map/ppermute | solution.py:526
  465.6 45.1 %copy-start.15 = (f32[2048]{0:T(1024)}, f32[2048]{0:T(1024)S(1)}, u32[]{:S(2)}) copy-start(f32[2048]{0:T(1024)S(1)} %slice_bitcast_fusion.5) | copy-start | bytes 24580
  468.5 26.4 %collective-permute-start.27 = (bf16[256,2048]{1,0:T(8,128)(2,1)}, bf16[256,2048]{1,0:T(8,128)(2,1)}, u32[]{:S(2)}, u32[]{:S(2)}) collective-permute-start(bf16[256,2048]{1,0:T(8,128)(2,1)} %get-tuple-element.195), channel_id=1, source_target_pairs={{0,16},{16,0},{1,17},{17,1},{2,18},{18,2},{3,19},{19,3},{4,20},{20... | collective-permute-start | bytes 3145736 | tf_op jit(solution)/shard_map/ppermute | solution.py:534
  486.3 21.7 %collective-permute-start.28 = (bf16[256,1024]{1,0:T(8,128)(2,1)}, bf16[256,1024]{1,0:T(8,128)(2,1)}, u32[]{:S(2)}, u32[]{:S(2)}) collective-permute-start(bf16[256,1024]{1,0:T(8,128)(2,1)} %get-tuple-element.199), channel_id=1, source_target_pairs={{0,16},{16,0},{1,17},{17,1},{2,18},{18,2},{3,19},{19,3},{4,20},{20... | collective-permute-start | bytes 1572872 | tf_op jit(solution)/shard_map/ppermute | solution.py:534
  503.1 8.2 %copy-start.1 = (bf16[512,2048]{1,0:T(8,128)(2,1)S(1)}, bf16[512,2048]{1,0:T(8,128)(2,1)}, u32[]{:S(2)}) copy-start(bf16[512,2048]{1,0:T(8,128)(2,1)} %param.27) | copy-start | bytes 6291460
  (15 other events, 49.9 us)
Sparse Core Ops, SparseCore 0:
  11.0 83.4 all-gather.3
  96.0 79.2 all-gather.5
  176.8 79.2 all-gather.7
  258.3 146.1 reduce-scatter.4
  406.7 77.4 reduce-scatter.2

commit v5 on v4

--- a/solution.py
+++ b/solution.py
@@ -795,12 +795,9 @@
     def halves(total):
         return pick(total, ex, chunk).astype(F32), pick(total, 1 - ex, chunk)
 
-    def share(total):
-        mine, given = halves(total)
-        return mine, x_swap(given)
-
-    first_mine, first_other = share(after(first_total, *input_two))
-    output_half = place_half(core, after(output_mine, *input_two))
+    first_mine, first_given = halves(after(first_total, *input_two))
+    first_other = x_swap(first_given)
+    output_half = place_half(core, after(output_mine, first_given, *input_two))
     output_rows = place_half(1 - core, after(output_other, output_half), output_half)
     biases, other = biases.reshape(-1), biases_other.reshape(-1)
     qkv_bias_grad = join(ex, biases[:qkv_cols], other[:qkv_cols])
@@ -808,16 +805,16 @@
     input_got, norms_other = after((input_got, norms_other), output_rows)
     norms = (norms + norms_other).reshape(4, width)
     input_mine, input_other = gather_last(input_two, input_got, core, why, ex)
-    up_mine, up_given = halves(after(up_total, input_mine))
+    grad_half = place_half(core, after(input_mine, norms))
+    up_mine, up_given = halves(after(up_total, grad_half))
     up_other = x_swap(up_given)
-    first_other = after(first_other, up_given)
+    grad_input = place_half(1 - core, after(input_other, up_given), grad_half)
+    first_other = after(first_other, grad_input)
     heads_mine, down_mine = first_mine[:, :-units], first_mine[:, -units:]
     other, down_other = first_other[:, :-units].astype(F32), first_other[:, -units:].astype(F32)
     qkv_out = join(ex, heads_mine[:, :qkv_cols], other[:, :qkv_cols], 1)
     out_out = join(ex, heads_mine[:, qkv_cols:].T, other[:, qkv_cols:].T, 0)
     down_out = join(ex, down_mine.T, down_other.T, 0)
-    grad_half = place_half(core, after(input_mine, norms, up_given))
-    grad_input = place_half(1 - core, after(input_other, grad_half), grad_half)
     up_other = after(up_other, qkv_out, out_out, down_out, grad_input)
     up_out = join(ex, up_mine, up_other.astype(F32), 1)
 

time: 524 us -> 526 us (level)
  other arithmetic: 86.9 us -> 92.8 us
    select_n x14, other arithmetic: 14.4 us -> 21.6 us  [join(): jnp.where(low_index == 0, jnp.concatenate([mine, other], axis), jnp.conca...]
  transfers between devices with their start and end apart: 34 -> 34, of which waited for: 16 -> 16; matrix products, arithmetic and copies ran while one was open for 21% -> 22% of each run, Pallas kernels for 37% -> 36%
where the time goes in v5:
time: 526 us; the launch traced here: 520 us
  Pallas kernels  189 us (36%)
  waiting for transfers between devices  171 us (33%)
  other arithmetic  92.8 us (18%)
  starting transfers between devices  24 us (5%)
  local copies, waits for them, and re-layouts  20.3 us (4%)
  between operations  15.4 us (3%)
  matrix products  6.94 us (1%)
    pallas_call x2, Pallas kernels, weight_grad(): pl.pallas_call(partial(weight_grad_kernel, pairs=len(pairs)), grid=(2 * c...  39.4 us
    all_gather x1, waiting for transfers between devices, local(): heads_full = lax.all_gather(heads_shard, 'dp', axis=0, tiled=True)  38.8 us
    all_gather x1, waiting for transfers between devices, local(): down_full = lax.all_gather(down_shard, 'dp', axis=0, tiled=True)  38.2 us
    ppermute x12, waiting for transfers between devices, x_swap(): return lax.ppermute(block, 'branch', XAX)  36.6 us
    pallas_call x2, Pallas kernels, dgrad_half(): pl.pallas_call(partial(dgrad_half_kernel, chunk=chunk), grid_spec=pltpu.P...  24.8 us
    ppermute x9, waiting for transfers between devices, y_swap(): return lax.ppermute(block, 'tensor', YAX)  23.8 us
    select_n x14, other arithmetic, join(): jnp.where(low_index == 0, jnp.concatenate([mine, other], axis), jnp.conca...  21.6 us
    pallas_call x2, Pallas kernels, branch_half(): pl.pallas_call(partial(branch_kernel, chunk=chunk), grid_spec=pltpu.Prefe...  20.3 us
  transfers between devices with their start and end apart: 34, of which 16 were waited for; matrix products, arithmetic and copies ran while one was open for 22% of the time, Pallas kernels for 36%

profile of v5, /device:TPU:0, one launch (start us, length us, event | category | flops | bytes accessed | tf_op | source)
XLA Modules:
  0.0 519.5 jit_solution(10372158954137041158)
XLA Ops:
  16.2 4.5 convert_reduce_fusion
  20.8 6.4 %fusion.8 = f32[2048]{0:T(1024)S(1)} fusion(bf16[2048,2048]{1,0:T(8,128)(2,1)} %rows_ref.5, f32[2048]{0:T(1024)S(1)} %broadcast_multiply_fusion.1), kind=kLoop, calls=%fused_computation.10 | loop fusion | flops 16775168 | bytes 8404992 | tf_op jit(solution)/shard_map/reduce_sum | solution.py:662
  32.6 3.9 fusion.28
  36.6 2.5 maximum_maximum_fusion.2
  39.1 16.5 %fusion.7 = (bf16[2048,2048]{1,0:T(8,128)(2,1)}, bf16[2048,2048]{1,0:T(8,128)(2,1)}, f32[2048]{0:T(1024)S(1)}, bf16[2048,2048]{1,0:T(8,128)(2,1)}) fusion(bf16[2048,2048]{1,0:T(8,128)(2,1)} %rows_ref.5, f32[2048]{0:T(1024)S(1)} %copy-done.11, f32[2048]{0:T(1024)S(1)} %copy-done.8, f32[2048]{0:T(1024)S(1)} %add_rsqrt_fusion, ...), kind=kLoop, calls=%fused_computation.9 | loop fusion | flops 50329600 | bytes 42004480 | tf_op jit(solution)/shard_map/convert_element_type | solution.py:666
  55.7 38.8 %all-gather.4.cloned.1.call-done.weight_ref.out_ref_w = bf16[2048,1024]{1,0:T(8,128)(2,1)} async-done(((bf16[512,1024]{1,0:T(8,128)(2,1)}), bf16[2048,1024]{1,0:T(8,128)(2,1)}) %all-gather.4.cloned.1.call-update) | async-done | bytes 4194320 | tf_op jit(solution)/shard_map/all_gather | solution.py:649
  94.5 11.8 %project.1.query_ref.key_ref.value_ref = bf16[2048,768]{1,0:T(8,128)(2,1)} custom-call(bf16[2048,2048]{1,0:T(8,128)(2,1)} %get-tuple-element.183.rows_ref.refs_0_, bf16[2048,1024]{1,0:T(8,128)(2,1)} %all-gather.4.cloned.1.call-done.weight_ref.out_ref_w, f32[1,768]{1,0:T(1,128)} %broadcast_in_dim.22.bias_ref, f32[2048,128]{1,0:T(8,128)} %get-tuple-element.217.cos_ref, ...), custom_call_target="tpu_custom_call" | custom-call | flops 6442450 | bytes 14680 | tf_op jit(solution)/shard_map/project/pallas_call | solution.py:77
  107.6 8.7 %attend.1 = (bf16[2048,256]{1,0:T(8,128)(2,1)}, f32[8,2048]{1,0:T(8,128)}) custom-call(bf16[2048,768]{1,0:T(8,128)(2,1)} %project.1.query_ref.key_ref.value_ref, bf16[2048,768]{1,0:T(8,128)(2,1)} %project.1.query_ref.key_ref.value_ref, bf16[2048,768]{1,0:T(8,128)(2,1)} %project.1.query_ref.key_ref.value_ref, f32[2048,128]{1,0:T(8,128)} %broadcast_in_dim.27.bias_ref), custom_call_target="tpu_custom_call" | custom-call | flops 2684354 | bytes 4194 | tf_op jit(solution)/shard_map/attend/pallas_call | solution.py:140
  116.3 6.9 %convolution_convert_fusion.grad_ref = bf16[2048,256]{1,0:T(8,128)(2,1)} fusion(bf16[2048,2048]{1,0:T(8,128)(2,1)} %get-tuple-element.88.refs_2_.refs_4_.grad_ref, bf16[2048,1024]{1,0:T(8,128)(2,1)} %all-gather.4.cloned.1.call-done.weight_ref.out_ref_w), kind=kOutput, calls=%fused_computation.15 | convolution fusion | flops 2148007936 | bytes 10485760 | tf_op jit(solution)/shard_map/dot_general | solution.py:678
  123.3 14.9 %attend_back.1 = (bf16[2048,768]{1,0:T(8,128)(2,1)}, f32[1,768]{1,0:T(1,128)}) custom-call(bf16[2048,768]{1,0:T(8,128)(2,1)} %project.1.query_ref.key_ref.value_ref, bf16[2048,768]{1,0:T(8,128)(2,1)} %project.1.query_ref.key_ref.value_ref, bf16[2048,768]{1,0:T(8,128)(2,1)} %project.1.query_ref.key_ref.value_ref, ...), custom_call_target="tpu_custom_call" | custom-call | flops 6710886 | bytes 8388 | tf_op jit(solution)/shard_map/attend_back/pallas_call | solution.py:213
  138.2 17.2 %dgrad_first.1 = (f32[2048,2048]{1,0:T(8,128)}, f32[1,2048]{1,0:T(1,128)}, f32[1,2048]{1,0:T(1,128)}) custom-call(bf16[2048,768]{1,0:T(8,128)(2,1)} %get-tuple-element.83.grad_ref.refs_1_, bf16[2048,1024]{1,0:T(8,128)(2,1)} %all-gather.4.cloned.1.call-done.weight_ref.out_ref_w, bf16[2048,2048]{1,0:T(8,128)(2,1)} %rows_ref.5, f32[2048,1]{1,0:T(8,128)} %copy.37.mean_ref, ...), custom_call_target="tpu_custom_call" | custom-call | flops 6442450 | bytes 28311 | tf_op jit(solution)/shard_map/dgrad_first/pallas_call | solution.py:364
  155.3 19.9 %all-gather.6.cloned.1.call-done.weight_ref = bf16[2048,1024]{1,0:T(8,128)(2,1)} async-done(((bf16[512,1024]{1,0:T(8,128)(2,1)}), bf16[2048,1024]{1,0:T(8,128)(2,1)}) %all-gather.6.cloned.1.call-update) | async-done | bytes 4194320 | tf_op jit(solution)/shard_map/all_gather | solution.py:650
  175.3 17.4 %up_gelu.1 = (bf16[2048,1024]{1,0:T(8,128)(2,1)}, f32[2048,1024]{1,0:T(8,128)}) custom-call(bf16[2048,2048]{1,0:T(8,128)(2,1)} %get-tuple-element.108.rows_ref.refs_0_, bf16[2048,1024]{1,0:T(8,128)(2,1)} %all-gather.6.cloned.1.call-done.weight_ref, f32[1,1024]{1,0:T(1,128)} %bitcast.57), custom_call_target="tpu_custom_call" | custom-call | flops 8589934 | bytes 25165 | tf_op jit(solution)/shard_map/up_gelu/pallas_call | solution.py:260
  192.7 25.1 %weight_grad.2 = bf16[2048,2048]{1,0:T(8,128)(2,1)} custom-call(bf16[2048,2048]{1,0:T(8,128)(2,1)} %get-tuple-element.183.rows_ref.refs_0_, bf16[2048,768]{1,0:T(8,128)(2,1)} %get-tuple-element.83.grad_ref.refs_1_, bf16[2048,2048]{1,0:T(8,128)(2,1)} %get-tuple-element.88.refs_2_.refs_4_.grad_ref, bf16[2048,256]{1,0:T(8,128)(2,1)} %get-tuple-element.77.refs_3_.heads_ref, ...), custom_call_target="tpu_custom_call" | custom-call | flops 17179868 | bytes 25165 | tf_op jit(solution)/shard_map/weight_grad/pallas_call | solution.py:481
  217.9 38.2 %all-gather.8.cloned.1.call-done.down_ref.weight_ref = bf16[2048,1024]{1,0:T(8,128)(2,1)} async-done(((bf16[512,1024]{1,0:T(8,128)(2,1)}), bf16[2048,1024]{1,0:T(8,128)(2,1)}) %all-gather.8.cloned.1.call-update) | async-done | bytes 4194320 | tf_op jit(solution)/shard_map/all_gather | solution.py:651
  256.1 10.2 %branch_half.2 = bf16[1024,2048]{1,0:T(8,128)(2,1)} custom-call(s32[1]{0:T(128)} %bitcast.half_ref.core_ref, bf16[2048,256]{1,0:T(8,128)(2,1)} %get-tuple-element.77.refs_3_.heads_ref, bf16[2048,1024]{1,0:T(8,128)(2,1)} %all-gather.4.cloned.1.call-done.weight_ref.out_ref_w, bf16[2048,1024]{1,0:T(8,128)(2,1)} %get-tuple-element.86.refs_5_.act_ref, ...), custom_call_target="tpu_custom_call" | custom-call | flops 5368709 | bytes 10485 | tf_op jit(solution)/shard_map/branch_half/pallas_call | solution.py:434
  266.4 10.1 %branch_half.3 = bf16[1024,2048]{1,0:T(8,128)(2,1)} custom-call(s32[1]{0:T(128)} %bitcast.2.half_ref.core_ref, bf16[2048,256]{1,0:T(8,128)(2,1)} %get-tuple-element.77.refs_3_.heads_ref, bf16[2048,1024]{1,0:T(8,128)(2,1)} %all-gather.4.cloned.1.call-done.weight_ref.out_ref_w, bf16[2048,1024]{1,0:T(8,128)(2,1)} %get-tuple-element.86.refs_5_.act_ref, ...), custom_call_target="tpu_custom_call" | custom-call | flops 5368709 | bytes 10485 | tf_op jit(solution)/shard_map/branch_half/pallas_call | solution.py:434
  276.5 3.1 add_convert_fusion.2
  282.6 15.6 %hidden_back.1 = (bf16[2048,1024]{1,0:T(8,128)(2,1)}, f32[1,1024]{1,0:T(1,128)}) custom-call(bf16[2048,2048]{1,0:T(8,128)(2,1)} %get-tuple-element.88.refs_2_.refs_4_.grad_ref, bf16[2048,1024]{1,0:T(8,128)(2,1)} %all-gather.8.cloned.1.call-done.down_ref.weight_ref, f32[2048,1024]{1,0:T(8,128)} %get-tuple-element.89.slope_ref), custom_call_target="tpu_custom_call" | custom-call | flops 8589934 | bytes 25165 | tf_op jit(solution)/shard_map/hidden_back/pallas_call | solution.py:297
  298.2 7.0 %collective-permute-done.1 = bf16[256,2048]{1,0:T(8,128)(2,1)S(1)} collective-permute-done((bf16[256,2048]{1,0:T(8,128)(2,1)S(1)}, bf16[256,2048]{1,0:T(8,128)(2,1)S(1)}, u32[]{:S(2)}, u32[]{:S(2)}) %collective-permute-start.1) | collective-permute-done | bytes 1048608 | tf_op jit(solution)/shard_map/ppermute | solution.py:530
  306.5 2.2 add_convert_fusion.6
  308.8 12.5 %dgrad_half.2 = (bf16[1024,2048]{1,0:T(8,128)(2,1)}, f32[1,2048]{1,0:T(1,128)}, f32[1,2048]{1,0:T(1,128)}) custom-call(s32[1]{0:T(128)} %bitcast.half_ref.core_ref, bf16[2048,1024]{1,0:T(8,128)(2,1)} %get-tuple-element.95.grad_ref.refs_1_, bf16[2048,1024]{1,0:T(8,128)(2,1)} %all-gather.6.cloned.1.call-done.weight_ref, bf16[2048,2048]{1,0:T(8,128)(2,1)} %rows_ref.5, ...), custom_call_target="tpu_custom_call" | custom-call | flops 4294967 | bytes 16777 | tf_op jit(solution)/shard_map/dgrad_half/pallas_call | solution.py:394
  323.6 12.3 %dgrad_half.3 = (bf16[1024,2048]{1,0:T(8,128)(2,1)}, f32[1,2048]{1,0:T(1,128)}, f32[1,2048]{1,0:T(1,128)}) custom-call(s32[1]{0:T(128)} %bitcast.2.half_ref.core_ref, bf16[2048,1024]{1,0:T(8,128)(2,1)} %get-tuple-element.95.grad_ref.refs_1_, bf16[2048,1024]{1,0:T(8,128)(2,1)} %all-gather.6.cloned.1.call-done.weight_ref, bf16[2048,2048]{1,0:T(8,128)(2,1)} %rows_ref.5, ...), custom_call_target="tpu_custom_call" | custom-call | flops 4294967 | bytes 16777 | tf_op jit(solution)/shard_map/dgrad_half/pallas_call | solution.py:394
  337.4 3.1 add_convert_fusion
  342.7 3.4 fusion.18
  349.2 14.2 %weight_grad.3 = bf16[2048,1024]{1,0:T(8,128)(2,1)} custom-call(bf16[2048,2048]{1,0:T(8,128)(2,1)} %get-tuple-element.108.rows_ref.refs_0_, bf16[2048,1024]{1,0:T(8,128)(2,1)} %get-tuple-element.95.grad_ref.refs_1_), custom_call_target="tpu_custom_call" | custom-call | flops 8589934 | bytes 16777 | tf_op jit(solution)/shard_map/weight_grad/pallas_call | solution.py:481
  363.5 3.2 collective-permute-done.11
  369.5 2.4 add_convert_fusion.4
  376.5 2.9 collective-permute-done.6
  385.4 5.2 %collective-permute-done.17 = bf16[128,2048]{1,0:T(8,128)(2,1)S(1)} collective-permute-done((bf16[128,2048]{1,0:T(8,128)(2,1)S(1)}, bf16[128,2048]{1,0:T(8,128)(2,1)S(1)}, u32[]{:S(2)}, u32[]{:S(2)}) %collective-permute-start.17) | collective-permute-done | bytes 524320 | tf_op jit(solution)/shard_map/ppermute | solution.py:534
  390.6 3.2 fusion.22
  393.8 2.3 fusion.26
  396.1 15.8 %collective-permute-done.16 = f32[14,128]{1,0:T(8,128)S(1)} collective-permute-done((f32[14,128]{1,0:T(8,128)S(1)}, f32[14,128]{1,0:T(8,128)S(1)}, u32[]{:S(2)}, u32[]{:S(2)}) %collective-permute-start.16) | collective-permute-done | bytes 7200 | tf_op jit(solution)/shard_map/ppermute | solution.py:534
  414.0 2.6 pad_maximum_fusion.rows_ref
  419.2 12.7 %collective-permute-done.22 = f32[64,128]{1,0:T(8,128)S(1)} collective-permute-done((f32[64,128]{1,0:T(8,128)S(1)}, f32[64,128]{1,0:T(8,128)S(1)}, u32[]{:S(2)}, u32[]{:S(2)}) %collective-permute-start.22) | collective-permute-done | bytes 32800 | tf_op jit(solution)/shard_map/ppermute | solution.py:530
  433.5 2.6 maximum_select_fusion.9
  438.7 2.8 dynamic-slice_convert_fusion
  441.5 5.0 place_half.4.refs_0_
  446.5 4.7 place_half.5
  451.2 10.1 %collective-permute-done.25 = f32[64,128]{1,0:T(8,128)S(1)} collective-permute-done((f32[64,128]{1,0:T(8,128)S(1)}, f32[64,128]{1,0:T(8,128)S(1)}, u32[]{:S(2)}, u32[]{:S(2)}) %collective-permute-start.25) | collective-permute-done | bytes 32800 | tf_op jit(solution)/shard_map/ppermute | solution.py:534
  462.3 3.3 maximum_select_fusion.2
  465.6 2.5 maximum_select_fusion.3
  468.1 2.7 pad_maximum_fusion.1.rows_ref
  472.7 4.7 place_half.6.refs_0_
  480.1 10.7 %reduce-scatter.5.cloned.1.call-done = bf16[512,1024]{1,0:T(8,128)(2,1)} async-done(((bf16[2048,1024]{1,0:T(8,128)(2,1)}), bf16[512,1024]{1,0:T(8,128)(2,1)}) %reduce-scatter.5.cloned.1.call-update) | async-done | bytes 1048592 | tf_op jit(solution)/shard_map/reduce_scatter | solution.py:685
  490.8 2.2 dynamic-slice_convert_fusion.1
  494.5 4.7 place_half.7
  506.1 3.3 maximum_select_fusion.6
  (184 shorter events, 67.7 us)
Async XLA Ops:
  7.2 87.3 %all-gather.4.cloned.1.call-start = ((), (), s32[]{:S(2)}) async-start(), calls=%async_computation.2 | async-start | bytes 5242880 | tf_op jit(solution)/shard_map/all_gather | solution.py:649
  10.8 164.4 %all-gather.6.cloned.1.call-start = ((), (), s32[]{:S(2)}) async-start(), calls=%async_computation.3 | async-start | bytes 5242880 | tf_op jit(solution)/shard_map/all_gather | solution.py:650
  12.0 244.1 %all-gather.8.cloned.1.call-start = ((), (), s32[]{:S(2)}) async-start(), calls=%async_computation.4 | async-start | bytes 5242880 | tf_op jit(solution)/shard_map/all_gather | solution.py:651
  14.7 424.0 %reduce-scatter.3.cloned.1.call-start = ((), (), s32[]{:S(2)}) async-start(), calls=%async_computation.5 | async-start | bytes 10485760 | tf_op jit(solution)/shard_map/reduce_scatter | solution.py:685
  20.8 9.1 %copy-start.23 = (f32[2048]{0:T(1024)S(1)}, f32[2048]{0:T(1024)}, u32[]{:S(2)}) copy-start(f32[2048]{0:T(1024)} %param.28) | copy-start | bytes 24580
  20.8 9.7 %copy-start.17 = (s32[2048]{0:T(1024)S(1)}, s32[2048]{0:T(1024)}, u32[]{:S(2)}) copy-start(s32[2048]{0:T(1024)} %param.18) | copy-start | bytes 24580
  217.9 273.0 %reduce-scatter.5.cloned.1.call-start = ((), (), s32[]{:S(2)}) async-start(), calls=%async_computation.6 | async-start | bytes 5242880 | tf_op jit(solution)/shard_map/reduce_scatter | solution.py:685
  266.3 10.1 %collective-permute-start = (bf16[1024,2048]{1,0:T(8,128)(2,1)}, bf16[1024,2048]{1,0:T(8,128)(2,1)}, u32[]{:S(2)}, u32[]{:S(2)}) collective-permute-start(bf16[1024,2048]{1,0:T(8,128)(2,1)} %branch_half.2), channel_id=1, source_target_pairs={{0,4},{4,0},{8,12},{12,8},{1,5},{5,1},{9,13},{13,9},{2,6},{6,2},{1... | collective-permute-start | bytes 12582920 | tf_op jit(solution)/shard_map/ppermute | solution.py:526
  279.6 25.6 %collective-permute-start.1 = (bf16[256,2048]{1,0:T(8,128)(2,1)S(1)}, bf16[256,2048]{1,0:T(8,128)(2,1)S(1)}, u32[]{:S(2)}, u32[]{:S(2)}) collective-permute-start(bf16[256,2048]{1,0:T(8,128)(2,1)S(1)} %get-tuple-element.191), channel_id=1, source_target_pairs={{0,8},{8,0},{4,12},{12,4},{1,9},{9,1},{5,13},{13,5},{2,10},{10,2},... | collective-permute-start | bytes 3145736 | tf_op jit(solution)/shard_map/ppermute | solution.py:530
  281.1 25.3 %collective-permute-start.2 = (bf16[256,2048]{1,0:T(8,128)(2,1)S(1)}, bf16[256,2048]{1,0:T(8,128)(2,1)}, u32[]{:S(2)}, u32[]{:S(2)}) collective-permute-start(bf16[256,2048]{1,0:T(8,128)(2,1)S(1)} %get-tuple-element.190), channel_id=1, source_target_pairs={{0,16},{16,0},{1,17},{17,1},{2,18},{18,2},{3,19},{19,3},{4,20},{20... | collective-permute-start | bytes 3145736 | tf_op jit(solution)/shard_map/ppermute | solution.py:534
  305.2 16.1 %copy-start.6 = (bf16[256,2048]{1,0:T(8,128)(2,1)}, bf16[256,2048]{1,0:T(8,128)(2,1)S(1)}, u32[]{:S(2)}) copy-start(bf16[256,2048]{1,0:T(8,128)(2,1)S(1)} %collective-permute-done.1) | copy-start | bytes 3145732
  308.7 12.7 %copy-start.13 = (f32[2048]{0:T(1024)S(1)}, f32[2048]{0:T(1024)}, u32[]{:S(2)}) copy-start(f32[2048]{0:T(1024)} %param.24) | copy-start | bytes 24580
  308.7 12.7 %copy-start.14 = (f32[2048]{0:T(1024)S(1)}, f32[2048]{0:T(1024)}, u32[]{:S(2)}) copy-start(f32[2048]{0:T(1024)} %param.30) | copy-start | bytes 24580
  308.7 12.8 %copy-start.19 = (f32[1,2048]{1,0:T(1,128)S(1)}, f32[1,2048]{1,0:T(1,128)}, u32[]{:S(2)}) copy-start(f32[1,2048]{1,0:T(1,128)} %get-tuple-element.100) | copy-start | bytes 24580
  308.7 14.8 %copy-start.18 = (f32[1,2048]{1,0:T(1,128)S(1)}, f32[1,2048]{1,0:T(1,128)}, u32[]{:S(2)}) copy-start(f32[1,2048]{1,0:T(1,128)} %get-tuple-element.101) | copy-start | bytes 24580
  308.7 14.8 %copy-start.21 = (f32[1,768]{1,0:T(1,128)S(1)}, f32[1,768]{1,0:T(1,128)}, u32[]{:S(2)}) copy-start(f32[1,768]{1,0:T(1,128)} %get-tuple-element.106) | copy-start | bytes 9220
  321.3 16.1 %collective-permute-start.5 = (bf16[1024,2048]{1,0:T(8,128)(2,1)}, bf16[1024,2048]{1,0:T(8,128)(2,1)}, u32[]{:S(2)}, u32[]{:S(2)}) collective-permute-start(bf16[1024,2048]{1,0:T(8,128)(2,1)} %get-tuple-element.94), channel_id=1, source_target_pairs={{0,4},{4,0},{8,12},{12,8},{1,5},{5,1},{9,13},{13,9},{2,6},{6,2},{1... | collective-permute-start | bytes 12582920 | tf_op jit(solution)/shard_map/ppermute | solution.py:526
  321.5 21.1 %collective-permute-start.3 = (bf16[128,2048]{1,0:T(8,128)(2,1)S(1)}, bf16[128,2048]{1,0:T(8,128)(2,1)}, u32[]{:S(2)}, u32[]{:S(2)}) collective-permute-start(bf16[128,2048]{1,0:T(8,128)(2,1)S(1)} %get-tuple-element.189), channel_id=1, source_target_pairs={{0,16},{16,0},{1,17},{17,1},{2,18},{18,2},{3,19},{19,3},{4,20},{20... | collective-permute-start | bytes 1572872 | tf_op jit(solution)/shard_map/ppermute | solution.py:534
  323.1 19.6 %collective-permute-start.4 = (bf16[128,2048]{1,0:T(8,128)(2,1)S(1)}, bf16[128,2048]{1,0:T(8,128)(2,1)}, u32[]{:S(2)}, u32[]{:S(2)}) collective-permute-start(bf16[128,2048]{1,0:T(8,128)(2,1)S(1)} %get-tuple-element.188), channel_id=1, source_target_pairs={{0,8},{8,0},{4,12},{12,4},{1,9},{9,1},{5,13},{13,5},{2,10},{10,2},... | collective-permute-start | bytes 1572872 | tf_op jit(solution)/shard_map/ppermute | solution.py:530
  323.6 12.3 %copy-start.16 = (f32[1,2048]{1,0:T(1,128)S(1)}, f32[1,2048]{1,0:T(1,128)}, u32[]{:S(2)}) copy-start(f32[1,2048]{1,0:T(1,128)} %get-tuple-element.104) | copy-start | bytes 24580
  323.6 13.0 %copy-start.15 = (f32[1,2048]{1,0:T(1,128)S(1)}, f32[1,2048]{1,0:T(1,128)}, u32[]{:S(2)}) copy-start(f32[1,2048]{1,0:T(1,128)} %get-tuple-element.102) | copy-start | bytes 24580
  340.5 26.2 %collective-permute-start.11 = (bf16[256,2048]{1,0:T(8,128)(2,1)S(1)}, bf16[256,2048]{1,0:T(8,128)(2,1)}, u32[]{:S(2)}, u32[]{:S(2)}) collective-permute-start(bf16[256,2048]{1,0:T(8,128)(2,1)S(1)} %get-tuple-element.187), channel_id=1, source_target_pairs={{0,8},{8,0},{4,12},{12,4},{1,9},{9,1},{5,13},{13,5},{2,10},{10,2},... | collective-permute-start | bytes 3145736 | tf_op jit(solution)/shard_map/ppermute | solution.py:530
  342.1 26.1 %collective-permute-start.12 = (bf16[256,2048]{1,0:T(8,128)(2,1)S(1)}, bf16[256,2048]{1,0:T(8,128)(2,1)}, u32[]{:S(2)}, u32[]{:S(2)}) collective-permute-start(bf16[256,2048]{1,0:T(8,128)(2,1)S(1)} %get-tuple-element.186), channel_id=1, source_target_pairs={{0,16},{16,0},{1,17},{17,1},{2,18},{18,2},{3,19},{19,3},{4,20},{20... | collective-permute-start | bytes 3145736 | tf_op jit(solution)/shard_map/ppermute | solution.py:534
  346.1 33.3 %collective-permute-start.6 = (bf16[128,2048]{1,0:T(8,128)(2,1)S(1)}, bf16[128,2048]{1,0:T(8,128)(2,1)}, u32[]{:S(2)}, u32[]{:S(2)}) collective-permute-start(bf16[128,2048]{1,0:T(8,128)(2,1)S(1)} %get-tuple-element.179), channel_id=1, source_target_pairs={{0,16},{16,0},{1,17},{17,1},{2,18},{18,2},{3,19},{19,3},{4,20},{20... | collective-permute-start | bytes 1572872 | tf_op jit(solution)/shard_map/ppermute | solution.py:534
  347.6 31.8 %collective-permute-start.7 = (bf16[128,2048]{1,0:T(8,128)(2,1)S(1)}, bf16[128,2048]{1,0:T(8,128)(2,1)}, u32[]{:S(2)}, u32[]{:S(2)}) collective-permute-start(bf16[128,2048]{1,0:T(8,128)(2,1)S(1)} %get-tuple-element.178), channel_id=1, source_target_pairs={{0,8},{8,0},{4,12},{12,4},{1,9},{9,1},{5,13},{13,5},{2,10},{10,2},... | collective-permute-start | bytes 1572872 | tf_op jit(solution)/shard_map/ppermute | solution.py:530
  348.1 23.8 %collective-permute-start.10 = (f32[94,128]{1,0:T(8,128)S(1)}, f32[94,128]{1,0:T(8,128)S(1)}, u32[]{:S(2)}, u32[]{:S(2)}) collective-permute-start(f32[94,128]{1,0:T(8,128)S(1)} %bitcast.51), channel_id=1, source_target_pairs={{0,3},{1,0},{2,1},{3,2},{4,7},{5,4},{6,5},{7,6},{8,11},{9,8},{10,9... | collective-permute-start | bytes 144392 | tf_op jit(solution)/shard_map/ppermute | solution.py:765
  366.7 7.3 %collective-permute-start.8 = (f32[94,128]{1,0:T(8,128)S(1)}, f32[94,128]{1,0:T(8,128)S(1)}, u32[]{:S(2)}, u32[]{:S(2)}) collective-permute-start(f32[94,128]{1,0:T(8,128)S(1)} %bitcast.52), channel_id=1, source_target_pairs={{0,1},{1,2},{2,3},{3,0},{4,5},{5,6},{6,7},{7,4},{8,9},{9,10},{10,1... | collective-permute-start | bytes 144392 | tf_op jit(solution)/shard_map/ppermute | solution.py:765
  368.2 8.3 %collective-permute-start.9 = (f32[94,128]{1,0:T(8,128)S(1)}, f32[94,128]{1,0:T(8,128)S(1)}, u32[]{:S(2)}, u32[]{:S(2)}) collective-permute-start(f32[94,128]{1,0:T(8,128)S(1)} %bitcast.53), channel_id=1, source_target_pairs={{0,2},{1,3},{2,0},{3,1},{4,6},{5,7},{6,4},{7,5},{8,10},{9,11},{10,... | collective-permute-start | bytes 144392 | tf_op jit(solution)/shard_map/ppermute | solution.py:765
  372.0 18.6 %collective-permute-start.17 = (bf16[128,2048]{1,0:T(8,128)(2,1)S(1)}, bf16[128,2048]{1,0:T(8,128)(2,1)S(1)}, u32[]{:S(2)}, u32[]{:S(2)}) collective-permute-start(bf16[128,2048]{1,0:T(8,128)(2,1)S(1)} %get-tuple-element.185), channel_id=1, source_target_pairs={{0,16},{16,0},{1,17},{17,1},{2,18},{18,2},{3,19},{19,3},{4,20},{20... | collective-permute-start | bytes 1572872 | tf_op jit(solution)/shard_map/ppermute | solution.py:534
  373.9 16.6 %collective-permute-start.18 = (bf16[128,2048]{1,0:T(8,128)(2,1)S(1)}, bf16[128,2048]{1,0:T(8,128)(2,1)S(1)}, u32[]{:S(2)}, u32[]{:S(2)}) collective-permute-start(bf16[128,2048]{1,0:T(8,128)(2,1)S(1)} %get-tuple-element.184), channel_id=1, source_target_pairs={{0,8},{8,0},{4,12},{12,4},{1,9},{9,1},{5,13},{13,5},{2,10},{10,2},... | collective-permute-start | bytes 1572872 | tf_op jit(solution)/shard_map/ppermute | solution.py:530
  382.6 1.3 collective-permute-start.15
  382.8 29.1 %collective-permute-start.14 = (bf16[256,2048]{1,0:T(8,128)(2,1)S(1)}, bf16[256,2048]{1,0:T(8,128)(2,1)S(1)}, u32[]{:S(2)}, u32[]{:S(2)}) collective-permute-start(bf16[256,2048]{1,0:T(8,128)(2,1)S(1)} %maximum_select_fusion.8), channel_id=1, source_target_pairs={{0,16},{16,0},{1,17},{17,1},{2,18},{18,2},{3,19},{19,3},{4,20},{20... | collective-permute-start | bytes 3145736 | tf_op jit(solution)/shard_map/ppermute | solution.py:534
  383.4 28.5 %collective-permute-start.13 = (bf16[256,2048]{1,0:T(8,128)(2,1)S(1)}, bf16[256,2048]{1,0:T(8,128)(2,1)S(1)}, u32[]{:S(2)}, u32[]{:S(2)}) collective-permute-start(bf16[256,2048]{1,0:T(8,128)(2,1)S(1)} %maximum_select_fusion.7), channel_id=1, source_target_pairs={{0,8},{8,0},{4,12},{12,4},{1,9},{9,1},{5,13},{13,5},{2,10},{10,2},... | collective-permute-start | bytes 3145736 | tf_op jit(solution)/shard_map/ppermute | solution.py:530
  383.9 28.0 %collective-permute-start.16 = (f32[14,128]{1,0:T(8,128)S(1)}, f32[14,128]{1,0:T(8,128)S(1)}, u32[]{:S(2)}, u32[]{:S(2)}) collective-permute-start(f32[14,128]{1,0:T(8,128)S(1)} %slice.103), channel_id=1, source_target_pairs={{0,16},{16,0},{1,17},{17,1},{2,18},{18,2},{3,19},{19,3},{4,20},{20... | collective-permute-start | bytes 21512 | tf_op jit(solution)/shard_map/ppermute | solution.py:534
  396.1 20.5 %copy-start.4 = (bf16[128,2048]{1,0:T(8,128)(2,1)}, bf16[128,2048]{1,0:T(8,128)(2,1)S(1)}, u32[]{:S(2)}) copy-start(bf16[128,2048]{1,0:T(8,128)(2,1)S(1)} %get-tuple-element.181) | copy-start | bytes 1572868
  396.1 21.1 %copy-start.5 = (bf16[128,2048]{1,0:T(8,128)(2,1)}, bf16[128,2048]{1,0:T(8,128)(2,1)S(1)}, u32[]{:S(2)}) copy-start(bf16[128,2048]{1,0:T(8,128)(2,1)S(1)} %get-tuple-element.180) | copy-start | bytes 1572868
  416.6 29.9 %collective-permute-start.19 = (bf16[1024,2048]{1,0:T(8,128)(2,1)}, bf16[1024,2048]{1,0:T(8,128)(2,1)}, u32[]{:S(2)}, u32[]{:S(2)}) collective-permute-start(bf16[1024,2048]{1,0:T(8,128)(2,1)} %pad_maximum_fusion.rows_ref), channel_id=1, source_target_pairs={{0,4},{4,0},{8,12},{12,8},{1,5},{5,1},{9,13},{13,9},{2,6},{6,2},{1... | collective-permute-start | bytes 12582920 | tf_op jit(solution)/shard_map/ppermute | solution.py:526
  416.7 15.3 %collective-permute-start.20 = (bf16[128,2048]{1,0:T(8,128)(2,1)S(1)}, bf16[128,2048]{1,0:T(8,128)(2,1)S(1)}, u32[]{:S(2)}, u32[]{:S(2)}) collective-permute-start(bf16[128,2048]{1,0:T(8,128)(2,1)S(1)} %get-tuple-element.181), channel_id=1, source_target_pairs={{0,16},{16,0},{1,17},{17,1},{2,18},{18,2},{3,19},{19,3},{4,20},{20... | collective-permute-start | bytes 1572872 | tf_op jit(solution)/shard_map/ppermute | solution.py:534
  417.2 14.8 %collective-permute-start.21 = (bf16[128,2048]{1,0:T(8,128)(2,1)S(1)}, bf16[128,2048]{1,0:T(8,128)(2,1)S(1)}, u32[]{:S(2)}, u32[]{:S(2)}) collective-permute-start(bf16[128,2048]{1,0:T(8,128)(2,1)S(1)} %get-tuple-element.180), channel_id=1, source_target_pairs={{0,8},{8,0},{4,12},{12,4},{1,9},{9,1},{5,13},{13,5},{2,10},{10,2},... | collective-permute-start | bytes 1572872 | tf_op jit(solution)/shard_map/ppermute | solution.py:530
  417.7 14.2 %collective-permute-start.22 = (f32[64,128]{1,0:T(8,128)S(1)}, f32[64,128]{1,0:T(8,128)S(1)}, u32[]{:S(2)}, u32[]{:S(2)}) collective-permute-start(f32[64,128]{1,0:T(8,128)S(1)} %slice_add_fusion), channel_id=1, source_target_pairs={{0,8},{8,0},{4,12},{12,4},{1,9},{9,1},{5,13},{13,5},{2,10},{10,2},... | collective-permute-start | bytes 98312 | tf_op jit(solution)/shard_map/ppermute | solution.py:530
  436.1 25.2 %collective-permute-start.24 = (bf16[256,2048]{1,0:T(8,128)(2,1)S(1)}, bf16[256,2048]{1,0:T(8,128)(2,1)}, u32[]{:S(2)}, u32[]{:S(2)}) collective-permute-start(bf16[256,2048]{1,0:T(8,128)(2,1)S(1)} %maximum_select_fusion.10), channel_id=1, source_target_pairs={{0,16},{16,0},{1,17},{17,1},{2,18},{18,2},{3,19},{19,3},{4,20},{20... | collective-permute-start | bytes 3145736 | tf_op jit(solution)/shard_map/ppermute | solution.py:534
  437.7 24.6 %collective-permute-start.23 = (bf16[256,2048]{1,0:T(8,128)(2,1)}, bf16[256,2048]{1,0:T(8,128)(2,1)}, u32[]{:S(2)}, u32[]{:S(2)}) collective-permute-start(bf16[256,2048]{1,0:T(8,128)(2,1)} %maximum_select_fusion.9), channel_id=1, source_target_pairs={{0,8},{8,0},{4,12},{12,4},{1,9},{9,1},{5,13},{13,5},{2,10},{10,2},... | collective-permute-start | bytes 3145736 | tf_op jit(solution)/shard_map/ppermute | solution.py:530
  438.2 23.2 %collective-permute-start.25 = (f32[64,128]{1,0:T(8,128)S(1)}, f32[64,128]{1,0:T(8,128)S(1)}, u32[]{:S(2)}, u32[]{:S(2)}) collective-permute-start(f32[64,128]{1,0:T(8,128)S(1)} %add.393), channel_id=1, source_target_pairs={{0,16},{16,0},{1,17},{17,1},{2,18},{18,2},{3,19},{19,3},{4,20},{20... | collective-permute-start | bytes 98312 | tf_op jit(solution)/shard_map/ppermute | solution.py:534
  470.8 23.7 %collective-permute-start.26 = (bf16[1024,2048]{1,0:T(8,128)(2,1)}, bf16[1024,2048]{1,0:T(8,128)(2,1)}, u32[]{:S(2)}, u32[]{:S(2)}) collective-permute-start(bf16[1024,2048]{1,0:T(8,128)(2,1)} %pad_maximum_fusion.1.rows_ref), channel_id=1, source_target_pairs={{0,4},{4,0},{8,12},{12,8},{1,5},{5,1},{9,13},{13,9},{2,6},{6,2},{1... | collective-permute-start | bytes 12582920 | tf_op jit(solution)/shard_map/ppermute | solution.py:526
  470.8 41.4 %copy-start.10 = (f32[2048]{0:T(1024)}, f32[2048]{0:T(1024)S(1)}, u32[]{:S(2)}) copy-start(f32[2048]{0:T(1024)S(1)} %slice_bitcast_fusion.5) | copy-start | bytes 24580
  470.8 28.4 %collective-permute-start.27 = (bf16[256,2048]{1,0:T(8,128)(2,1)}, bf16[256,2048]{1,0:T(8,128)(2,1)}, u32[]{:S(2)}, u32[]{:S(2)}) collective-permute-start(bf16[256,2048]{1,0:T(8,128)(2,1)} %get-tuple-element.193), channel_id=1, source_target_pairs={{0,16},{16,0},{1,17},{17,1},{2,18},{18,2},{3,19},{19,3},{4,20},{20... | collective-permute-start | bytes 3145736 | tf_op jit(solution)/shard_map/ppermute | solution.py:534
  493.0 16.4 %collective-permute-start.28 = (bf16[256,1024]{1,0:T(8,128)(2,1)}, bf16[256,1024]{1,0:T(8,128)(2,1)}, u32[]{:S(2)}, u32[]{:S(2)}) collective-permute-start(bf16[256,1024]{1,0:T(8,128)(2,1)} %get-tuple-element.197), channel_id=1, source_target_pairs={{0,16},{16,0},{1,17},{17,1},{2,18},{18,2},{3,19},{19,3},{4,20},{20... | collective-permute-start | bytes 1572872 | tf_op jit(solution)/shard_map/ppermute | solution.py:534
  506.1 6.7 %copy-start.1 = (bf16[512,2048]{1,0:T(8,128)(2,1)S(1)}, bf16[512,2048]{1,0:T(8,128)(2,1)}, u32[]{:S(2)}) copy-start(bf16[512,2048]{1,0:T(8,128)(2,1)} %param.27) | copy-start | bytes 6291460
  (10 other events, 31.4 us)
Sparse Core Ops, SparseCore 0:
  11.0 83.4 all-gather.3
  96.0 79.2 all-gather.5
  176.8 79.2 all-gather.7
  258.3 146.1 reduce-scatter.2
  416.8 74.0 reduce-scatter.4
